TPU v7x, 32 devices: a whole 2x2x4 slice. The times are simulated.
32 devices in a mesh: seq: 4 (over y, x), dp: 8 (over z, core).
Axes of the slice: x: 2, y: 2, z: 4, core: 2. Of those that a mesh axis runs over, the one named last changes fastest.
Arguments:
- tokens: bfloat16 [8, 2048, 768], P('dp', 'seq'), may hold values from -6 to 6
- doc_start: int32 [8, 2048], P('dp'), may hold values from 0 to 2047, as said below
- cotangent: bfloat16 [8, 2048, 768], P('dp', 'seq'), may hold values from -6 to 6
- norm_one: float32 [768], replicated, may hold values from 0.5 to 1.5
- w_qkv: bfloat16 [768, 2304], replicated, may hold values from -0.21875 to 0.21875
- w_out: bfloat16 [768, 768], replicated, may hold values from -0.875 to 0.875
- norm_two: float32 [768], replicated, may hold values from 0.5 to 1.5
- w_in: bfloat16 [768, 2304], replicated, may hold values from -0.21875 to 0.21875
- w_down: bfloat16 [1152, 768], replicated, may hold values from -0.1875 to 0.1875
Outputs:
- result: bfloat16 [8, 2048, 768], P('dp', 'seq')
- grad_tokens: float32 [8, 2048, 768], P('dp', 'seq')
- grad_norm_one: float32 [768], replicated
- grad_w_qkv: float32 [768, 2304], replicated
- grad_w_out: float32 [768, 768], replicated
- grad_norm_two: float32 [768], replicated
- grad_w_in: float32 [768, 2304], replicated
- grad_w_down: float32 [1152, 768], replicated
Inputs may be any that keep to these rules, and one draw needn't show every extreme that they name: Documents are contiguous: doc_start of a token is the place of the first token of its run of equal values, which begins at a place equal to that value; every row begins a document at 0 and ends with a document of one token at place 2048 - 1, and in every row one document starts before 2048 / 8 and runs to place 7 * 256 - 1 or further.
All inputs are finite; a program needn't handle non-finite values.
Results may differ from a plain program's by a relative error of at most 0.013.
Values may be sent and summed in bfloat16 or wider, within the bound.
No kernel may reach another device: no remote copies, remote signals or barrier semaphores. Data moves between devices by JAX's collectives and lax.ppermute only.
A program may use at most 128 MiB of HBM per device.

v0:
```python
import functools

import jax
import jax.numpy as jnp
from jax import lax
from jax.experimental import pallas as pl
from jax.experimental.pallas import tpu as pltpu
from jax.sharding import Mesh
from jax.sharding import PartitionSpec as P

D = 768
HEADS = 12
HEAD_DIM = 64
HALF = HEAD_DIM // 2
FF = 1152
WIDE = 3 * HEAD_DIM
LANES = D // 2

EPSILON = 1e-05
ROTARY_BASE = 160000.0
SCORE_SCALE = 0.125
SCORE_EXP2 = SCORE_SCALE * 1.4426950408889634
MASKED_SCORE = -1e30
KEY_CHUNK = 256
F32 = jnp.float32
BF16 = jnp.bfloat16

dot = functools.partial(jnp.dot, preferred_element_type=F32)


def cost(flops, moved, transcendentals=0):
    return pl.CostEstimate(
        flops=flops, bytes_accessed=moved, transcendentals=0
    )


def norm_kernel(tok_ref, norm_ref, out_ref):
    values = tok_ref[...].astype(F32)
    centered = values - jnp.mean(values, axis=-1, keepdims=True)
    variance = jnp.mean(centered * centered, axis=-1, keepdims=True)
    out_ref[...] = (centered * lax.rsqrt(variance + EPSILON) * norm_ref[...]).astype(BF16)


def first_norm(tokens, norm_one):
    rows = tokens.shape[0] // 2
    return pl.pallas_call(
        norm_kernel,
        grid=(2,),
        in_specs=[
            pl.BlockSpec((rows, D), lambda i: (i, 0)),
            pl.BlockSpec((1, D), lambda i: (0, 0)),
        ],
        out_specs=pl.BlockSpec((rows, D), lambda i: (i, 0)),
        out_shape=jax.ShapeDtypeStruct(tokens.shape, BF16),
        compiler_params=pltpu.CompilerParams(vmem_limit_bytes=8 << 20),
        cost_estimate=cost(1 << 20, 2 << 20),
        name="first_norm",
    )(tokens, norm_one[None, :])


def project_kernel(me_ref, hn_ref, w_ref, cos_ref, sin_ref, out_ref):
    part = pl.program_id(0)
    turned = dot(hn_ref[...], w_ref[...]).T
    cosine = jnp.where(part < 2, cos_ref[...], 1.0)
    sine = jnp.where(part < 2, sin_ref[...], 0.0)
    row = pl.multiple_of(part * HEAD_DIM, HEAD_DIM)
    for g in range(out_ref.shape[0]):
        slot = me_ref[0] ^ g
        first = turned[g * HEAD_DIM : g * HEAD_DIM + HALF]
        second = turned[g * HEAD_DIM + HALF : (g + 1) * HEAD_DIM]
        out_ref[slot, pl.ds(row, HALF), :] = (first * cosine - second * sine).astype(BF16)
        out_ref[slot, pl.ds(row + HALF, HALF), :] = (second * cosine + first * sine).astype(BF16)


def project(me, hn, w_qkv, cosine, sine, piece, groups):
    tokens = hn.shape[0]
    width = groups * HEAD_DIM
    pieces = D // width
    return pl.pallas_call(
        project_kernel,
        grid_spec=pltpu.PrefetchScalarGridSpec(
            num_scalar_prefetch=1,
            grid=(3,),
            in_specs=[
                pl.BlockSpec((tokens, D), lambda i, me: (0, 0)),
                pl.BlockSpec((D, width), lambda i, me: (0, i * pieces + piece)),
                pl.BlockSpec((HALF, tokens), lambda i, me: (0, 0)),
                pl.BlockSpec((HALF, tokens), lambda i, me: (0, 0)),
            ],
            out_specs=pl.BlockSpec((groups, WIDE, tokens), lambda i, me: (0, 0, 0)),
        ),
        out_shape=jax.ShapeDtypeStruct((groups, WIDE, tokens), BF16),
        compiler_params=pltpu.CompilerParams(vmem_limit_bytes=32 << 20),
        cost_estimate=cost(6 * tokens * D * width, 4 << 20),
        name="project",
    )(me, hn, w_qkv, cosine, sine)


def mask_scores(scores, chunk, chunks, edge, key_doc, query_doc, query_main):
    if chunk == 0 or chunk == chunks - 1:
        own = key_doc[chunk * KEY_CHUNK : (chunk + 1) * KEY_CHUNK, :]
        return jnp.where(own == query_doc, scores, MASKED_SCORE)
    if edge:
        return jnp.where(query_main, scores, MASKED_SCORE)
    return scores


def put_in_order(me, slots, qkv_s, key_s, value_s=None):
    span = qkv_s.shape[2]
    for k, ref in enumerate(slots):
        at = me ^ k
        piece = ref[...].reshape(WIDE, span)
        qkv_s[at] = piece
        rows = pl.ds(pl.multiple_of(at * span, span), span)
        key_s[rows, :] = piece[HEAD_DIM : 2 * HEAD_DIM].astype(F32).T.astype(BF16)
        if value_s is not None:
            value_s[rows, :] = piece[2 * HEAD_DIM :].astype(F32).T.astype(BF16)


def slot_specs(slots):
    own = pl.BlockSpec((1,) + slots[0].shape[1:], lambda i, me: (0, 0, 0))
    rest = [pl.BlockSpec(s.shape, lambda i, me: (0, 0)) for s in slots[1:]]
    return [own] + rest


def forward_kernel(bq, parts, me_ref, *refs):
    slots = refs[:parts]
    kdoc_ref, qdoc_ref, out_ref, lse_ref, qkv_s, key_s, score_s = refs[parts:]
    step = pl.program_id(0)
    steps = pl.num_programs(0)
    total = key_s.shape[0]
    chunks = total // KEY_CHUNK
    span = qkv_s.shape[2]
    ratio = span // bq

    @pl.when(step == 0)
    def _():
        put_in_order(me_ref[0], slots, qkv_s, key_s)

    def run(edge):
        lanes = pl.ds(pl.multiple_of((step % ratio) * bq, bq), bq)
        queries = qkv_s[step // ratio, 0:HEAD_DIM, lanes]
        query_doc = qdoc_ref[...]
        query_main = query_doc == kdoc_ref[total // 2 : total // 2 + 1, :]
        top = None
        for c in range(chunks):
            rows = slice(c * KEY_CHUNK, (c + 1) * KEY_CHUNK)
            scores = dot(key_s[rows, :], queries)
            scores = mask_scores(scores, c, chunks, edge, kdoc_ref, query_doc, query_main)
            score_s[rows, :] = scores
            peak = jnp.max(scores.reshape(KEY_CHUNK // 8, 8, bq), axis=0)
            top = peak if top is None else jnp.maximum(top, peak)
        top = jnp.max(top, axis=0, keepdims=True) * SCORE_EXP2
        mass, acc = None, None
        for c in range(chunks):
            rows = slice(c * KEY_CHUNK, (c + 1) * KEY_CHUNK)
            weight = jnp.exp2(score_s[rows, :] * SCORE_EXP2 - top)
            part = jnp.sum(weight.reshape(KEY_CHUNK // 8, 8, bq), axis=0)
            mass = part if mass is None else mass + part
            at = c * KEY_CHUNK % span
            values = qkv_s[c * KEY_CHUNK // span, 2 * HEAD_DIM :, at : at + KEY_CHUNK]
            term = dot(values, weight.astype(BF16))
            acc = term if acc is None else acc + term
        mass = jnp.sum(mass, axis=0, keepdims=True)
        out_ref[0] = (acc / mass).astype(BF16)
        lse_ref[...] = top + jnp.log2(mass)

    at_edge = (step == 0) | (step == steps - 1)
    pl.when(at_edge)(lambda: run(True))
    pl.when(jnp.logical_not(at_edge))(lambda: run(False))


def attend_forward(me, slots, key_doc, query_doc, bq):
    parts, _, span = slots[0].shape
    total = parts * span
    ratio = span // bq
    return pl.pallas_call(
        functools.partial(forward_kernel, bq, parts),
        grid_spec=pltpu.PrefetchScalarGridSpec(
            num_scalar_prefetch=1,
            grid=(total // bq,),
            in_specs=slot_specs(slots)
            + [
                pl.BlockSpec((total, 1), lambda i, me: (0, 0)),
                pl.BlockSpec((1, bq), lambda i, me: (0, i)),
            ],
            out_specs=[
                pl.BlockSpec((1, HEAD_DIM, bq), lambda i, me: (i // ratio ^ me[0], 0, i % ratio)),
                pl.BlockSpec((1, bq), lambda i, me: (0, i)),
            ],
            scratch_shapes=[
                pltpu.VMEM((parts, WIDE, span), BF16),
                pltpu.VMEM((total, HEAD_DIM), BF16),
                pltpu.VMEM((total, bq), F32),
            ],
        ),
        out_shape=[
            jax.ShapeDtypeStruct((parts, HEAD_DIM, span), BF16),
            jax.ShapeDtypeStruct((1, total), F32),
        ],
        compiler_params=pltpu.CompilerParams(vmem_limit_bytes=40 << 20),
        cost_estimate=cost(16 * HEAD_DIM * total * total, 4 << 20, total * total),
        name="attend_forward",
    )(me, *slots, key_doc, query_doc)


def backward_kernel(bq, parts, me_ref, *refs):
    slots, ups = refs[:parts], refs[parts : 2 * parts]
    (kdoc_ref, qdoc_ref, o_ref, lse_ref, cos_ref, sin_ref, grad_ref,
     qkv_s, key_s, value_s, up_s, dk_s, dv_s) = refs[2 * parts :]
    step = pl.program_id(0)
    steps = pl.num_programs(0)
    total = key_s.shape[0]
    chunks = total // KEY_CHUNK
    span = qkv_s.shape[2]
    ratio = span // bq

    @pl.when(step == 0)
    def _():
        put_in_order(me_ref[0], slots, qkv_s, key_s, value_s)
        for k, ref in enumerate(ups):
            up_s[me_ref[0] ^ k] = ref[...].reshape(HEAD_DIM, span)
        dk_s[...] = jnp.zeros_like(dk_s)
        dv_s[...] = jnp.zeros_like(dv_s)

    def turn_back(grad, cosine, sine):
        first, second = grad[:HALF], grad[HALF:]
        return first * cosine + second * sine, second * cosine - first * sine

    def run(edge):
        lanes = pl.ds(pl.multiple_of((step % ratio) * bq, bq), bq)
        here = pl.ds(pl.multiple_of(step * bq, bq), bq)
        queries = qkv_s[step // ratio, 0:HEAD_DIM, lanes]
        upstream = up_s[step // ratio, :, lanes]
        wide_up = upstream.astype(F32)
        centre = jnp.sum(wide_up * o_ref[0].astype(F32), axis=0, keepdims=True)
        query_rows = queries.astype(F32).T.astype(BF16)
        up_rows = wide_up.T.astype(BF16)
        query_doc = qdoc_ref[...]
        query_main = query_doc == kdoc_ref[total // 2 : total // 2 + 1, :]
        lse = lse_ref[...]
        dq = None
        for c in range(chunks):
            rows = slice(c * KEY_CHUNK, (c + 1) * KEY_CHUNK)
            scores = dot(key_s[rows, :], queries)
            scores = mask_scores(scores, c, chunks, edge, kdoc_ref, query_doc, query_main)
            probs = jnp.exp2(scores * SCORE_EXP2 - lse)
            grad_prob = dot(value_s[rows, :], upstream)
            grad_scores = (probs * (grad_prob - centre)).astype(BF16)
            dv_s[rows, :] += dot(probs.astype(BF16), up_rows)
            dk_s[rows, :] += dot(grad_scores, query_rows)
            at = c * KEY_CHUNK % span
            keys = qkv_s[c * KEY_CHUNK // span, HEAD_DIM : 2 * HEAD_DIM, at : at + KEY_CHUNK]
            term = dot(keys, grad_scores)
            dq = term if dq is None else dq + term
        one, two = turn_back(dq * SCORE_SCALE, cos_ref[:, here], sin_ref[:, here])
        slot = me_ref[0] ^ (step // ratio)
        grad_ref[slot, 0:HALF, lanes] = one.astype(BF16)
        grad_ref[slot, HALF:HEAD_DIM, lanes] = two.astype(BF16)

    at_edge = (step == 0) | (step == steps - 1)
    pl.when(at_edge)(lambda: run(True))
    pl.when(jnp.logical_not(at_edge))(lambda: run(False))

    @pl.when(step == steps - 1)
    def _():
        for s in range(parts):
            slot = me_ref[0] ^ s
            rows = slice(s * span, (s + 1) * span)
            one, two = turn_back(dk_s[rows, :].T * SCORE_SCALE, cos_ref[:, rows], sin_ref[:, rows])
            grad_ref[slot, HEAD_DIM : HEAD_DIM + HALF, :] = one.astype(BF16)
            grad_ref[slot, HEAD_DIM + HALF : 2 * HEAD_DIM, :] = two.astype(BF16)
            grad_ref[slot, 2 * HEAD_DIM :, :] = dv_s[rows, :].T.astype(BF16)


def attend_backward(me, slots, key_doc, query_doc, upstream, piece, context, lse, cosine, sine, bq):
    parts, _, span = slots[0].shape
    total = parts * span
    ratio = span // bq
    return pl.pallas_call(
        functools.partial(backward_kernel, bq, parts),
        grid_spec=pltpu.PrefetchScalarGridSpec(
            num_scalar_prefetch=1,
            grid=(total // bq,),
            in_specs=slot_specs(slots)
            + [pl.BlockSpec((1, HEAD_DIM, span), lambda i, me: (piece, 0, 0))] * parts
            + [
                pl.BlockSpec((total, 1), lambda i, me: (0, 0)),
                pl.BlockSpec((1, bq), lambda i, me: (0, i)),
                pl.BlockSpec((1, HEAD_DIM, bq), lambda i, me: (i // ratio ^ me[0], 0, i % ratio)),
                pl.BlockSpec((1, bq), lambda i, me: (0, i)),
                pl.BlockSpec((HALF, total), lambda i, me: (0, 0)),
                pl.BlockSpec((HALF, total), lambda i, me: (0, 0)),
            ],
            out_specs=pl.BlockSpec((parts, WIDE, span), lambda i, me: (0, 0, 0)),
            scratch_shapes=[
                pltpu.VMEM((parts, WIDE, span), BF16),
                pltpu.VMEM((total, HEAD_DIM), BF16),
                pltpu.VMEM((total, HEAD_DIM), BF16),
                pltpu.VMEM((parts, HEAD_DIM, span), BF16),
                pltpu.VMEM((total, HEAD_DIM), F32),
                pltpu.VMEM((total, HEAD_DIM), F32),
            ],
        ),
        out_shape=jax.ShapeDtypeStruct((parts, WIDE, span), BF16),
        compiler_params=pltpu.CompilerParams(vmem_limit_bytes=40 << 20),
        cost_estimate=cost(40 * HEAD_DIM * total * total, 6 << 20, total * total),
        name="attend_backward",
    )(me, *slots, *upstream, key_doc, query_doc, context, lse, cosine, sine)


def dot_rows(a, b):
    return lax.dot_general(a, b, (((1,), (1,)), ((), ())), preferred_element_type=F32)


def middle_kernel(parts, me_ref, *refs):
    slots = refs[:parts]
    (tok_ref, cot_ref, wout_ref, norm_ref, win_ref, wdown_ref,
     ctx_ref, n2_ref, gu_ref, inner_ref, low_ref, mid_ref, result_ref) = refs[parts : parts + 13]
    outs, down_s = refs[parts + 13 : -1], refs[-1]
    pieces = slots[0].shape[0]

    def rows_of(j, k):
        at = (j * parts + (me_ref[0] ^ k)) * HEAD_DIM
        return pl.ds(pl.multiple_of(at, HEAD_DIM), HEAD_DIM)

    for k, ref in enumerate(slots):
        for j in range(pieces):
            ctx_ref[rows_of(j, k), :] = ref[j]
    context = ctx_ref[...].astype(F32).T.astype(BF16)
    middle = tok_ref[...].astype(F32) + dot(context, wout_ref[...])
    centered = middle - jnp.mean(middle, axis=-1, keepdims=True)
    scale = lax.rsqrt(jnp.mean(centered * centered, axis=-1, keepdims=True) + EPSILON)
    unit = centered * scale
    normed = (unit * norm_ref[...]).astype(BF16)
    n2_ref[...] = normed
    cotangent = cot_ref[...]
    for c in range(FF // LANES):
        cols = slice(c * LANES, (c + 1) * LANES)
        high = slice(FF + c * LANES, FF + (c + 1) * LANES)
        gate = dot(normed, win_ref[:, cols])
        up = dot(normed, win_ref[:, high])
        grad_inner = dot_rows(cotangent, wdown_ref[cols, :])
        share = 0.5 + 0.5 * lax.erf(gate * 0.7071067811865476)
        slope = share + gate * (0.3989422804014327 * jnp.exp(-0.5 * gate * gate))
        gelu = gate * share
        inner_ref[:, cols] = (gelu * up).astype(BF16)
        gu_ref[:, cols] = (slope * up * grad_inner).astype(BF16)
        gu_ref[:, high] = (gelu * grad_inner).astype(BF16)
    upstream = dot_rows(gu_ref[...], win_ref[...]) * norm_ref[...]
    flat = jnp.mean(upstream, axis=-1, keepdims=True)
    along = jnp.mean(upstream * unit, axis=-1, keepdims=True)
    grad_middle = cotangent.astype(F32) + (upstream - flat - unit * along) * scale
    mid_ref[...] = grad_middle
    low = grad_middle.astype(BF16)
    low_ref[...] = low
    down_s[...] = dot_rows(wout_ref[...], low).astype(BF16)
    for k, ref in enumerate(outs):
        for j in range(pieces):
            ref[j] = down_s[rows_of(j, k), :]
    result_ref[...] = (middle + dot(inner_ref[...], wdown_ref[...])).astype(BF16)


def middle_part(me, slots, tokens, cotangent, w_out, norm_two, w_in, w_down):
    parts, span = len(slots), tokens.shape[0]
    vmem = pl.BlockSpec(memory_space=pltpu.VMEM)
    like = lambda shape, kind=BF16: jax.ShapeDtypeStruct(shape, kind)
    out_shape = [
        like((D, span)),
        like((span, D)),
        like((span, 2 * FF)),
        like((span, FF)),
        like((span, D)),
        like((span, D), F32),
        like((span, D)),
    ] + [like(slots[0].shape)] * parts
    return pl.pallas_call(
        functools.partial(middle_kernel, parts),
        in_specs=[pl.BlockSpec(memory_space=pltpu.SMEM)] + [vmem] * (parts + 6),
        out_specs=[vmem] * len(out_shape),
        out_shape=out_shape,
        scratch_shapes=[pltpu.VMEM((D, span), BF16)],
        compiler_params=pltpu.CompilerParams(vmem_limit_bytes=50 << 20),
        cost_estimate=cost(2 * span * D * (2 * D + 5 * FF + 2 * FF), 20 << 20),
        name="middle_part",
    )(me, *slots, tokens, cotangent, w_out, norm_two[None, :], w_in, w_down)


def early_grad_kernel(at_ref, n2_ref, gu_ref, inner_ref, cot_ref, ctx_ref, mid_ref, keep_ref, give_ref):
    pieces = keep_ref.shape[0]
    rows = D // (2 * pieces)
    low = at_ref[0] == 0

    def put(first, second, count, at):
        kept = jnp.where(low, first, second).astype(BF16)
        given = jnp.where(low, second, first).astype(BF16)
        for p in range(pieces):
            here = slice(p * count, (p + 1) * count)
            place = at_ref[1 + p]
            keep_ref[place, at : at + count, :] = kept[here]
            give_ref[place, at : at + count, :] = given[here]

    n2_t = n2_ref[...].astype(F32).T.astype(BF16)
    for u in range(2 * FF // LANES):
        block = dot(n2_t, gu_ref[:, u * LANES : (u + 1) * LANES])
        put(block[: D // 2], block[D // 2 :], rows, u * rows)
    inner_t = inner_ref[...].astype(F32).T.astype(BF16)
    down = dot(inner_t, cot_ref[...])
    put(down[:, :LANES], down[:, LANES:], 3 * rows, 6 * rows)
    for u in range(2):
        block = dot(ctx_ref[...], mid_ref[:, u * LANES : (u + 1) * LANES])
        put(block[: D // 2], block[D // 2 :], rows, (9 + u) * rows)


def early_places(me, parts, near):
    half = near // 2
    first = [(k, q) for k in (1, 3) for q in range(half)]
    second = [(k, q) for k in (2, 3) for q in range(half, near)]
    kept = [(k, q) for k in (0, 2) for q in range(half)]
    kept += [(k, q) for k in (0, 1) for q in range(half, near)]
    order = {slot: i for i, slot in enumerate(first + second + kept)}
    table = jnp.array([order[k, q] for k in range(parts) for q in range(near)], jnp.int32)
    piece = jnp.arange(parts * near, dtype=jnp.int32)
    return jnp.concatenate([me[2:], table[piece ^ (me[0] * near + me[1])]])


def early_grads(me, n2, gate_up, inner, cotangent, context_t, mid, parts, near):
    rows = D // (2 * parts * near)
    shape = jax.ShapeDtypeStruct((parts * near, 11 * rows, LANES), BF16)
    operands = (n2, gate_up, inner, cotangent, context_t, mid)
    once = lambda a: pl.BlockSpec(a.shape, lambda i, at: (0,) * len(a.shape))
    return pl.pallas_call(
        early_grad_kernel,
        grid_spec=pltpu.PrefetchScalarGridSpec(
            num_scalar_prefetch=1,
            grid=(1,),
            in_specs=[once(a) for a in operands],
            out_specs=[once(shape), once(shape)],
        ),
        out_shape=[shape, shape],
        compiler_params=pltpu.CompilerParams(vmem_limit_bytes=44 << 20),
        cost_estimate=cost(2 * n2.shape[0] * 4224 * D, 14 << 20),
        name="early_grads",
    )(early_places(me, parts, near), *operands)


def late_grad_kernel(pieces, me_ref, *refs):
    grads = refs[:pieces]
    hn_ref, keep_ref, give_ref = refs[pieces:]
    parts = hn_ref.shape[0]
    near = keep_ref.shape[0]
    low = me_ref[2] == 0
    for j, ref in enumerate(grads):
        block = None
        for s in range(parts):
            term = dot(ref[s], hn_ref[s])
            block = term if block is None else block + term
        for part in range(3):
            head = block[part * HEAD_DIM : (part + 1) * HEAD_DIM]
            first, second = head[:HALF], head[HALF:]
            kept = jnp.where(low, first, second).astype(BF16)
            given = jnp.where(low, second, first).astype(BF16)
            for r in range(near):
                slot = me_ref[1] ^ r
                keep_ref[slot, 3 * j + part] = kept[8 * r : 8 * r + 8]
                give_ref[slot, 3 * j + part] = given[8 * r : 8 * r + 8]


def late_grads(me, grads, hn_row, near):
    pieces = len(grads)
    shape = jax.ShapeDtypeStruct((near, 3 * pieces, 8, D), BF16)
    vmem = pl.BlockSpec(memory_space=pltpu.VMEM)
    return pl.pallas_call(
        functools.partial(late_grad_kernel, pieces),
        in_specs=[pl.BlockSpec(memory_space=pltpu.SMEM)] + [vmem] * (pieces + 1),
        out_specs=[vmem, vmem],
        out_shape=[shape, shape],
        compiler_params=pltpu.CompilerParams(vmem_limit_bytes=32 << 20),
        cost_estimate=cost(2 * 2048 * 576 * D, 6 << 20),
        name="late_grads",
    )(me, *grads, hn_row)


def fold_lanes(wide):
    total = wide[:, :128]
    for i in range(1, wide.shape[1] // 128):
        total += wide[:, 128 * i : 128 * (i + 1)]
    return total


def early_kernel(
    me_ref, mine_ref, other_ref, w_ref, norm_ref, win_ref, wdown_ref, wout_ref, gain_ref, part_s
):
    near = mine_ref.shape[1]
    step = pl.program_id(0)
    steps = pl.num_programs(0)
    parts = steps // 2
    rows = D // (steps * near)

    def run(ref):
        for r in range(near):
            piece = ref[0, me_ref[1] ^ r].astype(F32)
            here = slice(r * rows, (r + 1) * rows)
            wide = jnp.concatenate([piece[rows * u : rows * (u + 1)] for u in range(6)], axis=1)
            win_ref[here, :] = wide
            at = pl.multiple_of((step * near + r) * rows, rows)
            part_s[pl.ds(at, rows), :] = fold_lanes(wide * w_ref[here, :].astype(F32))
            wdown_ref[3 * r * rows : 3 * (r + 1) * rows, :] = piece[6 * rows : 9 * rows]
            wout_ref[here, :LANES] = piece[9 * rows : 10 * rows]
            wout_ref[here, LANES:] = piece[10 * rows :]

    ours = (step // parts) == me_ref[2]
    pl.when(ours)(lambda: run(mine_ref))
    pl.when(jnp.logical_not(ours))(lambda: run(other_ref))

    @pl.when(step == steps - 1)
    def _():
        gain_ref[...] = jnp.sum(part_s[...].T, axis=0, keepdims=True) / norm_ref[...]


def assemble_early(me, mine, other, w_in, norm_two):
    parts, near = mine.shape[:2]
    steps = 2 * parts
    rows = D // steps

    def slot(own):
        def index(p, me):
            used = (p // parts == me[2]) == own
            return (jnp.where(used, me[0] ^ (p % parts), 0), 0, 0, 0)

        return pl.BlockSpec((1,) + mine.shape[1:], index)

    return pl.pallas_call(
        early_kernel,
        grid_spec=pltpu.PrefetchScalarGridSpec(
            num_scalar_prefetch=1,
            grid=(steps,),
            in_specs=[
                slot(True),
                slot(False),
                pl.BlockSpec((rows, 2 * FF), lambda p, me: (p, 0)),
                pl.BlockSpec((1, D), lambda p, me: (0, 0)),
            ],
            out_specs=[
                pl.BlockSpec((rows, 2 * FF), lambda p, me: (p, 0)),
                pl.BlockSpec((3 * rows, LANES), lambda p, me: (p % parts, p // parts)),
                pl.BlockSpec((rows, D), lambda p, me: (p, 0)),
                pl.BlockSpec((1, D), lambda p, me: (0, 0)),
            ],
            scratch_shapes=[pltpu.VMEM((D, 128), F32)],
        ),
        out_shape=[
            jax.ShapeDtypeStruct((D, 2 * FF), F32),
            jax.ShapeDtypeStruct((FF, D), F32),
            jax.ShapeDtypeStruct((D, D), F32),
            jax.ShapeDtypeStruct((1, D), F32),
        ],
        compiler_params=pltpu.CompilerParams(vmem_limit_bytes=24 << 20),
        cost_estimate=cost(1 << 20, 24 << 20),
        name="assemble_early",
    )(me, mine, other, w_in, norm_two[None, :])


def late_kernel(me_ref, *refs):
    mine, other = refs[:5], refs[5:10]
    w_ref, norm_ref, out_ref, gain_ref, rows_s, part_s, unit_s = refs[10:]
    block = pl.program_id(0)
    near = mine[0].shape[0]
    pieces = mine[0].shape[1] // 3
    low = me_ref[2] == 0
    row = (block % pieces) * 3 + block // pieces

    @pl.when(block == 0)
    def _():
        ones = lax.broadcasted_iota(jnp.int32, unit_s.shape, 0) == lax.broadcasted_iota(
            jnp.int32, unit_s.shape, 1
        )
        unit_s[...] = ones.astype(F32).astype(BF16)

    for k in range(4):
        for q in range(near):
            which = k if k < 3 else 3 + q // (near // 2)
            place = q if k < 3 else q % (near // 2)
            kept, swapped = mine[which][place, row], other[which][place, row]
            at = (me_ref[0] ^ k) * HEAD_DIM + (me_ref[1] ^ q) * 8
            lower = jnp.where(low, kept.astype(F32), swapped.astype(F32))
            upper = jnp.where(low, swapped.astype(F32), kept.astype(F32))
            rows_s[pl.ds(pl.multiple_of(at, 8), 8), :] = lower
            rows_s[pl.ds(pl.multiple_of(at + HALF, 8), 8), :] = upper
    wide = lax.dot_general(
        unit_s[...], rows_s[...].astype(BF16), (((1,), (1,)), ((), ())), preferred_element_type=F32
    )
    out_ref[...] = wide
    part = fold_lanes(wide * w_ref[...].astype(F32))

    @pl.when(block == 0)
    def _():
        part_s[...] = part

    @pl.when(block > 0)
    def _():
        part_s[...] += part

    @pl.when(block == pl.num_programs(0) - 1)
    def _():
        gain_ref[...] = jnp.sum(part_s[...].T, axis=0, keepdims=True) / norm_ref[...]


def assemble_late(me, mine, other, w_qkv, norm_one):
    groups, blocks = 4, mine[0].shape[1]
    pieces = blocks // 3
    width = groups * HEAD_DIM
    sums = [pl.BlockSpec(v.shape, lambda b, me: (0, 0, 0, 0)) for v in mine]
    return pl.pallas_call(
        late_kernel,
        grid_spec=pltpu.PrefetchScalarGridSpec(
            num_scalar_prefetch=1,
            grid=(blocks,),
            in_specs=sums
            + sums
            + [
                pl.BlockSpec((D, width), lambda b, me: (0, b)),
                pl.BlockSpec((1, D), lambda b, me: (0, 0)),
            ],
            out_specs=[
                pl.BlockSpec((D, width), lambda b, me: (0, b)),
                pl.BlockSpec((1, D), lambda b, me: (0, 0)),
            ],
            scratch_shapes=[
                pltpu.VMEM((width, D), F32),
                pltpu.VMEM((D, 128), F32),
                pltpu.VMEM((D, D), BF16),
            ],
        ),
        out_shape=[
            jax.ShapeDtypeStruct((D, 3 * D), F32),
            jax.ShapeDtypeStruct((1, D), F32),
        ],
        compiler_params=pltpu.CompilerParams(vmem_limit_bytes=60 << 20),
        cost_estimate=cost(1 << 20, 14 << 20),
        name="assemble_late",
    )(me, *mine, *other, w_qkv, norm_one[None, :])


def input_grad_kernel(parts, pieces, me_ref, *refs):
    pair, last = refs[:parts], refs[parts : 2 * parts]
    w_ref, tok_ref, norm_ref, mid_ref, out_ref, proj_s = refs[2 * parts :]
    span = proj_s.shape[1]
    for k in range(parts):
        group = me_ref[0] ^ k
        for j in range(pieces):
            if j < pieces - 1:
                piece = pair[k][...].reshape(pieces - 1, WIDE, span)[j]
            else:
                piece = last[k][...].reshape(WIDE, span)
            for part in range(3):
                at = part * D + (j * parts + group) * HEAD_DIM
                proj_s[pl.ds(pl.multiple_of(at, HEAD_DIM), HEAD_DIM), :] = piece[
                    part * HEAD_DIM : (part + 1) * HEAD_DIM
                ]
    upstream = dot(w_ref[...], proj_s[...]).T * norm_ref[...]
    values = tok_ref[...].astype(F32)
    centered = values - jnp.mean(values, axis=-1, keepdims=True)
    scale = lax.rsqrt(jnp.mean(centered * centered, axis=-1, keepdims=True) + EPSILON)
    unit = centered * scale
    flat = jnp.mean(upstream, axis=-1, keepdims=True)
    along = jnp.mean(upstream * unit, axis=-1, keepdims=True)
    out_ref[...] = mid_ref[...] + (upstream - flat - unit * along) * scale


def input_grad(me, pair, last, w_qkv, tokens, norm_one, grad_middle):
    parts = len(pair)
    span = tokens.shape[0]
    vmem = pl.BlockSpec(memory_space=pltpu.VMEM)
    return pl.pallas_call(
        functools.partial(input_grad_kernel, parts, 3),
        in_specs=[pl.BlockSpec(memory_space=pltpu.SMEM)] + [vmem] * (2 * parts + 4),
        out_specs=vmem,
        out_shape=jax.ShapeDtypeStruct((span, D), F32),
        scratch_shapes=[pltpu.VMEM((3 * D, span), BF16)],
        compiler_params=pltpu.CompilerParams(vmem_limit_bytes=40 << 20),
        cost_estimate=cost(2 * span * 3 * D * D, 10 << 20),
        name="input_grad",
    )(me, *pair, *last, w_qkv, tokens, norm_one[None, :], grad_middle)


def swap(values, axis, k):
    size = lax.axis_size(axis)
    return lax.ppermute(values, axis, [(i, i ^ k) for i in range(size)])


def add(*terms):
    total = terms[0].astype(F32)
    for term in terms[1:]:
        total += term.astype(F32)
    return total.astype(BF16)


def scatter_near(slots):
    return add(slots[0], *[swap(slots[k], "near", k) for k in range(1, len(slots))])


def gather_near(values):
    return jnp.stack([values] + [swap(values, "near", k) for k in range(1, lax.axis_size("near"))])


def tie(*values):
    return lax.optimization_barrier(values)


def on_device(tokens, doc_start, cotangent, norm_one, w_qkv, w_out, norm_two, w_in, w_down):
    parts = lax.axis_size("seq")
    near = lax.axis_size("near")
    far = lax.axis_size("far")
    span = tokens.shape[1]
    total = span * parts
    pieces = HEADS // parts
    bq = min(512, span)
    me_seq = lax.axis_index("seq").astype(jnp.int32)
    me = jnp.stack([lax.axis_index(a).astype(jnp.int32) for a in ("seq", "near", "core")])
    first_token = me_seq * span
    starts = doc_start[0]
    key_doc = starts[:, None]
    query_doc = starts[None, :]

    frequency = ROTARY_BASE ** (-(jnp.arange(HALF, dtype=F32) * 2.0 / HEAD_DIM))
    offset = (jnp.arange(total, dtype=jnp.int32) - starts).astype(F32)
    angles = frequency[:, None] * offset[None, :]
    cosine, sine = jnp.cos(angles), jnp.sin(angles)
    own_cosine = lax.dynamic_slice_in_dim(cosine, first_token, span, axis=1)
    own_sine = lax.dynamic_slice_in_dim(sine, first_token, span, axis=1)

    def sum_far(values):
        return lax.psum(values, "far") if far > 1 else values

    hn = first_norm(tokens[0], norm_one)
    qkv = []
    for j in range(pieces):
        sent = project(me, hn, w_qkv, own_cosine, own_sine, j, parts)
        qkv.append([sent] + [swap(sent[k], "seq", k) for k in range(1, parts)])
    contexts, lses = [], []
    for j in range(pieces):
        if j == pieces - 1:
            hn_late, qkv[j] = tie(hn, qkv[j])
            hn_near = [swap(hn_late, "seq", 1), swap(hn_late, "seq", 2)]
        context, lse = attend_forward(me, qkv[j], key_doc, query_doc, bq)
        contexts.append(context)
        lses.append(lse)
    arrived = [jnp.stack([c[k] for c in contexts]) for k in range(parts)]
    arrived[1:] = [swap(arrived[k], "seq", k) for k in range(1, parts)]
    arrived, hn_near = tie(arrived, hn_near)
    hn_far = [swap(hn_near[1][: span // 2], "seq", 1), swap(hn_near[0][span // 2 :], "seq", 2)]
    outs = middle_part(me, arrived, tokens[0], cotangent[0], w_out, norm_two, w_in, w_down)
    outs, hn_far = tie(outs, hn_far)
    context_t, normed_two, grad_gate_up, inner, grad_mid_low, grad_middle, result = outs[:7]
    hn_row = jnp.stack([hn, hn_near[0], hn_near[1], jnp.concatenate(hn_far)])
    upstream = [outs[7]] + [swap(outs[7 + k], "seq", k) for k in range(1, parts)]
    keep, give = early_grads(
        me, normed_two, grad_gate_up, inner, cotangent[0], context_t, grad_mid_low, parts, near
    )
    taken = swap(give, "core", 1)
    half = near // 2
    at = [2 * half, 4 * half, 5 * half, 6 * half, 7 * half, 8 * half]
    send_one = add(keep[: at[0]], taken[: at[0]])
    send_two = add(keep[at[0] : at[1]], taken[at[0] : at[1]])
    early = add(keep[at[1] :], taken[at[1] :])
    a_own, a_two, b_own, b_one = (early[i * half : (i + 1) * half] for i in range(4))
    send_one, send_two, early, upstream = tie(send_one, send_two, early, upstream)

    def backward(j, upstream):
        return attend_backward(
            me, qkv[j], key_doc, query_doc, upstream, j, contexts[j], lses[j], cosine, sine, bq
        )

    from_one, from_two = swap(send_one, "seq", 1), swap(send_two, "seq", 2)
    grads = [backward(0, upstream)]
    grads[0], upstream, from_one, from_two = tie(grads[0], upstream, from_one, from_two)
    by_two = swap(add(a_two, from_one[half:]), "seq", 2)
    by_one = swap(add(b_one, from_two[half:]), "seq", 1)
    grads.append(backward(1, upstream))
    grads, upstream, by_two, by_one = tie(grads, upstream, by_two, by_one)
    own = jnp.stack(grads, axis=1)
    pair = [own[0]] + [swap(own[k], "seq", k) for k in range(1, parts)]
    early = [add(a_own[i], from_one[i], by_two[i]) for i in range(half)]
    early += [add(b_own[i], from_two[i], by_one[i]) for i in range(half)]
    early = scatter_near(early)
    grads.append(backward(2, upstream))

    kept, given = late_grads(me, grads, hn_row, near)
    grads, early, pair, kept, given = tie(grads, early, pair, kept, given)
    last = [grads[2][0]] + [swap(grads[2][k], "seq", k) for k in range(1, parts)]
    early = sum_far(early)
    slots = [early, swap(early, "near", 1), swap(early, "near", 2), swap(early, "near", 3)]
    late = add(kept, swap(given, "core", 1))
    last, slots, late = tie(last, slots, late)
    early = jnp.stack(slots)
    one, two = swap(early, "seq", 1), swap(early, "seq", 2)
    late = sum_far(scatter_near(late))
    grad_input = input_grad(me, pair, last, w_qkv, tokens[0], norm_one, grad_middle)
    one, two, late, grad_input = tie(one, two, late, grad_input)
    far_one, far_two = swap(two[: near // 2], "seq", 1), swap(one[near // 2 :], "seq", 2)
    late = gather_near(late)
    far_one, far_two, late = tie(far_one, far_two, late)
    early = jnp.stack([early, one, two, jnp.concatenate([far_one, far_two])])
    early_other = swap(early, "core", 1)
    one, two = swap(late, "seq", 1), swap(late, "seq", 2)
    one, two, early_other = tie(one, two, early_other)
    far = [swap(two[: near // 2], "seq", 1), swap(one[near // 2 :], "seq", 2)]
    mine = [late, one, two]
    other = [swap(v, "core", 1) for v in mine]
    sum_w_in, sum_w_down, sum_w_out, sum_norm_two = assemble_early(
        me, early, early_other, w_in, norm_two
    )
    sum_w_in, far, other = tie(sum_w_in, far, other)
    mine += far
    other += [swap(v, "core", 1) for v in far]
    sum_w_qkv, sum_norm_one = assemble_late(me, mine, other, w_qkv, norm_one)
    return (
        result[None],
        grad_input[None],
        sum_norm_one[0],
        sum_w_qkv,
        sum_w_out,
        sum_norm_two[0],
        sum_w_in,
        sum_w_down,
    )


def solution(mesh):
    parts = mesh.shape["seq"]
    near = min(4, mesh.shape["dp"] // 2)
    split = Mesh(mesh.devices.reshape(parts, -1, near, 2), ("seq", "far", "near", "core"))
    rows = ("far", "near", "core")
    tokens_at = P(rows, "seq", None)
    return jax.shard_map(
        on_device,
        mesh=split,
        in_specs=(tokens_at, P(rows, None), tokens_at, P(), P(), P(), P(), P(), P()),
        out_specs=(tokens_at, tokens_at, P(), P(), P(), P(), P(), P()),
        check_vma=False,
    )
```

profile of v0, /device:TPU:0, one launch (start us, length us, event | category | flops | bytes accessed | tf_op | source)
XLA Modules:
  0.0 280.0 jit_solution(16101288965218618919)
XLA Ops:
  10.4 2.9 %collective-permute-start.6 = (bf16[192,512]{1,0:T(8,128)(2,1)}, bf16[192,512]{1,0:T(8,128)(2,1)}, u32[]{:S(2)}, u32[]{:S(2)}) collective-permute-start(bf16[192,512]{1,0:T(8,128)(2,1)} %get-tuple-element.243), channel_id=1, source_target_pairs={{0,8},{8,0},{16,24},{24,16},{1,9},{9,1},{17,25},{25,17},{2,10},{10... | collective-permute-start | bytes 589832 | tf_op jit(solution)/shard_map/ppermute | solution.py:689
  30.2 8.7 %attend_forward.5 = (bf16[4,64,512]{2,1,0:T(8,128)(2,1)S(1)}, f32[1,2048]{1,0:T(1,128)S(1)}) custom-call(s32[3]{0:T(128)S(1)} %pad_add_fusion.me_ref, bf16[4,192,512]{2,1,0:T(8,128)(2,1)S(1)} %project.5.refs_0_, bf16[192,512]{1,0:T(8,128)(2,1)} %collective-permute-done.6.refs_1_, bf16[192,512]{1,0:T(8,128)(2,1)} %collective-permute-done.7.refs_2_, ...), custom_call_target="tpu_custom_call" | custom-call | flops 4294967296 | bytes 4194304 | tf_op jit(solution)/shard_map/attend_forward/pallas_call | solution.py:177
  42.5 8.6 %attend_forward.4 = (bf16[4,64,512]{2,1,0:T(8,128)(2,1)S(1)}, f32[1,2048]{1,0:T(1,128)S(1)}) custom-call(s32[3]{0:T(128)S(1)} %pad_add_fusion.me_ref, bf16[4,192,512]{2,1,0:T(8,128)(2,1)S(1)} %project.4.refs_0_, bf16[192,512]{1,0:T(8,128)(2,1)} %collective-permute-done.3.refs_1_, bf16[192,512]{1,0:T(8,128)(2,1)} %collective-permute-done.4.refs_2_, ...), custom_call_target="tpu_custom_call" | custom-call | flops 4294967296 | bytes 4194304 | tf_op jit(solution)/shard_map/attend_forward/pallas_call | solution.py:177
  51.1 18.3 %attend_forward.3 = (bf16[4,64,512]{2,1,0:T(8,128)(2,1)S(1)}, f32[1,2048]{1,0:T(1,128)S(1)}) custom-call(s32[3]{0:T(128)S(1)} %pad_add_fusion.me_ref, bf16[4,192,512]{2,1,0:T(8,128)(2,1)S(1)} %project.3.refs_0_, bf16[192,512]{1,0:T(8,128)(2,1)S(1)} %collective-permute-done.refs_1_, bf16[192,512]{1,0:T(8,128)(2,1)S(1)} %collective-permute-done.1.refs_2_, ...), custom_call_target="tpu_custom_call" | custom-call | flops 4294967296 | bytes 4194304 | tf_op jit(solution)/shard_map/attend_forward/pallas_call | solution.py:177
  70.4 2.9 %collective-permute-start.11 = (bf16[3,64,512]{2,1,0:T(8,128)(2,1)S(1)}, bf16[3,64,512]{2,1,0:T(8,128)(2,1)S(1)}, u32[]{:S(2)}, u32[]{:S(2)}) collective-permute-start(bf16[3,64,512]{2,1,0:T(8,128)(2,1)S(1)} %pad_maximum_fusion.8), channel_id=1, source_target_pairs={{0,24},{8,16},{16,8},{24,0},{1,25},{9,17},{17,9},{25,1},{2,26},{10... | collective-permute-start | bytes 589832 | tf_op jit(solution)/shard_map/ppermute | solution.py:689
  81.8 15.3 %middle_part.1 = (bf16[768,512]{1,0:T(8,128)(2,1)S(1)}, bf16[512,768]{1,0:T(8,128)(2,1)S(1)}, bf16[512,2304]{1,0:T(8,128)(2,1)}, bf16[512,1152]{1,0:T(8,128)(2,1...) custom-call(s32[3]{0:T(128)S(1)} %pad_add_fusion.me_ref, ...), custom_call_target="tpu_custom_call" | custom-call | flops 7549747200 | bytes 20971520 | tf_op jit(solution)/shard_map/middle_part/pallas_call | solution.py:377
  100.9 7.1 %early_grads.1 = (bf16[16,264,384]{2,1,0:T(8,128)(2,1)S(1)}, bf16[16,264,384]{2,1,0:T(8,128)(2,1)}) custom-call(s32[17]{0:T(128)S(1)} %pad_add_fusion.1.at_ref, bf16[512,768]{1,0:T(8,128)(2,1)S(1)} %get-tuple-element.139.n2_ref, bf16[512,2304]{1,0:T(8,128)(2,1)S(1)} %copy-done.14, bf16[512,1152]{1,0:T(8,128)(2,1)S(1)} %copy-done.15, ...), custom_call_target="tpu_custom_call" | custom-call | flops 3321888768 | bytes 14680064 | tf_op jit(solution)/shard_map/early_grads/pallas_call | solution.py:432
  115.8 4.0 %collective-permute-done.18.refs_6_ = bf16[3,64,512]{2,1,0:T(8,128)(2,1)S(1)} collective-permute-done((bf16[3,64,512]{2,1,0:T(8,128)(2,1)S(1)}, bf16[3,64,512]{2,1,0:T(8,128)(2,1)S(1)}, u32[]{:S(2)}, u32[]{:S(2)}) %collective-permute-start.18) | collective-permute-done | bytes 196640 | tf_op jit(solution)/shard_map/ppermute | solution.py:689
  121.8 12.2 %attend_backward.3.refs_0_ = bf16[4,192,512]{2,1,0:T(8,128)(2,1)S(1)} custom-call(s32[3]{0:T(128)S(1)} %pad_add_fusion.me_ref, bf16[4,192,512]{2,1,0:T(8,128)(2,1)S(1)} %project.3.refs_0_, bf16[192,512]{1,0:T(8,128)(2,1)S(1)} %collective-permute-done.refs_1_, bf16[192,512]{1,0:T(8,128)(2,1)S(1)} %collective-permute-done.1.refs_2_, ...), custom_call_target="tpu_custom_call" | custom-call | flops 10737418240 | bytes 6291456 | tf_op jit(solution)/shard_map/attend_backward/pallas_call | solution.py:280
  134.0 5.2 %collective-permute-done.20 = bf16[4,264,384]{2,1,0:T(8,128)(2,1)S(1)} collective-permute-done((bf16[4,264,384]{2,1,0:T(8,128)(2,1)S(1)}, bf16[4,264,384]{2,1,0:T(8,128)(2,1)S(1)}, u32[]{:S(2)}, u32[]{:S(2)}) %collective-permute-start.20) | collective-permute-done | bytes 811040 | tf_op jit(solution)/shard_map/ppermute | solution.py:689
  142.8 13.7 %attend_backward.4.refs_1_ = bf16[4,192,512]{2,1,0:T(8,128)(2,1)S(1)} custom-call(s32[3]{0:T(128)S(1)} %pad_add_fusion.me_ref, bf16[4,192,512]{2,1,0:T(8,128)(2,1)S(1)} %project.4.refs_0_, bf16[192,512]{1,0:T(8,128)(2,1)} %collective-permute-done.3.refs_1_, bf16[192,512]{1,0:T(8,128)(2,1)} %collective-permute-done.4.refs_2_, ...), custom_call_target="tpu_custom_call" | custom-call | flops 10737418240 | bytes 6291456 | tf_op jit(solution)/shard_map/attend_backward/pallas_call | solution.py:280
  156.8 3.6 %collective-permute-start.26 = (bf16[264,384]{1,0:T(8,128)(2,1)S(1)}, bf16[264,384]{1,0:T(8,128)(2,1)S(1)}, u32[]{:S(2)}, u32[]{:S(2)}) collective-permute-start(bf16[264,384]{1,0:T(8,128)(2,1)S(1)} %get-tuple-element.221), channel_id=1, source_target_pairs={{0,6},{2,4},{4,2},{6,0},{1,7},{3,5},{5,3},{7,1},{8,14},{10,12},{12... | collective-permute-start | bytes 608264 | tf_op jit(solution)/shard_map/ppermute | solution.py:689
  163.4 13.7 %attend_backward.5.refs_2_ = bf16[4,192,512]{2,1,0:T(8,128)(2,1)S(1)} custom-call(s32[3]{0:T(128)S(1)} %pad_add_fusion.me_ref, bf16[4,192,512]{2,1,0:T(8,128)(2,1)S(1)} %project.5.refs_0_, bf16[192,512]{1,0:T(8,128)(2,1)} %collective-permute-done.6.refs_1_, bf16[192,512]{1,0:T(8,128)(2,1)} %collective-permute-done.7.refs_2_, ...), custom_call_target="tpu_custom_call" | custom-call | flops 10737418240 | bytes 6291456 | tf_op jit(solution)/shard_map/attend_backward/pallas_call | solution.py:280
  181.6 4.4 %collective-permute-done.29.refs_3_ = bf16[2,192,512]{2,1,0:T(8,128)(2,1)S(1)} collective-permute-done((bf16[2,192,512]{2,1,0:T(8,128)(2,1)S(1)}, bf16[2,192,512]{2,1,0:T(8,128)(2,1)S(1)}, u32[]{:S(2)}, u32[]{:S(2)}) %collective-permute-start.29) | collective-permute-done | bytes 393248 | tf_op jit(solution)/shard_map/ppermute | solution.py:689
  187.7 2.9 %collective-permute-start.34 = (bf16[264,384]{1,0:T(8,128)(2,1)S(1)}, bf16[264,384]{1,0:T(8,128)(2,1)S(1)}, u32[]{:S(2)}, u32[]{:S(2)}) collective-permute-start(bf16[264,384]{1,0:T(8,128)(2,1)S(1)} %fusion.2), channel_id=1, source_target_pairs={{0,4},{2,6},{4,0},{6,2},{1,5},{3,7},{5,1},{7,3},{8,12},{10,14},{12... | collective-permute-start | bytes 608264 | tf_op jit(solution)/shard_map/ppermute | solution.py:689
  195.4 8.7 %collective-permute-done.31.refs_6_ = bf16[192,512]{1,0:T(8,128)(2,1)S(1)} collective-permute-done((bf16[192,512]{1,0:T(8,128)(2,1)S(1)}, bf16[192,512]{1,0:T(8,128)(2,1)S(1)}, u32[]{:S(2)}, u32[]{:S(2)}) %collective-permute-start.31) | collective-permute-done | bytes 196640 | tf_op jit(solution)/shard_map/ppermute | solution.py:689
  210.2 3.2 %collective-permute-start.40 = (bf16[9,8,768]{2,1,0:T(8,128)(2,1)S(1)}, bf16[9,8,768]{2,1,0:T(8,128)(2,1)S(1)}, u32[]{:S(2)}, u32[]{:S(2)}) collective-permute-start(bf16[9,8,768]{2,1,0:T(8,128)(2,1)S(1)} %get-tuple-element.246), channel_id=1, source_target_pairs={{0,4},{2,6},{4,0},{6,2},{1,5},{3,7},{5,1},{7,3},{8,12},{10,14},{12... | collective-permute-start | bytes 331784 | tf_op jit(solution)/shard_map/ppermute | solution.py:689
  213.5 4.8 %input_grad.1 = f32[512,768]{1,0:T(8,128)} custom-call(s32[3]{0:T(128)S(1)} %pad_add_fusion.me_ref, bf16[2,192,512]{2,1,0:T(8,128)(2,1)S(1)} %get-tuple-element.187.refs_0_, bf16[2,192,512]{2,1,0:T(8,128)(2,1)S(1)} %collective-permute-done.27.refs_1_, bf16[2,192,512]{2,1,0:T(8,128)(2,1)S(1)} %collective-permute-done.28.refs_2_, ...), custom_call_target="tpu_custom_call" | custom-call | flops 1811939328 | bytes 10485760 | tf_op jit(solution)/shard_map/input_grad/pallas_call | solution.py:675
  221.2 3.0 %collective-permute-done.37 = bf16[4,264,384]{2,1,0:T(8,128)(2,1)S(1)} collective-permute-done((bf16[4,264,384]{2,1,0:T(8,128)(2,1)S(1)}, bf16[4,264,384]{2,1,0:T(8,128)(2,1)S(1)}, u32[]{:S(2)}, u32[]{:S(2)}) %collective-permute-start.37) | collective-permute-done | bytes 811040 | tf_op jit(solution)/shard_map/ppermute | solution.py:689
  229.9 4.0 %collective-permute-start.45 = (bf16[9,8,768]{2,1,0:T(8,128)(2,1)S(1)}, bf16[9,8,768]{2,1,0:T(8,128)(2,1)S(1)}, u32[]{:S(2)}, u32[]{:S(2)}) collective-permute-start(bf16[9,8,768]{2,1,0:T(8,128)(2,1)S(1)} %fusion.12), channel_id=1, source_target_pairs={{0,4},{2,6},{4,0},{6,2},{1,5},{3,7},{5,1},{7,3},{8,12},{10,14},{12... | collective-permute-start | bytes 331784 | tf_op jit(solution)/shard_map/ppermute | solution.py:689
  234.3 6.0 %collective-permute-done.45 = bf16[9,8,768]{2,1,0:T(8,128)(2,1)S(1)} collective-permute-done((bf16[9,8,768]{2,1,0:T(8,128)(2,1)S(1)}, bf16[9,8,768]{2,1,0:T(8,128)(2,1)S(1)}, u32[]{:S(2)}, u32[]{:S(2)}) %collective-permute-start.45) | collective-permute-done | bytes 110624 | tf_op jit(solution)/shard_map/ppermute | solution.py:689
  243.5 10.3 %collective-permute-done.47.refs_1_ = bf16[4,9,8,768]{3,2,1,0:T(8,128)(2,1)S(1)} collective-permute-done((bf16[4,9,8,768]{3,2,1,0:T(8,128)(2,1)S(1)}, bf16[4,9,8,768]{3,2,1,0:T(8,128)(2,1)S(1)}, u32[]{:S(2)}, u32[]{:S(2)}) %collective-permute-start.47) | collective-permute-done | bytes 442400 | tf_op jit(solution)/shard_map/ppermute | solution.py:689
  256.9 6.4 %assemble_early.1 = (f32[768,2304]{1,0:T(8,128)}, f32[1152,768]{1,0:T(8,128)}, f32[768,768]{1,0:T(8,128)}, f32[1,768]{1,0:T(1,128)S(1)}) custom-call(s32[3]{0:T(128)S(1)} %pad_add_fusion.me_ref, bf16[4,4,264,384]{3,2,1,0:T(8,128)(2,1)S(1)} %pad_maximum_fusion.mine_ref, bf16[4,4,264,384]{3,2,1,0:T(8,128)(2,1)S(1)} %collective-permute-done.49.other_ref, ...), custom_call_target="tpu_custom_call" | custom-call | flops 1048576 | bytes 25165824 | tf_op jit(solution)/shard_map/assemble_early/pallas_call | solution.py:533
  266.3 12.1 %assemble_late.1 = (f32[768,2304]{1,0:T(8,128)}, f32[1,768]{1,0:T(1,128)}) custom-call(s32[3]{0:T(128)} %copy-done.12, bf16[4,9,8,768]{3,2,1,0:T(8,128)(2,1)} %copy-done.17, bf16[4,9,8,768]{3,2,1,0:T(8,128)(2,1)} %copy-done.21, bf16[4,9,8,768]{3,2,1,0:T(8,128)(2,1)} %copy-done.22, bf16[2,9,8,768]{3,2,1,0:T(8,128)(2,1)} %copy-done.30, ...), custom_call_target="tpu_custom_call" | custom-call | flops 1048576 | bytes 14680064 | tf_op jit(solution)/shard_map/assemble_late/pallas_call | solution.py:614
  (222 shorter events, 96.1 us)
Async XLA Ops:
  10.4 15.0 %collective-permute-start.6 = (bf16[192,512]{1,0:T(8,128)(2,1)}, bf16[192,512]{1,0:T(8,128)(2,1)}, u32[]{:S(2)}, u32[]{:S(2)}) collective-permute-start(bf16[192,512]{1,0:T(8,128)(2,1)} %get-tuple-element.243), channel_id=1, source_target_pairs={{0,8},{8,0},{16,24},{24,16},{1,9},{9,1},{17,25},{25,17},{2,10},{10... | collective-permute-start | bytes 589832 | tf_op jit(solution)/shard_map/ppermute | solution.py:689
  17.8 21.2 %collective-permute-start.3 = (bf16[192,512]{1,0:T(8,128)(2,1)}, bf16[192,512]{1,0:T(8,128)(2,1)}, u32[]{:S(2)}, u32[]{:S(2)}) collective-permute-start(bf16[192,512]{1,0:T(8,128)(2,1)} %get-tuple-element.240), channel_id=1, source_target_pairs={{0,8},{8,0},{16,24},{24,16},{1,9},{9,1},{17,25},{25,17},{2,10},{10... | collective-permute-start | bytes 589832 | tf_op jit(solution)/shard_map/ppermute | solution.py:689
  19.7 19.4 %collective-permute-start.4 = (bf16[192,512]{1,0:T(8,128)(2,1)}, bf16[192,512]{1,0:T(8,128)(2,1)}, u32[]{:S(2)}, u32[]{:S(2)}) collective-permute-start(bf16[192,512]{1,0:T(8,128)(2,1)} %get-tuple-element.239), channel_id=1, source_target_pairs={{0,16},{8,24},{16,0},{24,8},{1,17},{9,25},{17,1},{25,9},{2,18},{10... | collective-permute-start | bytes 589832 | tf_op jit(solution)/shard_map/ppermute | solution.py:689
  25.4 15.5 %collective-permute-start.5 = (bf16[192,512]{1,0:T(8,128)(2,1)}, bf16[192,512]{1,0:T(8,128)(2,1)S(1)}, u32[]{:S(2)}, u32[]{:S(2)}) collective-permute-start(bf16[192,512]{1,0:T(8,128)(2,1)} %get-tuple-element.238), channel_id=1, source_target_pairs={{0,24},{8,16},{16,8},{24,0},{1,25},{9,17},{17,9},{25,1},{2,26},{10... | collective-permute-start | bytes 589832 | tf_op jit(solution)/shard_map/ppermute | solution.py:689
  25.5 25.6 %collective-permute-start = (bf16[192,512]{1,0:T(8,128)(2,1)S(1)}, bf16[192,512]{1,0:T(8,128)(2,1)S(1)}, u32[]{:S(2)}, u32[]{:S(2)}) collective-permute-start(bf16[192,512]{1,0:T(8,128)(2,1)S(1)} %get-tuple-element.237), channel_id=1, source_target_pairs={{0,8},{8,0},{16,24},{24,16},{1,9},{9,1},{17,25},{25,17},{2,10},{10... | collective-permute-start | bytes 589832 | tf_op jit(solution)/shard_map/ppermute | solution.py:689
  27.5 23.6 %collective-permute-start.1 = (bf16[192,512]{1,0:T(8,128)(2,1)S(1)}, bf16[192,512]{1,0:T(8,128)(2,1)S(1)}, u32[]{:S(2)}, u32[]{:S(2)}) collective-permute-start(bf16[192,512]{1,0:T(8,128)(2,1)S(1)} %get-tuple-element.236), channel_id=1, source_target_pairs={{0,16},{8,24},{16,0},{24,8},{1,17},{9,25},{17,1},{25,9},{2,18},{10... | collective-permute-start | bytes 589832 | tf_op jit(solution)/shard_map/ppermute | solution.py:689
  39.1 39.0 %collective-permute-start.12 = (bf16[512,768]{1,0:T(8,128)(2,1)S(1)}, bf16[512,768]{1,0:T(8,128)(2,1)S(1)}, u32[]{:S(2)}, u32[]{:S(2)}) collective-permute-start(bf16[512,768]{1,0:T(8,128)(2,1)S(1)} %first_norm.1.hn_ref), channel_id=1, source_target_pairs={{0,8},{8,0},{16,24},{24,16},{1,9},{9,1},{17,25},{25,17},{2,10},{10... | collective-permute-start | bytes 2359304 | tf_op jit(solution)/shard_map/ppermute | solution.py:689
  41.0 37.1 %collective-permute-start.13 = (bf16[512,768]{1,0:T(8,128)(2,1)S(1)}, bf16[512,768]{1,0:T(8,128)(2,1)S(1)}, u32[]{:S(2)}, u32[]{:S(2)}) collective-permute-start(bf16[512,768]{1,0:T(8,128)(2,1)S(1)} %first_norm.1.hn_ref), channel_id=1, source_target_pairs={{0,16},{8,24},{16,0},{24,8},{1,17},{9,25},{17,1},{25,9},{2,18},{10... | collective-permute-start | bytes 2359304 | tf_op jit(solution)/shard_map/ppermute | solution.py:689
  78.1 19.0 %collective-permute-start.14 = (bf16[256,768]{1,0:T(8,128)(2,1)S(1)}, bf16[256,768]{1,0:T(8,128)(2,1)S(1)}, u32[]{:S(2)}, u32[]{:S(2)}) collective-permute-start(bf16[256,768]{1,0:T(8,128)(2,1)S(1)} %slice.210), channel_id=1, source_target_pairs={{0,8},{8,0},{16,24},{24,16},{1,9},{9,1},{17,25},{25,17},{2,10},{10... | collective-permute-start | bytes 1179656 | tf_op jit(solution)/shard_map/ppermute | solution.py:689
  80.1 17.0 %collective-permute-start.15 = (bf16[256,768]{1,0:T(8,128)(2,1)S(1)}, bf16[256,768]{1,0:T(8,128)(2,1)S(1)}, u32[]{:S(2)}, u32[]{:S(2)}) collective-permute-start(bf16[256,768]{1,0:T(8,128)(2,1)S(1)} %slice.211), channel_id=1, source_target_pairs={{0,16},{8,24},{16,0},{24,8},{1,17},{9,25},{17,1},{25,9},{2,18},{10... | collective-permute-start | bytes 1179656 | tf_op jit(solution)/shard_map/ppermute | solution.py:689
  119.8 19.4 %collective-permute-start.20 = (bf16[4,264,384]{2,1,0:T(8,128)(2,1)S(1)}, bf16[4,264,384]{2,1,0:T(8,128)(2,1)S(1)}, u32[]{:S(2)}, u32[]{:S(2)}) collective-permute-start(bf16[4,264,384]{2,1,0:T(8,128)(2,1)S(1)} %get-tuple-element.155), channel_id=1, source_target_pairs={{0,8},{8,0},{16,24},{24,16},{1,9},{9,1},{17,25},{25,17},{2,10},{10... | collective-permute-start | bytes 2433032 | tf_op jit(solution)/shard_map/ppermute | solution.py:689
  121.3 19.1 %collective-permute-start.21 = (bf16[4,264,384]{2,1,0:T(8,128)(2,1)S(1)}, bf16[4,264,384]{2,1,0:T(8,128)(2,1)S(1)}, u32[]{:S(2)}, u32[]{:S(2)}) collective-permute-start(bf16[4,264,384]{2,1,0:T(8,128)(2,1)S(1)} %get-tuple-element.156), channel_id=1, source_target_pairs={{0,16},{8,24},{16,0},{24,8},{1,17},{9,25},{17,1},{25,9},{2,18},{10... | collective-permute-start | bytes 2433032 | tf_op jit(solution)/shard_map/ppermute | solution.py:689
  140.7 15.8 %collective-permute-start.22 = (bf16[2,264,384]{2,1,0:T(8,128)(2,1)S(1)}, bf16[2,264,384]{2,1,0:T(8,128)(2,1)S(1)}, u32[]{:S(2)}, u32[]{:S(2)}) collective-permute-start(bf16[2,264,384]{2,1,0:T(8,128)(2,1)S(1)} %get-tuple-element.224), channel_id=1, source_target_pairs={{0,16},{8,24},{16,0},{24,8},{1,17},{9,25},{17,1},{25,9},{2,18},{10... | collective-permute-start | bytes 1216520 | tf_op jit(solution)/shard_map/ppermute | solution.py:689
  141.3 15.2 %collective-permute-start.23 = (bf16[2,264,384]{2,1,0:T(8,128)(2,1)S(1)}, bf16[2,264,384]{2,1,0:T(8,128)(2,1)S(1)}, u32[]{:S(2)}, u32[]{:S(2)}) collective-permute-start(bf16[2,264,384]{2,1,0:T(8,128)(2,1)S(1)} %get-tuple-element.223), channel_id=1, source_target_pairs={{0,8},{8,0},{16,24},{24,16},{1,9},{9,1},{17,25},{25,17},{2,10},{10... | collective-permute-start | bytes 1216520 | tf_op jit(solution)/shard_map/ppermute | solution.py:689
  156.8 20.4 %collective-permute-start.26 = (bf16[264,384]{1,0:T(8,128)(2,1)S(1)}, bf16[264,384]{1,0:T(8,128)(2,1)S(1)}, u32[]{:S(2)}, u32[]{:S(2)}) collective-permute-start(bf16[264,384]{1,0:T(8,128)(2,1)S(1)} %get-tuple-element.221), channel_id=1, source_target_pairs={{0,6},{2,4},{4,2},{6,0},{1,7},{3,5},{5,3},{7,1},{8,14},{10,12},{12... | collective-permute-start | bytes 608264 | tf_op jit(solution)/shard_map/ppermute | solution.py:689
  160.4 21.0 %collective-permute-start.25 = (bf16[264,384]{1,0:T(8,128)(2,1)S(1)}, bf16[264,384]{1,0:T(8,128)(2,1)S(1)}, u32[]{:S(2)}, u32[]{:S(2)}) collective-permute-start(bf16[264,384]{1,0:T(8,128)(2,1)S(1)} %get-tuple-element.220), channel_id=1, source_target_pairs={{0,4},{2,6},{4,0},{6,2},{1,5},{3,7},{5,1},{7,3},{8,12},{10,14},{12... | collective-permute-start | bytes 608264 | tf_op jit(solution)/shard_map/ppermute | solution.py:689
  160.4 21.0 %collective-permute-start.24 = (bf16[264,384]{1,0:T(8,128)(2,1)S(1)}, bf16[264,384]{1,0:T(8,128)(2,1)S(1)}, u32[]{:S(2)}, u32[]{:S(2)}) collective-permute-start(bf16[264,384]{1,0:T(8,128)(2,1)S(1)} %get-tuple-element.222), channel_id=1, source_target_pairs={{0,2},{2,0},{4,6},{6,4},{1,3},{3,1},{5,7},{7,5},{8,10},{10,8},{12,... | collective-permute-start | bytes 608264 | tf_op jit(solution)/shard_map/ppermute | solution.py:689
  161.4 20.2 %collective-permute-start.27 = (bf16[2,192,512]{2,1,0:T(8,128)(2,1)S(1)}, bf16[2,192,512]{2,1,0:T(8,128)(2,1)S(1)}, u32[]{:S(2)}, u32[]{:S(2)}) collective-permute-start(bf16[2,192,512]{2,1,0:T(8,128)(2,1)S(1)} %get-tuple-element.227), channel_id=1, source_target_pairs={{0,8},{8,0},{16,24},{24,16},{1,9},{9,1},{17,25},{25,17},{2,10},{10... | collective-permute-start | bytes 1179656 | tf_op jit(solution)/shard_map/ppermute | solution.py:689
  161.9 19.6 %collective-permute-start.28 = (bf16[2,192,512]{2,1,0:T(8,128)(2,1)S(1)}, bf16[2,192,512]{2,1,0:T(8,128)(2,1)S(1)}, u32[]{:S(2)}, u32[]{:S(2)}) collective-permute-start(bf16[2,192,512]{2,1,0:T(8,128)(2,1)S(1)} %get-tuple-element.228), channel_id=1, source_target_pairs={{0,16},{8,24},{16,0},{24,8},{1,17},{9,25},{17,1},{25,9},{2,18},{10... | collective-permute-start | bytes 1179656 | tf_op jit(solution)/shard_map/ppermute | solution.py:689
  186.6 17.6 %collective-permute-start.33 = (bf16[264,384]{1,0:T(8,128)(2,1)S(1)}, bf16[264,384]{1,0:T(8,128)(2,1)S(1)}, u32[]{:S(2)}, u32[]{:S(2)}) collective-permute-start(bf16[264,384]{1,0:T(8,128)(2,1)S(1)} %fusion.2), channel_id=1, source_target_pairs={{0,2},{2,0},{4,6},{6,4},{1,3},{3,1},{5,7},{7,5},{8,10},{10,8},{12,... | collective-permute-start | bytes 608264 | tf_op jit(solution)/shard_map/ppermute | solution.py:689
  187.7 17.5 %collective-permute-start.34 = (bf16[264,384]{1,0:T(8,128)(2,1)S(1)}, bf16[264,384]{1,0:T(8,128)(2,1)S(1)}, u32[]{:S(2)}, u32[]{:S(2)}) collective-permute-start(bf16[264,384]{1,0:T(8,128)(2,1)S(1)} %fusion.2), channel_id=1, source_target_pairs={{0,4},{2,6},{4,0},{6,2},{1,5},{3,7},{5,1},{7,3},{8,12},{10,14},{12... | collective-permute-start | bytes 608264 | tf_op jit(solution)/shard_map/ppermute | solution.py:689
  205.4 18.8 %collective-permute-start.37 = (bf16[4,264,384]{2,1,0:T(8,128)(2,1)S(1)}, bf16[4,264,384]{2,1,0:T(8,128)(2,1)S(1)}, u32[]{:S(2)}, u32[]{:S(2)}) collective-permute-start(bf16[4,264,384]{2,1,0:T(8,128)(2,1)S(1)} %get-tuple-element.230), channel_id=1, source_target_pairs={{0,8},{8,0},{16,24},{24,16},{1,9},{9,1},{17,25},{25,17},{2,10},{10... | collective-permute-start | bytes 2433032 | tf_op jit(solution)/shard_map/ppermute | solution.py:689
  207.0 18.4 %collective-permute-start.38 = (bf16[4,264,384]{2,1,0:T(8,128)(2,1)S(1)}, bf16[4,264,384]{2,1,0:T(8,128)(2,1)S(1)}, u32[]{:S(2)}, u32[]{:S(2)}) collective-permute-start(bf16[4,264,384]{2,1,0:T(8,128)(2,1)S(1)} %get-tuple-element.230), channel_id=1, source_target_pairs={{0,16},{8,24},{16,0},{24,8},{1,17},{9,25},{17,1},{25,9},{2,18},{10... | collective-permute-start | bytes 2433032 | tf_op jit(solution)/shard_map/ppermute | solution.py:689
  243.5 19.9 %collective-permute-start.52 = (bf16[4,9,8,768]{3,2,1,0:T(8,128)(2,1)S(1)}, bf16[4,9,8,768]{3,2,1,0:T(8,128)(2,1)S(1)}, u32[]{:S(2)}, u32[]{:S(2)}) collective-permute-start(bf16[4,9,8,768]{3,2,1,0:T(8,128)(2,1)S(1)} %pad_maximum_fusion.3.refs_0_), channel_id=1, source_target_pairs={{0,1},{1,0},{2,3},{3,2},{4,5},{5,4},{6,7},{7,6},{8,9},{9,8},{10,11... | collective-permute-start | bytes 1327112 | tf_op jit(solution)/shard_map/ppermute | solution.py:689
  (68 other events, 1036.3 us)
where the time goes:
time: 283 us; the launch traced here: 280 us
  Pallas kernels  130 us (46%)
  starting transfers between devices  66.8 us (24%)
  waiting for transfers between devices  58.5 us (21%)
  local copies, waits for them, and re-layouts  14.6 us (5%)
  other arithmetic  8.07 us (3%)
    ppermute x57, starting transfers between devices, swap(): return lax.ppermute(values, axis, [(i, i ^ k) for i in range(size)])  66.8 us
    ppermute x57, waiting for transfers between devices, swap(): return lax.ppermute(values, axis, [(i, i ^ k) for i in range(size)])  58.5 us
    pallas_call x3, Pallas kernels, attend_backward(): pl.pallas_call(functools.partial(backward_kernel, bq, parts), grid_spec=p...  39.7 us
    pallas_call x3, Pallas kernels, attend_forward(): pl.pallas_call(functools.partial(forward_kernel, bq, parts), grid_spec=pl...  35.6 us
    pallas_call x1, Pallas kernels, middle_part(): pl.pallas_call(functools.partial(middle_kernel, parts), in_specs=[pl.Bloc...  15.3 us
    pallas_call x1, Pallas kernels, assemble_late(): pl.pallas_call(late_kernel, grid_spec=pltpu.PrefetchScalarGridSpec(num_sc...  12.1 us
    unnamed x70, local copies, waits for them, and re-layouts  9.87 us
    pallas_call x1, Pallas kernels, early_grads(): pl.pallas_call(early_grad_kernel, grid_spec=pltpu.PrefetchScalarGridSpec(...  7.11 us
  transfers between devices with their start and end apart: 57, of which 20 were waited for; matrix products, arithmetic and copies ran while one was open for 2% of the time, Pallas kernels for 39%

commit v1 on v0

--- a/solution.py
+++ b/solution.py
@@ -52,7 +52,7 @@
         ],
         out_specs=pl.BlockSpec((rows, D), lambda i: (i, 0)),
         out_shape=jax.ShapeDtypeStruct(tokens.shape, BF16),
-        compiler_params=pltpu.CompilerParams(vmem_limit_bytes=8 << 20),
+        compiler_params=pltpu.CompilerParams(vmem_limit_bytes=6 << 20),
         cost_estimate=cost(1 << 20, 2 << 20),
         name="first_norm",
     )(tokens, norm_one[None, :])
@@ -204,7 +204,7 @@
     )(me, *slots, key_doc, query_doc)
 
 
-def backward_kernel(bq, parts, me_ref, *refs):
+def backward_kernel(bq, parts, turn, me_ref, *refs):
     slots, ups = refs[:parts], refs[parts : 2 * parts]
     (kdoc_ref, qdoc_ref, o_ref, lse_ref, cos_ref, sin_ref, grad_ref,
      qkv_s, key_s, value_s, up_s, dk_s, dv_s) = refs[2 * parts :]
@@ -254,7 +254,7 @@
             term = dot(keys, grad_scores)
             dq = term if dq is None else dq + term
         one, two = turn_back(dq * SCORE_SCALE, cos_ref[:, here], sin_ref[:, here])
-        slot = me_ref[0] ^ (step // ratio)
+        slot = (me_ref[0] if turn else 0) ^ (step // ratio)
         grad_ref[slot, 0:HALF, lanes] = one.astype(BF16)
         grad_ref[slot, HALF:HEAD_DIM, lanes] = two.astype(BF16)
 
@@ -265,7 +265,7 @@
     @pl.when(step == steps - 1)
     def _():
         for s in range(parts):
-            slot = me_ref[0] ^ s
+            slot = (me_ref[0] if turn else 0) ^ s
             rows = slice(s * span, (s + 1) * span)
             one, two = turn_back(dk_s[rows, :].T * SCORE_SCALE, cos_ref[:, rows], sin_ref[:, rows])
             grad_ref[slot, HEAD_DIM : HEAD_DIM + HALF, :] = one.astype(BF16)
@@ -273,12 +273,14 @@
             grad_ref[slot, 2 * HEAD_DIM :, :] = dv_s[rows, :].T.astype(BF16)
 
 
-def attend_backward(me, slots, key_doc, query_doc, upstream, piece, context, lse, cosine, sine, bq):
+def attend_backward(
+    me, slots, key_doc, query_doc, upstream, piece, context, lse, cosine, sine, bq, turn
+):
     parts, _, span = slots[0].shape
     total = parts * span
     ratio = span // bq
     return pl.pallas_call(
-        functools.partial(backward_kernel, bq, parts),
+        functools.partial(backward_kernel, bq, parts, turn),
         grid_spec=pltpu.PrefetchScalarGridSpec(
             num_scalar_prefetch=1,
             grid=(total // bq,),
@@ -380,7 +382,7 @@
         out_specs=[vmem] * len(out_shape),
         out_shape=out_shape,
         scratch_shapes=[pltpu.VMEM((D, span), BF16)],
-        compiler_params=pltpu.CompilerParams(vmem_limit_bytes=50 << 20),
+        compiler_params=pltpu.CompilerParams(vmem_limit_bytes=18 << 20),
         cost_estimate=cost(2 * span * D * (2 * D + 5 * FF + 2 * FF), 20 << 20),
         name="middle_part",
     )(me, *slots, tokens, cotangent, w_out, norm_two[None, :], w_in, w_down)
@@ -438,7 +440,7 @@
             out_specs=[once(shape), once(shape)],
         ),
         out_shape=[shape, shape],
-        compiler_params=pltpu.CompilerParams(vmem_limit_bytes=44 << 20),
+        compiler_params=pltpu.CompilerParams(vmem_limit_bytes=28 << 20),
         cost_estimate=cost(2 * n2.shape[0] * 4224 * D, 14 << 20),
         name="early_grads",
     )(early_places(me, parts, near), *operands)
@@ -475,7 +477,7 @@
         in_specs=[pl.BlockSpec(memory_space=pltpu.SMEM)] + [vmem] * (pieces + 1),
         out_specs=[vmem, vmem],
         out_shape=[shape, shape],
-        compiler_params=pltpu.CompilerParams(vmem_limit_bytes=32 << 20),
+        compiler_params=pltpu.CompilerParams(vmem_limit_bytes=12 << 20),
         cost_estimate=cost(2 * 2048 * 576 * D, 6 << 20),
         name="late_grads",
     )(me, *grads, hn_row)
@@ -555,7 +557,7 @@
             jax.ShapeDtypeStruct((D, D), F32),
             jax.ShapeDtypeStruct((1, D), F32),
         ],
-        compiler_params=pltpu.CompilerParams(vmem_limit_bytes=24 << 20),
+        compiler_params=pltpu.CompilerParams(vmem_limit_bytes=12 << 20),
         cost_estimate=cost(1 << 20, 24 << 20),
         name="assemble_early",
     )(me, mine, other, w_in, norm_two[None, :])
@@ -563,74 +565,49 @@
 
 def late_kernel(me_ref, *refs):
     mine, other = refs[:5], refs[5:10]
-    w_ref, norm_ref, out_ref, gain_ref, rows_s, part_s, unit_s = refs[10:]
-    block = pl.program_id(0)
+    w_ref, norm_ref, out_ref, gain_ref, rows_s = refs[10:]
     near = mine[0].shape[0]
     pieces = mine[0].shape[1] // 3
-    low = me_ref[2] == 0
-    row = (block % pieces) * 3 + block // pieces
-
-    @pl.when(block == 0)
-    def _():
-        ones = lax.broadcasted_iota(jnp.int32, unit_s.shape, 0) == lax.broadcasted_iota(
-            jnp.int32, unit_s.shape, 1
-        )
-        unit_s[...] = ones.astype(F32).astype(BF16)
-
-    for k in range(4):
-        for q in range(near):
-            which = k if k < 3 else 3 + q // (near // 2)
-            place = q if k < 3 else q % (near // 2)
-            kept, swapped = mine[which][place, row], other[which][place, row]
-            at = (me_ref[0] ^ k) * HEAD_DIM + (me_ref[1] ^ q) * 8
-            lower = jnp.where(low, kept.astype(F32), swapped.astype(F32))
-            upper = jnp.where(low, swapped.astype(F32), kept.astype(F32))
-            rows_s[pl.ds(pl.multiple_of(at, 8), 8), :] = lower
-            rows_s[pl.ds(pl.multiple_of(at + HALF, 8), 8), :] = upper
-    wide = lax.dot_general(
-        unit_s[...], rows_s[...].astype(BF16), (((1,), (1,)), ((), ())), preferred_element_type=F32
-    )
-    out_ref[...] = wide
-    part = fold_lanes(wide * w_ref[...].astype(F32))
-
-    @pl.when(block == 0)
-    def _():
-        part_s[...] = part
-
-    @pl.when(block > 0)
-    def _():
-        part_s[...] += part
-
-    @pl.when(block == pl.num_programs(0) - 1)
-    def _():
-        gain_ref[...] = jnp.sum(part_s[...].T, axis=0, keepdims=True) / norm_ref[...]
+    width = rows_s.shape[1]
+    lanes = pl.ds(pl.multiple_of(pl.program_id(0) * 128, 128), 128)
+    total = None
+    for block in range(3 * pieces):
+        row = (block % pieces) * 3 + block // pieces
+        for k in range(4):
+            for q in range(near):
+                which = k if k < 3 else 3 + q // (near // 2)
+                place = q if k < 3 else q % (near // 2)
+                at = (me_ref[0] ^ k) * HEAD_DIM + (me_ref[1] ^ q) * 8
+                for ref, core in ((mine, me_ref[2]), (other, 1 - me_ref[2])):
+                    here = pl.ds(pl.multiple_of(at + core * HALF, 8), 8)
+                    rows_s[block, here, :] = ref[which][place, row, :, lanes].astype(F32)
+        wide = rows_s[block].T
+        cols = slice(block * width, (block + 1) * width)
+        out_ref[:, cols] = wide
+        part = fold_lanes(wide * w_ref[:, cols].astype(F32))
+        total = part if total is None else total + part
+    gain_ref[...] = jnp.sum(total.T, axis=0, keepdims=True) / norm_ref[...]
 
 
 def assemble_late(me, mine, other, w_qkv, norm_one):
-    groups, blocks = 4, mine[0].shape[1]
-    pieces = blocks // 3
-    width = groups * HEAD_DIM
+    blocks = mine[0].shape[1]
     sums = [pl.BlockSpec(v.shape, lambda b, me: (0, 0, 0, 0)) for v in mine]
     return pl.pallas_call(
         late_kernel,
         grid_spec=pltpu.PrefetchScalarGridSpec(
             num_scalar_prefetch=1,
-            grid=(blocks,),
+            grid=(D // 128,),
             in_specs=sums
             + sums
             + [
-                pl.BlockSpec((D, width), lambda b, me: (0, b)),
-                pl.BlockSpec((1, D), lambda b, me: (0, 0)),
+                pl.BlockSpec((128, 3 * D), lambda b, me: (b, 0)),
+                pl.BlockSpec((1, 128), lambda b, me: (0, b)),
             ],
             out_specs=[
-                pl.BlockSpec((D, width), lambda b, me: (0, b)),
-                pl.BlockSpec((1, D), lambda b, me: (0, 0)),
-            ],
-            scratch_shapes=[
-                pltpu.VMEM((width, D), F32),
-                pltpu.VMEM((D, 128), F32),
-                pltpu.VMEM((D, D), BF16),
-            ],
+                pl.BlockSpec((128, 3 * D), lambda b, me: (b, 0)),
+                pl.BlockSpec((1, 128), lambda b, me: (0, b)),
+            ],
+            scratch_shapes=[pltpu.VMEM((blocks, 3 * D // blocks, 128), F32)],
         ),
         out_shape=[
             jax.ShapeDtypeStruct((D, 3 * D), F32),
@@ -678,7 +655,7 @@
         out_specs=vmem,
         out_shape=jax.ShapeDtypeStruct((span, D), F32),
         scratch_shapes=[pltpu.VMEM((3 * D, span), BF16)],
-        compiler_params=pltpu.CompilerParams(vmem_limit_bytes=40 << 20),
+        compiler_params=pltpu.CompilerParams(vmem_limit_bytes=20 << 20),
         cost_estimate=cost(2 * span * 3 * D * D, 10 << 20),
         name="input_grad",
     )(me, *pair, *last, w_qkv, tokens, norm_one[None, :], grad_middle)
@@ -769,7 +746,8 @@
 
     def backward(j, upstream):
         return attend_backward(
-            me, qkv[j], key_doc, query_doc, upstream, j, contexts[j], lses[j], cosine, sine, bq
+            me, qkv[j], key_doc, query_doc, upstream, j, contexts[j], lses[j], cosine, sine, bq,
+            True,
         )
 
     from_one, from_two = swap(send_one, "seq", 1), swap(send_two, "seq", 2)
@@ -786,15 +764,15 @@
     early = scatter_near(early)
     grads.append(backward(2, upstream))
 
-    kept, given = late_grads(me, grads, hn_row, near)
-    grads, early, pair, kept, given = tie(grads, early, pair, kept, given)
+    grads, early, pair[1], pair[2] = tie(grads, early, pair[1], pair[2])
+    early = sum_far(early)
+    slots = [early] + [swap(early, "near", k) for k in range(1, near)]
     last = [grads[2][0]] + [swap(grads[2][k], "seq", k) for k in range(1, parts)]
-    early = sum_far(early)
-    slots = [early, swap(early, "near", 1), swap(early, "near", 2), swap(early, "near", 3)]
-    late = add(kept, swap(given, "core", 1))
-    last, slots, late = tie(last, slots, late)
+    last, slots, grads, pair = tie(last, slots, grads, pair)
     early = jnp.stack(slots)
     one, two = swap(early, "seq", 1), swap(early, "seq", 2)
+    kept, given = late_grads(me, grads, hn_row, near)
+    late = add(kept, swap(given, "core", 1))
     late = sum_far(scatter_near(late))
     grad_input = input_grad(me, pair, last, w_qkv, tokens[0], norm_one, grad_middle)
     one, two, late, grad_input = tie(one, two, late, grad_input)

time: 283 us -> 266 us (0.940)
  Pallas kernels: 130 us -> 122 us
  starting transfers between devices: 66.8 us -> 62.6 us
  local copies, waits for them, and re-layouts: 14.6 us -> 10.8 us
    ppermute x57, starting transfers between devices: 66.8 us -> 62.6 us  [swap(): return lax.ppermute(values, axis, [(i, i ^ k) for i in range(size)])]
    unnamed x70 -> x54, local copies, waits for them, and re-layouts: 9.87 us -> 6.09 us
    pallas_call x1, Pallas kernels: 15.3 us -> 11.8 us  [middle_part(): pl.pallas_call(functools.partial(middle_kernel, parts), in_specs=[pl.Bloc...]
    pallas_call x1, Pallas kernels: 12.1 us -> 8.9 us  [assemble_late(): pl.pallas_call(late_kernel, grid_spec=pltpu.PrefetchScalarGridSpec(num_sc...]
where the time goes in v1:
time: 266 us; the launch traced here: 263 us
  Pallas kernels  122 us (46%)
  starting transfers between devices  62.6 us (24%)
  waiting for transfers between devices  59.2 us (22%)
  local copies, waits for them, and re-layouts  10.8 us (4%)
  other arithmetic  7.24 us (3%)
    ppermute x57, starting transfers between devices, swap(): return lax.ppermute(values, axis, [(i, i ^ k) for i in range(size)])  62.6 us
    ppermute x57, waiting for transfers between devices, swap(): return lax.ppermute(values, axis, [(i, i ^ k) for i in range(size)])  59.2 us
    pallas_call x3, Pallas kernels, attend_backward(): pl.pallas_call(functools.partial(backward_kernel, bq, parts, turn), grid_...  39.5 us
    pallas_call x3, Pallas kernels, attend_forward(): pl.pallas_call(functools.partial(forward_kernel, bq, parts), grid_spec=pl...  35.6 us
    pallas_call x1, Pallas kernels, middle_part(): pl.pallas_call(functools.partial(middle_kernel, parts), in_specs=[pl.Bloc...  11.8 us
    pallas_call x1, Pallas kernels, assemble_late(): pl.pallas_call(late_kernel, grid_spec=pltpu.PrefetchScalarGridSpec(num_sc...  8.9 us
    pallas_call x1, Pallas kernels, assemble_early(): pl.pallas_call(early_kernel, grid_spec=pltpu.PrefetchScalarGridSpec(num_s...  6.43 us
    pallas_call x3, Pallas kernels, project(): pl.pallas_call(project_kernel, grid_spec=pltpu.PrefetchScalarGridSpec(num...  6.17 us
  transfers between devices with their start and end apart: 57, of which 20 were waited for; matrix products, arithmetic and copies ran while one was open for 2% of the time, Pallas kernels for 39%

profile of v1, /device:TPU:0, one launch (start us, length us, event | category | flops | bytes accessed | tf_op | source)
XLA Modules:
  0.0 263.1 jit_solution(14053323609109736064)
XLA Ops:
  10.4 2.9 %collective-permute-start.6 = (bf16[192,512]{1,0:T(8,128)(2,1)}, bf16[192,512]{1,0:T(8,128)(2,1)}, u32[]{:S(2)}, u32[]{:S(2)}) collective-permute-start(bf16[192,512]{1,0:T(8,128)(2,1)} %get-tuple-element.251), channel_id=1, source_target_pairs={{0,8},{8,0},{16,24},{24,16},{1,9},{9,1},{17,25},{25,17},{2,10},{10... | collective-permute-start | bytes 589832 | tf_op jit(solution)/shard_map/ppermute | solution.py:666
  30.2 8.6 %attend_forward.5 = (bf16[4,64,512]{2,1,0:T(8,128)(2,1)S(1)}, f32[1,2048]{1,0:T(1,128)S(1)}) custom-call(s32[3]{0:T(128)S(1)} %pad_add_fusion.me_ref, bf16[4,192,512]{2,1,0:T(8,128)(2,1)S(1)} %project.5.refs_0_, bf16[192,512]{1,0:T(8,128)(2,1)} %collective-permute-done.6.refs_1_, bf16[192,512]{1,0:T(8,128)(2,1)} %collective-permute-done.7.refs_2_, ...), custom_call_target="tpu_custom_call" | custom-call | flops 4294967296 | bytes 4194304 | tf_op jit(solution)/shard_map/attend_forward/pallas_call | solution.py:177
  42.5 8.6 %attend_forward.4 = (bf16[4,64,512]{2,1,0:T(8,128)(2,1)S(1)}, f32[1,2048]{1,0:T(1,128)S(1)}) custom-call(s32[3]{0:T(128)S(1)} %pad_add_fusion.me_ref, bf16[4,192,512]{2,1,0:T(8,128)(2,1)S(1)} %project.4.refs_0_, bf16[192,512]{1,0:T(8,128)(2,1)} %collective-permute-done.3.refs_1_, bf16[192,512]{1,0:T(8,128)(2,1)} %collective-permute-done.4.refs_2_, ...), custom_call_target="tpu_custom_call" | custom-call | flops 4294967296 | bytes 4194304 | tf_op jit(solution)/shard_map/attend_forward/pallas_call | solution.py:177
  51.1 18.4 %attend_forward.3 = (bf16[4,64,512]{2,1,0:T(8,128)(2,1)S(1)}, f32[1,2048]{1,0:T(1,128)S(1)}) custom-call(s32[3]{0:T(128)S(1)} %pad_add_fusion.me_ref, bf16[4,192,512]{2,1,0:T(8,128)(2,1)S(1)} %project.3.refs_0_, bf16[192,512]{1,0:T(8,128)(2,1)S(1)} %collective-permute-done.refs_1_, bf16[192,512]{1,0:T(8,128)(2,1)S(1)} %collective-permute-done.1.refs_2_, ...), custom_call_target="tpu_custom_call" | custom-call | flops 4294967296 | bytes 4194304 | tf_op jit(solution)/shard_map/attend_forward/pallas_call | solution.py:177
  81.9 11.8 %middle_part.1 = (bf16[768,512]{1,0:T(8,128)(2,1)S(1)}, bf16[512,768]{1,0:T(8,128)(2,1)S(1)}, bf16[512,2304]{1,0:T(8,128)(2,1)S(1)}, bf16[512,1152]{1,0:T(8,128)...) custom-call(s32[3]{0:T(128)S(1)} %pad_add_fusion.me_ref, ...), custom_call_target="tpu_custom_call" | custom-call | flops 7549747200 | bytes 20971520 | tf_op jit(solution)/shard_map/middle_part/pallas_call | solution.py:379
  93.7 5.4 %early_grads.1 = (bf16[16,264,384]{2,1,0:T(8,128)(2,1)S(1)}, bf16[16,264,384]{2,1,0:T(8,128)(2,1)S(1)}) custom-call(s32[17]{0:T(128)S(1)} %pad_add_fusion.1.at_ref, bf16[512,768]{1,0:T(8,128)(2,1)S(1)} %get-tuple-element.143.n2_ref, bf16[512,2304]{1,0:T(8,128)(2,1)S(1)} %get-tuple-element.144.gu_ref, bf16[512,1152]{1,0:T(8,128)(2,1)S(1)} %get-tuple-element.145.inner_ref, ...), custom_call_target="tpu_custom_call" | custom-call | flops 3321888768 | bytes 14680064 | tf_op jit(solution)/shard_map/early_grads/pallas_call | solution.py:434
  106.9 4.0 %collective-permute-done.18.refs_6_ = bf16[3,64,512]{2,1,0:T(8,128)(2,1)S(1)} collective-permute-done((bf16[3,64,512]{2,1,0:T(8,128)(2,1)S(1)}, bf16[3,64,512]{2,1,0:T(8,128)(2,1)S(1)}, u32[]{:S(2)}, u32[]{:S(2)}) %collective-permute-start.18) | collective-permute-done | bytes 196640 | tf_op jit(solution)/shard_map/ppermute | solution.py:666
  112.8 12.2 %attend_backward.3.refs_0_ = bf16[4,192,512]{2,1,0:T(8,128)(2,1)S(1)} custom-call(s32[3]{0:T(128)S(1)} %pad_add_fusion.me_ref, bf16[4,192,512]{2,1,0:T(8,128)(2,1)S(1)} %project.3.refs_0_, bf16[192,512]{1,0:T(8,128)(2,1)S(1)} %collective-permute-done.refs_1_, bf16[192,512]{1,0:T(8,128)(2,1)S(1)} %collective-permute-done.1.refs_2_, ...), custom_call_target="tpu_custom_call" | custom-call | flops 10737418240 | bytes 6291456 | tf_op jit(solution)/shard_map/attend_backward/pallas_call | solution.py:282
  125.1 5.1 %collective-permute-done.20 = bf16[4,264,384]{2,1,0:T(8,128)(2,1)S(1)} collective-permute-done((bf16[4,264,384]{2,1,0:T(8,128)(2,1)S(1)}, bf16[4,264,384]{2,1,0:T(8,128)(2,1)S(1)}, u32[]{:S(2)}, u32[]{:S(2)}) %collective-permute-start.20) | collective-permute-done | bytes 811040 | tf_op jit(solution)/shard_map/ppermute | solution.py:666
  133.8 13.7 %attend_backward.4.refs_1_ = bf16[4,192,512]{2,1,0:T(8,128)(2,1)S(1)} custom-call(s32[3]{0:T(128)S(1)} %pad_add_fusion.me_ref, bf16[4,192,512]{2,1,0:T(8,128)(2,1)S(1)} %project.4.refs_0_, bf16[192,512]{1,0:T(8,128)(2,1)} %collective-permute-done.3.refs_1_, bf16[192,512]{1,0:T(8,128)(2,1)} %collective-permute-done.4.refs_2_, ...), custom_call_target="tpu_custom_call" | custom-call | flops 10737418240 | bytes 6291456 | tf_op jit(solution)/shard_map/attend_backward/pallas_call | solution.py:282
  147.7 3.6 %collective-permute-start.26 = (bf16[264,384]{1,0:T(8,128)(2,1)S(1)}, bf16[264,384]{1,0:T(8,128)(2,1)S(1)}, u32[]{:S(2)}, u32[]{:S(2)}) collective-permute-start(bf16[264,384]{1,0:T(8,128)(2,1)S(1)} %get-tuple-element.229), channel_id=1, source_target_pairs={{0,6},{2,4},{4,2},{6,0},{1,7},{3,5},{5,3},{7,1},{8,14},{10,12},{12... | collective-permute-start | bytes 608264 | tf_op jit(solution)/shard_map/ppermute | solution.py:666
  154.4 13.6 %attend_backward.5.refs_2_ = bf16[4,192,512]{2,1,0:T(8,128)(2,1)S(1)} custom-call(s32[3]{0:T(128)S(1)} %pad_add_fusion.me_ref, bf16[4,192,512]{2,1,0:T(8,128)(2,1)S(1)} %project.5.refs_0_, bf16[192,512]{1,0:T(8,128)(2,1)} %collective-permute-done.6.refs_1_, bf16[192,512]{1,0:T(8,128)(2,1)} %collective-permute-done.7.refs_2_, ...), custom_call_target="tpu_custom_call" | custom-call | flops 10737418240 | bytes 6291456 | tf_op jit(solution)/shard_map/attend_backward/pallas_call | solution.py:282
  171.8 3.0 %collective-permute-start.33 = (bf16[264,384]{1,0:T(8,128)(2,1)S(1)}, bf16[264,384]{1,0:T(8,128)(2,1)S(1)}, u32[]{:S(2)}, u32[]{:S(2)}) collective-permute-start(bf16[264,384]{1,0:T(8,128)(2,1)S(1)} %fusion.2), channel_id=1, source_target_pairs={{0,4},{2,6},{4,0},{6,2},{1,5},{3,7},{5,1},{7,3},{8,12},{10,14},{12... | collective-permute-start | bytes 608264 | tf_op jit(solution)/shard_map/ppermute | solution.py:666
  174.9 3.5 %collective-permute-done.35.refs_3_ = bf16[2,192,512]{2,1,0:T(8,128)(2,1)S(1)} collective-permute-done((bf16[2,192,512]{2,1,0:T(8,128)(2,1)S(1)}, bf16[2,192,512]{2,1,0:T(8,128)(2,1)S(1)}, u32[]{:S(2)}, u32[]{:S(2)}) %collective-permute-start.35) | collective-permute-done | bytes 393248 | tf_op jit(solution)/shard_map/ppermute | solution.py:666
  184.7 3.4 %collective-permute-done.31.refs_7_ = bf16[192,512]{1,0:T(8,128)(2,1)S(1)} collective-permute-done((bf16[192,512]{1,0:T(8,128)(2,1)S(1)}, bf16[192,512]{1,0:T(8,128)(2,1)S(1)}, u32[]{:S(2)}, u32[]{:S(2)}) %collective-permute-start.31) | collective-permute-done | bytes 196640 | tf_op jit(solution)/shard_map/ppermute | solution.py:666
  193.0 3.7 %collective-permute-start.41 = (bf16[9,8,768]{2,1,0:T(8,128)(2,1)S(1)}, bf16[9,8,768]{2,1,0:T(8,128)(2,1)S(1)}, u32[]{:S(2)}, u32[]{:S(2)}) collective-permute-start(bf16[9,8,768]{2,1,0:T(8,128)(2,1)S(1)} %get-tuple-element.253), channel_id=1, source_target_pairs={{0,6},{2,4},{4,2},{6,0},{1,7},{3,5},{5,3},{7,1},{8,14},{10,12},{12... | collective-permute-start | bytes 331784 | tf_op jit(solution)/shard_map/ppermute | solution.py:666
  197.4 4.8 %input_grad.1 = f32[512,768]{1,0:T(8,128)} custom-call(s32[3]{0:T(128)S(1)} %pad_add_fusion.me_ref, bf16[2,192,512]{2,1,0:T(8,128)(2,1)S(1)} %get-tuple-element.195.refs_0_, bf16[2,192,512]{2,1,0:T(8,128)(2,1)S(1)} %collective-permute-done.27.refs_1_, bf16[2,192,512]{2,1,0:T(8,128)(2,1)S(1)} %collective-permute-done.28.refs_2_, ...), custom_call_target="tpu_custom_call" | custom-call | flops 1811939328 | bytes 10485760 | tf_op jit(solution)/shard_map/input_grad/pallas_call | solution.py:652
  202.2 3.8 %collective-permute-done.40 = bf16[9,8,768]{2,1,0:T(8,128)(2,1)S(1)} collective-permute-done((bf16[9,8,768]{2,1,0:T(8,128)(2,1)S(1)}, bf16[9,8,768]{2,1,0:T(8,128)(2,1)S(1)}, u32[]{:S(2)}, u32[]{:S(2)}) %collective-permute-start.40) | collective-permute-done | bytes 110624 | tf_op jit(solution)/shard_map/ppermute | solution.py:666
  206.1 5.5 %collective-permute-done.36 = bf16[4,264,384]{2,1,0:T(8,128)(2,1)S(1)} collective-permute-done((bf16[4,264,384]{2,1,0:T(8,128)(2,1)S(1)}, bf16[4,264,384]{2,1,0:T(8,128)(2,1)S(1)}, u32[]{:S(2)}, u32[]{:S(2)}) %collective-permute-start.36) | collective-permute-done | bytes 811040 | tf_op jit(solution)/shard_map/ppermute | solution.py:666
  214.3 3.6 %collective-permute-start.46 = (bf16[9,8,768]{2,1,0:T(8,128)(2,1)S(1)}, bf16[9,8,768]{2,1,0:T(8,128)(2,1)S(1)}, u32[]{:S(2)}, u32[]{:S(2)}) collective-permute-start(bf16[9,8,768]{2,1,0:T(8,128)(2,1)S(1)} %fusion.12), channel_id=1, source_target_pairs={{0,6},{2,4},{4,2},{6,0},{1,7},{3,5},{5,3},{7,1},{8,14},{10,12},{12... | collective-permute-start | bytes 331784 | tf_op jit(solution)/shard_map/ppermute | solution.py:666
  221.4 4.6 %collective-permute-done.45 = bf16[9,8,768]{2,1,0:T(8,128)(2,1)S(1)} collective-permute-done((bf16[9,8,768]{2,1,0:T(8,128)(2,1)S(1)}, bf16[9,8,768]{2,1,0:T(8,128)(2,1)S(1)}, u32[]{:S(2)}, u32[]{:S(2)}) %collective-permute-start.45) | collective-permute-done | bytes 110624 | tf_op jit(solution)/shard_map/ppermute | solution.py:666
  229.8 9.6 %collective-permute-done.47.refs_1_ = bf16[4,9,8,768]{3,2,1,0:T(8,128)(2,1)S(1)} collective-permute-done((bf16[4,9,8,768]{3,2,1,0:T(8,128)(2,1)S(1)}, bf16[4,9,8,768]{3,2,1,0:T(8,128)(2,1)S(1)}, u32[]{:S(2)}, u32[]{:S(2)}) %collective-permute-start.47) | collective-permute-done | bytes 442400 | tf_op jit(solution)/shard_map/ppermute | solution.py:666
  243.3 6.4 %assemble_early.1 = (f32[768,2304]{1,0:T(8,128)}, f32[1152,768]{1,0:T(8,128)}, f32[768,768]{1,0:T(8,128)}, f32[1,768]{1,0:T(1,128)S(1)}) custom-call(s32[3]{0:T(128)S(1)} %pad_add_fusion.me_ref, bf16[4,4,264,384]{3,2,1,0:T(8,128)(2,1)S(1)} %pad_maximum_fusion.mine_ref, bf16[4,4,264,384]{3,2,1,0:T(8,128)(2,1)S(1)} %collective-permute-done.49.other_ref, ...), custom_call_target="tpu_custom_call" | custom-call | flops 1048576 | bytes 25165824 | tf_op jit(solution)/shard_map/assemble_early/pallas_call | solution.py:535
  252.7 8.9 %assemble_late.1 = (f32[768,2304]{1,0:T(8,128)}, f32[1,768]{1,0:T(1,128)}) custom-call(s32[3]{0:T(128)} %copy-done.11, bf16[4,9,8,768]{3,2,1,0:T(8,128)(2,1)} %copy-done.16, bf16[4,9,8,768]{3,2,1,0:T(8,128)(2,1)} %copy-done.17, bf16[4,9,8,768]{3,2,1,0:T(8,128)(2,1)} %copy-done.18, bf16[2,9,8,768]{3,2,1,0:T(8,128)(2,1)} %copy-done.22, ...), custom_call_target="tpu_custom_call" | custom-call | flops 1048576 | bytes 14680064 | tf_op jit(solution)/shard_map/assemble_late/pallas_call | solution.py:595
  (206 shorter events, 92.9 us)
Async XLA Ops:
  10.4 15.0 %collective-permute-start.6 = (bf16[192,512]{1,0:T(8,128)(2,1)}, bf16[192,512]{1,0:T(8,128)(2,1)}, u32[]{:S(2)}, u32[]{:S(2)}) collective-permute-start(bf16[192,512]{1,0:T(8,128)(2,1)} %get-tuple-element.251), channel_id=1, source_target_pairs={{0,8},{8,0},{16,24},{24,16},{1,9},{9,1},{17,25},{25,17},{2,10},{10... | collective-permute-start | bytes 589832 | tf_op jit(solution)/shard_map/ppermute | solution.py:666
  17.8 21.1 %collective-permute-start.3 = (bf16[192,512]{1,0:T(8,128)(2,1)}, bf16[192,512]{1,0:T(8,128)(2,1)}, u32[]{:S(2)}, u32[]{:S(2)}) collective-permute-start(bf16[192,512]{1,0:T(8,128)(2,1)} %get-tuple-element.248), channel_id=1, source_target_pairs={{0,8},{8,0},{16,24},{24,16},{1,9},{9,1},{17,25},{25,17},{2,10},{10... | collective-permute-start | bytes 589832 | tf_op jit(solution)/shard_map/ppermute | solution.py:666
  19.7 19.3 %collective-permute-start.4 = (bf16[192,512]{1,0:T(8,128)(2,1)}, bf16[192,512]{1,0:T(8,128)(2,1)}, u32[]{:S(2)}, u32[]{:S(2)}) collective-permute-start(bf16[192,512]{1,0:T(8,128)(2,1)} %get-tuple-element.247), channel_id=1, source_target_pairs={{0,16},{8,24},{16,0},{24,8},{1,17},{9,25},{17,1},{25,9},{2,18},{10... | collective-permute-start | bytes 589832 | tf_op jit(solution)/shard_map/ppermute | solution.py:666
  25.4 15.5 %collective-permute-start.5 = (bf16[192,512]{1,0:T(8,128)(2,1)}, bf16[192,512]{1,0:T(8,128)(2,1)S(1)}, u32[]{:S(2)}, u32[]{:S(2)}) collective-permute-start(bf16[192,512]{1,0:T(8,128)(2,1)} %get-tuple-element.246), channel_id=1, source_target_pairs={{0,24},{8,16},{16,8},{24,0},{1,25},{9,17},{17,9},{25,1},{2,26},{10... | collective-permute-start | bytes 589832 | tf_op jit(solution)/shard_map/ppermute | solution.py:666
  25.5 25.5 %collective-permute-start = (bf16[192,512]{1,0:T(8,128)(2,1)S(1)}, bf16[192,512]{1,0:T(8,128)(2,1)S(1)}, u32[]{:S(2)}, u32[]{:S(2)}) collective-permute-start(bf16[192,512]{1,0:T(8,128)(2,1)S(1)} %get-tuple-element.245), channel_id=1, source_target_pairs={{0,8},{8,0},{16,24},{24,16},{1,9},{9,1},{17,25},{25,17},{2,10},{10... | collective-permute-start | bytes 589832 | tf_op jit(solution)/shard_map/ppermute | solution.py:666
  27.5 23.6 %collective-permute-start.1 = (bf16[192,512]{1,0:T(8,128)(2,1)S(1)}, bf16[192,512]{1,0:T(8,128)(2,1)S(1)}, u32[]{:S(2)}, u32[]{:S(2)}) collective-permute-start(bf16[192,512]{1,0:T(8,128)(2,1)S(1)} %get-tuple-element.244), channel_id=1, source_target_pairs={{0,16},{8,24},{16,0},{24,8},{1,17},{9,25},{17,1},{25,9},{2,18},{10... | collective-permute-start | bytes 589832 | tf_op jit(solution)/shard_map/ppermute | solution.py:666
  39.1 39.1 %collective-permute-start.12 = (bf16[512,768]{1,0:T(8,128)(2,1)S(1)}, bf16[512,768]{1,0:T(8,128)(2,1)S(1)}, u32[]{:S(2)}, u32[]{:S(2)}) collective-permute-start(bf16[512,768]{1,0:T(8,128)(2,1)S(1)} %first_norm.1.hn_ref), channel_id=1, source_target_pairs={{0,8},{8,0},{16,24},{24,16},{1,9},{9,1},{17,25},{25,17},{2,10},{10... | collective-permute-start | bytes 2359304 | tf_op jit(solution)/shard_map/ppermute | solution.py:666
  41.0 37.2 %collective-permute-start.13 = (bf16[512,768]{1,0:T(8,128)(2,1)S(1)}, bf16[512,768]{1,0:T(8,128)(2,1)S(1)}, u32[]{:S(2)}, u32[]{:S(2)}) collective-permute-start(bf16[512,768]{1,0:T(8,128)(2,1)S(1)} %first_norm.1.hn_ref), channel_id=1, source_target_pairs={{0,16},{8,24},{16,0},{24,8},{1,17},{9,25},{17,1},{25,9},{2,18},{10... | collective-permute-start | bytes 2359304 | tf_op jit(solution)/shard_map/ppermute | solution.py:666
  78.2 15.5 %collective-permute-start.14 = (bf16[256,768]{1,0:T(8,128)(2,1)S(1)}, bf16[256,768]{1,0:T(8,128)(2,1)S(1)}, u32[]{:S(2)}, u32[]{:S(2)}) collective-permute-start(bf16[256,768]{1,0:T(8,128)(2,1)S(1)} %slice.210), channel_id=1, source_target_pairs={{0,8},{8,0},{16,24},{24,16},{1,9},{9,1},{17,25},{25,17},{2,10},{10... | collective-permute-start | bytes 1179656 | tf_op jit(solution)/shard_map/ppermute | solution.py:666
  110.9 19.3 %collective-permute-start.20 = (bf16[4,264,384]{2,1,0:T(8,128)(2,1)S(1)}, bf16[4,264,384]{2,1,0:T(8,128)(2,1)S(1)}, u32[]{:S(2)}, u32[]{:S(2)}) collective-permute-start(bf16[4,264,384]{2,1,0:T(8,128)(2,1)S(1)} %get-tuple-element.159), channel_id=1, source_target_pairs={{0,8},{8,0},{16,24},{24,16},{1,9},{9,1},{17,25},{25,17},{2,10},{10... | collective-permute-start | bytes 2433032 | tf_op jit(solution)/shard_map/ppermute | solution.py:666
  112.4 19.0 %collective-permute-start.21 = (bf16[4,264,384]{2,1,0:T(8,128)(2,1)S(1)}, bf16[4,264,384]{2,1,0:T(8,128)(2,1)S(1)}, u32[]{:S(2)}, u32[]{:S(2)}) collective-permute-start(bf16[4,264,384]{2,1,0:T(8,128)(2,1)S(1)} %get-tuple-element.160), channel_id=1, source_target_pairs={{0,16},{8,24},{16,0},{24,8},{1,17},{9,25},{17,1},{25,9},{2,18},{10... | collective-permute-start | bytes 2433032 | tf_op jit(solution)/shard_map/ppermute | solution.py:666
  131.7 15.8 %collective-permute-start.22 = (bf16[2,264,384]{2,1,0:T(8,128)(2,1)S(1)}, bf16[2,264,384]{2,1,0:T(8,128)(2,1)S(1)}, u32[]{:S(2)}, u32[]{:S(2)}) collective-permute-start(bf16[2,264,384]{2,1,0:T(8,128)(2,1)S(1)} %get-tuple-element.232), channel_id=1, source_target_pairs={{0,16},{8,24},{16,0},{24,8},{1,17},{9,25},{17,1},{25,9},{2,18},{10... | collective-permute-start | bytes 1216520 | tf_op jit(solution)/shard_map/ppermute | solution.py:666
  132.3 15.2 %collective-permute-start.23 = (bf16[2,264,384]{2,1,0:T(8,128)(2,1)S(1)}, bf16[2,264,384]{2,1,0:T(8,128)(2,1)S(1)}, u32[]{:S(2)}, u32[]{:S(2)}) collective-permute-start(bf16[2,264,384]{2,1,0:T(8,128)(2,1)S(1)} %get-tuple-element.231), channel_id=1, source_target_pairs={{0,8},{8,0},{16,24},{24,16},{1,9},{9,1},{17,25},{25,17},{2,10},{10... | collective-permute-start | bytes 1216520 | tf_op jit(solution)/shard_map/ppermute | solution.py:666
  147.7 20.2 %collective-permute-start.26 = (bf16[264,384]{1,0:T(8,128)(2,1)S(1)}, bf16[264,384]{1,0:T(8,128)(2,1)S(1)}, u32[]{:S(2)}, u32[]{:S(2)}) collective-permute-start(bf16[264,384]{1,0:T(8,128)(2,1)S(1)} %get-tuple-element.229), channel_id=1, source_target_pairs={{0,6},{2,4},{4,2},{6,0},{1,7},{3,5},{5,3},{7,1},{8,14},{10,12},{12... | collective-permute-start | bytes 608264 | tf_op jit(solution)/shard_map/ppermute | solution.py:666
  151.4 18.2 %collective-permute-start.25 = (bf16[264,384]{1,0:T(8,128)(2,1)S(1)}, bf16[264,384]{1,0:T(8,128)(2,1)S(1)}, u32[]{:S(2)}, u32[]{:S(2)}) collective-permute-start(bf16[264,384]{1,0:T(8,128)(2,1)S(1)} %get-tuple-element.228), channel_id=1, source_target_pairs={{0,4},{2,6},{4,0},{6,2},{1,5},{3,7},{5,1},{7,3},{8,12},{10,14},{12... | collective-permute-start | bytes 608264 | tf_op jit(solution)/shard_map/ppermute | solution.py:666
  151.4 18.2 %collective-permute-start.24 = (bf16[264,384]{1,0:T(8,128)(2,1)S(1)}, bf16[264,384]{1,0:T(8,128)(2,1)S(1)}, u32[]{:S(2)}, u32[]{:S(2)}) collective-permute-start(bf16[264,384]{1,0:T(8,128)(2,1)S(1)} %get-tuple-element.230), channel_id=1, source_target_pairs={{0,2},{2,0},{4,6},{6,4},{1,3},{3,1},{5,7},{7,5},{8,10},{10,8},{12,... | collective-permute-start | bytes 608264 | tf_op jit(solution)/shard_map/ppermute | solution.py:666
  152.3 17.4 %collective-permute-start.27 = (bf16[2,192,512]{2,1,0:T(8,128)(2,1)S(1)}, bf16[2,192,512]{2,1,0:T(8,128)(2,1)S(1)}, u32[]{:S(2)}, u32[]{:S(2)}) collective-permute-start(bf16[2,192,512]{2,1,0:T(8,128)(2,1)S(1)} %get-tuple-element.234), channel_id=1, source_target_pairs={{0,8},{8,0},{16,24},{24,16},{1,9},{9,1},{17,25},{25,17},{2,10},{10... | collective-permute-start | bytes 1179656 | tf_op jit(solution)/shard_map/ppermute | solution.py:666
  153.0 16.8 %collective-permute-start.28 = (bf16[2,192,512]{2,1,0:T(8,128)(2,1)S(1)}, bf16[2,192,512]{2,1,0:T(8,128)(2,1)S(1)}, u32[]{:S(2)}, u32[]{:S(2)}) collective-permute-start(bf16[2,192,512]{2,1,0:T(8,128)(2,1)S(1)} %get-tuple-element.235), channel_id=1, source_target_pairs={{0,16},{8,24},{16,0},{24,8},{1,17},{9,25},{17,1},{25,9},{2,18},{10... | collective-permute-start | bytes 1179656 | tf_op jit(solution)/shard_map/ppermute | solution.py:666
  170.5 17.6 %collective-permute-start.32 = (bf16[264,384]{1,0:T(8,128)(2,1)S(1)}, bf16[264,384]{1,0:T(8,128)(2,1)S(1)}, u32[]{:S(2)}, u32[]{:S(2)}) collective-permute-start(bf16[264,384]{1,0:T(8,128)(2,1)S(1)} %fusion.2), channel_id=1, source_target_pairs={{0,2},{2,0},{4,6},{6,4},{1,3},{3,1},{5,7},{7,5},{8,10},{10,8},{12,... | collective-permute-start | bytes 608264 | tf_op jit(solution)/shard_map/ppermute | solution.py:666
  171.8 16.3 %collective-permute-start.33 = (bf16[264,384]{1,0:T(8,128)(2,1)S(1)}, bf16[264,384]{1,0:T(8,128)(2,1)S(1)}, u32[]{:S(2)}, u32[]{:S(2)}) collective-permute-start(bf16[264,384]{1,0:T(8,128)(2,1)S(1)} %fusion.2), channel_id=1, source_target_pairs={{0,4},{2,6},{4,0},{6,2},{1,5},{3,7},{5,1},{7,3},{8,12},{10,14},{12... | collective-permute-start | bytes 608264 | tf_op jit(solution)/shard_map/ppermute | solution.py:666
  190.9 20.6 %collective-permute-start.36 = (bf16[4,264,384]{2,1,0:T(8,128)(2,1)S(1)}, bf16[4,264,384]{2,1,0:T(8,128)(2,1)S(1)}, u32[]{:S(2)}, u32[]{:S(2)}) collective-permute-start(bf16[4,264,384]{2,1,0:T(8,128)(2,1)S(1)} %get-tuple-element.238), channel_id=1, source_target_pairs={{0,8},{8,0},{16,24},{24,16},{1,9},{9,1},{17,25},{25,17},{2,10},{10... | collective-permute-start | bytes 2433032 | tf_op jit(solution)/shard_map/ppermute | solution.py:666
  192.8 20.2 %collective-permute-start.37 = (bf16[4,264,384]{2,1,0:T(8,128)(2,1)S(1)}, bf16[4,264,384]{2,1,0:T(8,128)(2,1)S(1)}, u32[]{:S(2)}, u32[]{:S(2)}) collective-permute-start(bf16[4,264,384]{2,1,0:T(8,128)(2,1)S(1)} %get-tuple-element.238), channel_id=1, source_target_pairs={{0,16},{8,24},{16,0},{24,8},{1,17},{9,25},{17,1},{25,9},{2,18},{10... | collective-permute-start | bytes 2433032 | tf_op jit(solution)/shard_map/ppermute | solution.py:666
  226.8 13.8 %collective-permute-start.49 = (bf16[4,4,264,384]{3,2,1,0:T(8,128)(2,1)S(1)}, bf16[4,4,264,384]{3,2,1,0:T(8,128)(2,1)S(1)}, u32[]{:S(2)}, u32[]{:S(2)}) collective-permute-start(bf16[4,4,264,384]{3,2,1,0:T(8,128)(2,1)S(1)} %pad_maximum_fusion.mine_ref), channel_id=1, source_target_pairs={{0,1},{1,0},{2,3},{3,2},{4,5},{5,4},{6,7},{7,6},{8,9},{9,8},{10,11... | collective-permute-start | bytes 9732104 | tf_op jit(solution)/shard_map/ppermute | solution.py:666
  229.8 19.9 %collective-permute-start.52 = (bf16[4,9,8,768]{3,2,1,0:T(8,128)(2,1)S(1)}, bf16[4,9,8,768]{3,2,1,0:T(8,128)(2,1)S(1)}, u32[]{:S(2)}, u32[]{:S(2)}) collective-permute-start(bf16[4,9,8,768]{3,2,1,0:T(8,128)(2,1)S(1)} %pad_maximum_fusion.3.refs_0_), channel_id=1, source_target_pairs={{0,1},{1,0},{2,3},{3,2},{4,5},{5,4},{6,7},{7,6},{8,9},{9,8},{10,11... | collective-permute-start | bytes 1327112 | tf_op jit(solution)/shard_map/ppermute | solution.py:666
  (60 other events, 949.9 us)

commit v2 on v1

--- a/solution.py
+++ b/solution.py
@@ -98,11 +98,18 @@
 
 def mask_scores(scores, chunk, chunks, edge, key_doc, query_doc, query_main):
     if chunk == 0 or chunk == chunks - 1:
-        own = key_doc[chunk * KEY_CHUNK : (chunk + 1) * KEY_CHUNK, :]
+        own = key_doc[: KEY_CHUNK, :] if chunk == 0 else key_doc[KEY_CHUNK :, :]
         return jnp.where(own == query_doc, scores, MASKED_SCORE)
     if edge:
         return jnp.where(query_main, scores, MASKED_SCORE)
     return scores
+
+
+def put_edges(doc_ref, edge_s):
+    total = doc_ref.shape[1]
+    for i, at in enumerate((0, total - KEY_CHUNK)):
+        tall = jnp.broadcast_to(doc_ref[:, at : at + KEY_CHUNK], (8, KEY_CHUNK)).T
+        edge_s[i * KEY_CHUNK : (i + 1) * KEY_CHUNK, :] = tall[:, :1]
 
 
 def put_in_order(me, slots, qkv_s, key_s, value_s=None):
@@ -125,7 +132,7 @@
 
 def forward_kernel(bq, parts, me_ref, *refs):
     slots = refs[:parts]
-    kdoc_ref, qdoc_ref, out_ref, lse_ref, qkv_s, key_s, score_s = refs[parts:]
+    doc_ref, out_ref, lse_ref, qkv_s, key_s, edge_s, score_s = refs[parts:]
     step = pl.program_id(0)
     steps = pl.num_programs(0)
     total = key_s.shape[0]
@@ -136,17 +143,18 @@
     @pl.when(step == 0)
     def _():
         put_in_order(me_ref[0], slots, qkv_s, key_s)
+        put_edges(doc_ref, edge_s)
 
     def run(edge):
         lanes = pl.ds(pl.multiple_of((step % ratio) * bq, bq), bq)
         queries = qkv_s[step // ratio, 0:HEAD_DIM, lanes]
-        query_doc = qdoc_ref[...]
-        query_main = query_doc == kdoc_ref[total // 2 : total // 2 + 1, :]
+        query_doc = doc_ref[:, pl.ds(pl.multiple_of(step * bq, bq), bq)]
+        query_main = query_doc == doc_ref[:, total // 2 : total // 2 + 1]
         top = None
         for c in range(chunks):
             rows = slice(c * KEY_CHUNK, (c + 1) * KEY_CHUNK)
             scores = dot(key_s[rows, :], queries)
-            scores = mask_scores(scores, c, chunks, edge, kdoc_ref, query_doc, query_main)
+            scores = mask_scores(scores, c, chunks, edge, edge_s, query_doc, query_main)
             score_s[rows, :] = scores
             peak = jnp.max(scores.reshape(KEY_CHUNK // 8, 8, bq), axis=0)
             top = peak if top is None else jnp.maximum(top, peak)
@@ -170,7 +178,7 @@
     pl.when(jnp.logical_not(at_edge))(lambda: run(False))
 
 
-def attend_forward(me, slots, key_doc, query_doc, bq):
+def attend_forward(me, slots, docs, bq):
     parts, _, span = slots[0].shape
     total = parts * span
     ratio = span // bq
@@ -181,8 +189,7 @@
             grid=(total // bq,),
             in_specs=slot_specs(slots)
             + [
-                pl.BlockSpec((total, 1), lambda i, me: (0, 0)),
-                pl.BlockSpec((1, bq), lambda i, me: (0, i)),
+                pl.BlockSpec((1, total), lambda i, me: (0, 0)),
             ],
             out_specs=[
                 pl.BlockSpec((1, HEAD_DIM, bq), lambda i, me: (i // ratio ^ me[0], 0, i % ratio)),
@@ -191,6 +198,7 @@
             scratch_shapes=[
                 pltpu.VMEM((parts, WIDE, span), BF16),
                 pltpu.VMEM((total, HEAD_DIM), BF16),
+                pltpu.VMEM((2 * KEY_CHUNK, 1), jnp.int32),
                 pltpu.VMEM((total, bq), F32),
             ],
         ),
@@ -201,13 +209,13 @@
         compiler_params=pltpu.CompilerParams(vmem_limit_bytes=40 << 20),
         cost_estimate=cost(16 * HEAD_DIM * total * total, 4 << 20, total * total),
         name="attend_forward",
-    )(me, *slots, key_doc, query_doc)
+    )(me, *slots, docs)
 
 
 def backward_kernel(bq, parts, turn, me_ref, *refs):
     slots, ups = refs[:parts], refs[parts : 2 * parts]
-    (kdoc_ref, qdoc_ref, o_ref, lse_ref, cos_ref, sin_ref, grad_ref,
-     qkv_s, key_s, value_s, up_s, dk_s, dv_s) = refs[2 * parts :]
+    (doc_ref, o_ref, lse_ref, cos_ref, sin_ref, grad_ref,
+     qkv_s, key_s, value_s, up_s, edge_s, dk_s, dv_s) = refs[2 * parts :]
     step = pl.program_id(0)
     steps = pl.num_programs(0)
     total = key_s.shape[0]
@@ -218,6 +226,7 @@
     @pl.when(step == 0)
     def _():
         put_in_order(me_ref[0], slots, qkv_s, key_s, value_s)
+        put_edges(doc_ref, edge_s)
         for k, ref in enumerate(ups):
             up_s[me_ref[0] ^ k] = ref[...].reshape(HEAD_DIM, span)
         dk_s[...] = jnp.zeros_like(dk_s)
@@ -236,14 +245,14 @@
         centre = jnp.sum(wide_up * o_ref[0].astype(F32), axis=0, keepdims=True)
         query_rows = queries.astype(F32).T.astype(BF16)
         up_rows = wide_up.T.astype(BF16)
-        query_doc = qdoc_ref[...]
-        query_main = query_doc == kdoc_ref[total // 2 : total // 2 + 1, :]
+        query_doc = doc_ref[:, pl.ds(pl.multiple_of(step * bq, bq), bq)]
+        query_main = query_doc == doc_ref[:, total // 2 : total // 2 + 1]
         lse = lse_ref[...]
         dq = None
         for c in range(chunks):
             rows = slice(c * KEY_CHUNK, (c + 1) * KEY_CHUNK)
             scores = dot(key_s[rows, :], queries)
-            scores = mask_scores(scores, c, chunks, edge, kdoc_ref, query_doc, query_main)
+            scores = mask_scores(scores, c, chunks, edge, edge_s, query_doc, query_main)
             probs = jnp.exp2(scores * SCORE_EXP2 - lse)
             grad_prob = dot(value_s[rows, :], upstream)
             grad_scores = (probs * (grad_prob - centre)).astype(BF16)
@@ -274,7 +283,7 @@
 
 
 def attend_backward(
-    me, slots, key_doc, query_doc, upstream, piece, context, lse, cosine, sine, bq, turn
+    me, slots, docs, upstream, piece, context, lse, cosine, sine, bq, turn
 ):
     parts, _, span = slots[0].shape
     total = parts * span
@@ -287,8 +296,7 @@
             in_specs=slot_specs(slots)
             + [pl.BlockSpec((1, HEAD_DIM, span), lambda i, me: (piece, 0, 0))] * parts
             + [
-                pl.BlockSpec((total, 1), lambda i, me: (0, 0)),
-                pl.BlockSpec((1, bq), lambda i, me: (0, i)),
+                pl.BlockSpec((1, total), lambda i, me: (0, 0)),
                 pl.BlockSpec((1, HEAD_DIM, bq), lambda i, me: (i // ratio ^ me[0], 0, i % ratio)),
                 pl.BlockSpec((1, bq), lambda i, me: (0, i)),
                 pl.BlockSpec((HALF, total), lambda i, me: (0, 0)),
@@ -300,6 +308,7 @@
                 pltpu.VMEM((total, HEAD_DIM), BF16),
                 pltpu.VMEM((total, HEAD_DIM), BF16),
                 pltpu.VMEM((parts, HEAD_DIM, span), BF16),
+                pltpu.VMEM((2 * KEY_CHUNK, 1), jnp.int32),
                 pltpu.VMEM((total, HEAD_DIM), F32),
                 pltpu.VMEM((total, HEAD_DIM), F32),
             ],
@@ -308,7 +317,7 @@
         compiler_params=pltpu.CompilerParams(vmem_limit_bytes=40 << 20),
         cost_estimate=cost(40 * HEAD_DIM * total * total, 6 << 20, total * total),
         name="attend_backward",
-    )(me, *slots, *upstream, key_doc, query_doc, context, lse, cosine, sine)
+    )(me, *slots, *upstream, docs, context, lse, cosine, sine)
 
 
 def dot_rows(a, b):
@@ -697,8 +706,7 @@
     me = jnp.stack([lax.axis_index(a).astype(jnp.int32) for a in ("seq", "near", "core")])
     first_token = me_seq * span
     starts = doc_start[0]
-    key_doc = starts[:, None]
-    query_doc = starts[None, :]
+    docs = doc_start
 
     frequency = ROTARY_BASE ** (-(jnp.arange(HALF, dtype=F32) * 2.0 / HEAD_DIM))
     offset = (jnp.arange(total, dtype=jnp.int32) - starts).astype(F32)
@@ -720,7 +728,7 @@
         if j == pieces - 1:
             hn_late, qkv[j] = tie(hn, qkv[j])
             hn_near = [swap(hn_late, "seq", 1), swap(hn_late, "seq", 2)]
-        context, lse = attend_forward(me, qkv[j], key_doc, query_doc, bq)
+        context, lse = attend_forward(me, qkv[j], docs, bq)
         contexts.append(context)
         lses.append(lse)
     arrived = [jnp.stack([c[k] for c in contexts]) for k in range(parts)]
@@ -746,7 +754,7 @@
 
     def backward(j, upstream):
         return attend_backward(
-            me, qkv[j], key_doc, query_doc, upstream, j, contexts[j], lses[j], cosine, sine, bq,
+            me, qkv[j], docs, upstream, j, contexts[j], lses[j], cosine, sine, bq,
             True,
         )
 
@@ -757,21 +765,25 @@
     by_one = swap(add(b_one, from_two[half:]), "seq", 1)
     grads.append(backward(1, upstream))
     grads, upstream, by_two, by_one = tie(grads, upstream, by_two, by_one)
+    kept, given = late_grads(me, grads, hn_row, near)
     own = jnp.stack(grads, axis=1)
     pair = [own[0]] + [swap(own[k], "seq", k) for k in range(1, parts)]
     early = [add(a_own[i], from_one[i], by_two[i]) for i in range(half)]
     early += [add(b_own[i], from_two[i], by_one[i]) for i in range(half)]
     early = scatter_near(early)
+    upstream, kept, given = tie(upstream, kept, given)
     grads.append(backward(2, upstream))
 
     grads, early, pair[1], pair[2] = tie(grads, early, pair[1], pair[2])
     early = sum_far(early)
     slots = [early] + [swap(early, "near", k) for k in range(1, near)]
     last = [grads[2][0]] + [swap(grads[2][k], "seq", k) for k in range(1, parts)]
-    last, slots, grads, pair = tie(last, slots, grads, pair)
+    last, slots, grads[2], pair = tie(last, slots, grads[2], pair)
     early = jnp.stack(slots)
     one, two = swap(early, "seq", 1), swap(early, "seq", 2)
-    kept, given = late_grads(me, grads, hn_row, near)
+    kept_last, given_last = late_grads(me, grads[2:], hn_row, near)
+    kept = jnp.concatenate([kept, kept_last], axis=1)
+    given = jnp.concatenate([given, given_last], axis=1)
     late = add(kept, swap(given, "core", 1))
     late = sum_far(scatter_near(late))
     grad_input = input_grad(me, pair, last, w_qkv, tokens[0], norm_one, grad_middle)

time: 266 us -> 265 us (level)
    unnamed x54 -> x50, local copies, waits for them, and re-layouts: 6.09 us -> 4.87 us
  transfers between devices with their start and end apart: 57 -> 57, of which waited for: 20 -> 21; matrix products, arithmetic and copies ran while one was open for 2% -> 2% of each run, Pallas kernels for 39% -> 39%
where the time goes in v2:
time: 265 us; the launch traced here: 263 us
  Pallas kernels  123 us (46%)
  starting transfers between devices  63.2 us (24%)
  waiting for transfers between devices  60.3 us (23%)
  local copies, waits for them, and re-layouts  8.22 us (3%)
  other arithmetic  7.12 us (3%)
    ppermute x57, starting transfers between devices, swap(): return lax.ppermute(values, axis, [(i, i ^ k) for i in range(size)])  63.2 us
    ppermute x57, waiting for transfers between devices, swap(): return lax.ppermute(values, axis, [(i, i ^ k) for i in range(size)])  60.3 us
    pallas_call x3, Pallas kernels, attend_backward(): pl.pallas_call(functools.partial(backward_kernel, bq, parts, turn), grid_...  39.6 us
    pallas_call x3, Pallas kernels, attend_forward(): pl.pallas_call(functools.partial(forward_kernel, bq, parts), grid_spec=pl...  35.7 us
    pallas_call x1, Pallas kernels, middle_part(): pl.pallas_call(functools.partial(middle_kernel, parts), in_specs=[pl.Bloc...  11.8 us
    pallas_call x1, Pallas kernels, assemble_late(): pl.pallas_call(late_kernel, grid_spec=pltpu.PrefetchScalarGridSpec(num_sc...  8.9 us
    pallas_call x1, Pallas kernels, assemble_early(): pl.pallas_call(early_kernel, grid_spec=pltpu.PrefetchScalarGridSpec(num_s...  6.43 us
    pallas_call x3, Pallas kernels, project(): pl.pallas_call(project_kernel, grid_spec=pltpu.PrefetchScalarGridSpec(num...  6.17 us
  transfers between devices with their start and end apart: 57, of which 21 were waited for; matrix products, arithmetic and copies ran while one was open for 2% of the time, Pallas kernels for 39%

profile of v2, /device:TPU:0, one launch (start us, length us, event | category | flops | bytes accessed | tf_op | source)
XLA Modules:
  0.0 263.1 jit_solution(17926791371485000099)
XLA Ops:
  10.4 2.9 %collective-permute-start.6 = (bf16[192,512]{1,0:T(8,128)(2,1)}, bf16[192,512]{1,0:T(8,128)(2,1)}, u32[]{:S(2)}, u32[]{:S(2)}) collective-permute-start(bf16[192,512]{1,0:T(8,128)(2,1)} %get-tuple-element.259), channel_id=1, source_target_pairs={{0,8},{8,0},{16,24},{24,16},{1,9},{9,1},{17,25},{25,17},{2,10},{10... | collective-permute-start | bytes 589832 | tf_op jit(solution)/shard_map/ppermute | solution.py:675
  27.7 8.7 %attend_forward.5 = (bf16[4,64,512]{2,1,0:T(8,128)(2,1)S(1)}, f32[1,2048]{1,0:T(1,128)S(1)}) custom-call(s32[3]{0:T(128)S(1)} %pad_add_fusion.me_ref, bf16[4,192,512]{2,1,0:T(8,128)(2,1)S(1)} %project.5.refs_0_, bf16[192,512]{1,0:T(8,128)(2,1)} %collective-permute-done.6.refs_1_, bf16[192,512]{1,0:T(8,128)(2,1)} %collective-permute-done.7.refs_2_, ...), custom_call_target="tpu_custom_call" | custom-call | flops 4294967296 | bytes 4194304 | tf_op jit(solution)/shard_map/attend_forward/pallas_call | solution.py:185
  40.0 8.6 %attend_forward.4 = (bf16[4,64,512]{2,1,0:T(8,128)(2,1)S(1)}, f32[1,2048]{1,0:T(1,128)S(1)}) custom-call(s32[3]{0:T(128)S(1)} %pad_add_fusion.me_ref, bf16[4,192,512]{2,1,0:T(8,128)(2,1)S(1)} %project.4.refs_0_, bf16[192,512]{1,0:T(8,128)(2,1)} %collective-permute-done.3.refs_1_, bf16[192,512]{1,0:T(8,128)(2,1)} %collective-permute-done.4.refs_2_, ...), custom_call_target="tpu_custom_call" | custom-call | flops 4294967296 | bytes 4194304 | tf_op jit(solution)/shard_map/attend_forward/pallas_call | solution.py:185
  48.7 18.4 %attend_forward.3 = (bf16[4,64,512]{2,1,0:T(8,128)(2,1)S(1)}, f32[1,2048]{1,0:T(1,128)S(1)}) custom-call(s32[3]{0:T(128)S(1)} %pad_add_fusion.me_ref, bf16[4,192,512]{2,1,0:T(8,128)(2,1)S(1)} %project.3.refs_0_, bf16[192,512]{1,0:T(8,128)(2,1)S(1)} %collective-permute-done.refs_1_, bf16[192,512]{1,0:T(8,128)(2,1)S(1)} %collective-permute-done.1.refs_2_, ...), custom_call_target="tpu_custom_call" | custom-call | flops 4294967296 | bytes 4194304 | tf_op jit(solution)/shard_map/attend_forward/pallas_call | solution.py:185
  72.9 4.2 %collective-permute-done.10.refs_2_ = bf16[3,64,512]{2,1,0:T(8,128)(2,1)S(1)} collective-permute-done((bf16[3,64,512]{2,1,0:T(8,128)(2,1)S(1)}, bf16[3,64,512]{2,1,0:T(8,128)(2,1)S(1)}, u32[]{:S(2)}, u32[]{:S(2)}) %collective-permute-start.10) | collective-permute-done | bytes 196640 | tf_op jit(solution)/shard_map/ppermute | solution.py:675
  79.8 11.8 %middle_part.1 = (bf16[768,512]{1,0:T(8,128)(2,1)S(1)}, bf16[512,768]{1,0:T(8,128)(2,1)S(1)}, bf16[512,2304]{1,0:T(8,128)(2,1)S(1)}, bf16[512,1152]{1,0:T(8,128)...) custom-call(s32[3]{0:T(128)S(1)} %pad_add_fusion.me_ref, ...), custom_call_target="tpu_custom_call" | custom-call | flops 7549747200 | bytes 20971520 | tf_op jit(solution)/shard_map/middle_part/pallas_call | solution.py:388
  91.6 5.4 %early_grads.1 = (bf16[16,264,384]{2,1,0:T(8,128)(2,1)S(1)}, bf16[16,264,384]{2,1,0:T(8,128)(2,1)S(1)}) custom-call(s32[17]{0:T(128)S(1)} %pad_add_fusion.1.at_ref, bf16[512,768]{1,0:T(8,128)(2,1)S(1)} %get-tuple-element.147.n2_ref, bf16[512,2304]{1,0:T(8,128)(2,1)S(1)} %get-tuple-element.148.gu_ref, bf16[512,1152]{1,0:T(8,128)(2,1)S(1)} %get-tuple-element.149.inner_ref, ...), custom_call_target="tpu_custom_call" | custom-call | flops 3321888768 | bytes 14680064 | tf_op jit(solution)/shard_map/early_grads/pallas_call | solution.py:443
  104.9 5.4 %collective-permute-done.18.refs_6_ = bf16[3,64,512]{2,1,0:T(8,128)(2,1)S(1)} collective-permute-done((bf16[3,64,512]{2,1,0:T(8,128)(2,1)S(1)}, bf16[3,64,512]{2,1,0:T(8,128)(2,1)S(1)}, u32[]{:S(2)}, u32[]{:S(2)}) %collective-permute-start.18) | collective-permute-done | bytes 196640 | tf_op jit(solution)/shard_map/ppermute | solution.py:675
  112.1 12.3 %attend_backward.3.refs_0_ = bf16[4,192,512]{2,1,0:T(8,128)(2,1)S(1)} custom-call(s32[3]{0:T(128)S(1)} %pad_add_fusion.me_ref, bf16[4,192,512]{2,1,0:T(8,128)(2,1)S(1)} %project.3.refs_0_, bf16[192,512]{1,0:T(8,128)(2,1)S(1)} %collective-permute-done.refs_1_, bf16[192,512]{1,0:T(8,128)(2,1)S(1)} %collective-permute-done.1.refs_2_, ...), custom_call_target="tpu_custom_call" | custom-call | flops 10737418240 | bytes 6291456 | tf_op jit(solution)/shard_map/attend_backward/pallas_call | solution.py:291
  124.4 5.3 %collective-permute-done.20 = bf16[4,264,384]{2,1,0:T(8,128)(2,1)S(1)} collective-permute-done((bf16[4,264,384]{2,1,0:T(8,128)(2,1)S(1)}, bf16[4,264,384]{2,1,0:T(8,128)(2,1)S(1)}, u32[]{:S(2)}, u32[]{:S(2)}) %collective-permute-start.20) | collective-permute-done | bytes 811040 | tf_op jit(solution)/shard_map/ppermute | solution.py:675
  132.2 13.7 %attend_backward.4.refs_1_ = bf16[4,192,512]{2,1,0:T(8,128)(2,1)S(1)} custom-call(s32[3]{0:T(128)S(1)} %pad_add_fusion.me_ref, bf16[4,192,512]{2,1,0:T(8,128)(2,1)S(1)} %project.4.refs_0_, bf16[192,512]{1,0:T(8,128)(2,1)} %collective-permute-done.3.refs_1_, bf16[192,512]{1,0:T(8,128)(2,1)} %collective-permute-done.4.refs_2_, ...), custom_call_target="tpu_custom_call" | custom-call | flops 10737418240 | bytes 6291456 | tf_op jit(solution)/shard_map/attend_backward/pallas_call | solution.py:291
  148.1 3.1 %collective-permute-start.26 = (bf16[264,384]{1,0:T(8,128)(2,1)S(1)}, bf16[264,384]{1,0:T(8,128)(2,1)S(1)}, u32[]{:S(2)}, u32[]{:S(2)}) collective-permute-start(bf16[264,384]{1,0:T(8,128)(2,1)S(1)} %get-tuple-element.237), channel_id=1, source_target_pairs={{0,6},{2,4},{4,2},{6,0},{1,7},{3,5},{5,3},{7,1},{8,14},{10,12},{12... | collective-permute-start | bytes 608264 | tf_op jit(solution)/shard_map/ppermute | solution.py:675
  154.6 13.6 %attend_backward.5.refs_0_ = bf16[4,192,512]{2,1,0:T(8,128)(2,1)S(1)} custom-call(s32[3]{0:T(128)S(1)} %pad_add_fusion.me_ref, bf16[4,192,512]{2,1,0:T(8,128)(2,1)S(1)} %project.5.refs_0_, bf16[192,512]{1,0:T(8,128)(2,1)} %collective-permute-done.6.refs_1_, bf16[192,512]{1,0:T(8,128)(2,1)} %collective-permute-done.7.refs_2_, ...), custom_call_target="tpu_custom_call" | custom-call | flops 10737418240 | bytes 6291456 | tf_op jit(solution)/shard_map/attend_backward/pallas_call | solution.py:291
  185.3 4.5 %collective-permute-done.31.refs_7_ = bf16[192,512]{1,0:T(8,128)(2,1)S(1)} collective-permute-done((bf16[192,512]{1,0:T(8,128)(2,1)S(1)}, bf16[192,512]{1,0:T(8,128)(2,1)S(1)}, u32[]{:S(2)}, u32[]{:S(2)}) %collective-permute-start.31) | collective-permute-done | bytes 196640 | tf_op jit(solution)/shard_map/ppermute | solution.py:675
  193.2 3.1 %collective-permute-start.41 = (bf16[9,8,768]{2,1,0:T(8,128)(2,1)S(1)}, bf16[9,8,768]{2,1,0:T(8,128)(2,1)S(1)}, u32[]{:S(2)}, u32[]{:S(2)}) collective-permute-start(bf16[9,8,768]{2,1,0:T(8,128)(2,1)S(1)} %get-tuple-element.261), channel_id=1, source_target_pairs={{0,6},{2,4},{4,2},{6,0},{1,7},{3,5},{5,3},{7,1},{8,14},{10,12},{12... | collective-permute-start | bytes 331784 | tf_op jit(solution)/shard_map/ppermute | solution.py:675
  197.7 4.8 %input_grad.1 = f32[512,768]{1,0:T(8,128)} custom-call(s32[3]{0:T(128)S(1)} %pad_add_fusion.me_ref, bf16[2,192,512]{2,1,0:T(8,128)(2,1)S(1)} %get-tuple-element.203.refs_0_, bf16[2,192,512]{2,1,0:T(8,128)(2,1)S(1)} %collective-permute-done.27.refs_1_, bf16[2,192,512]{2,1,0:T(8,128)(2,1)S(1)} %collective-permute-done.28.refs_2_, ...), custom_call_target="tpu_custom_call" | custom-call | flops 1811939328 | bytes 10485760 | tf_op jit(solution)/shard_map/input_grad/pallas_call | solution.py:661
  202.5 3.2 %collective-permute-done.40 = bf16[9,8,768]{2,1,0:T(8,128)(2,1)S(1)} collective-permute-done((bf16[9,8,768]{2,1,0:T(8,128)(2,1)S(1)}, bf16[9,8,768]{2,1,0:T(8,128)(2,1)S(1)}, u32[]{:S(2)}, u32[]{:S(2)}) %collective-permute-start.40) | collective-permute-done | bytes 110624 | tf_op jit(solution)/shard_map/ppermute | solution.py:675
  205.7 6.3 %collective-permute-done.36 = bf16[4,264,384]{2,1,0:T(8,128)(2,1)S(1)} collective-permute-done((bf16[4,264,384]{2,1,0:T(8,128)(2,1)S(1)}, bf16[4,264,384]{2,1,0:T(8,128)(2,1)S(1)}, u32[]{:S(2)}, u32[]{:S(2)}) %collective-permute-start.36) | collective-permute-done | bytes 811040 | tf_op jit(solution)/shard_map/ppermute | solution.py:675
  214.2 3.0 %collective-permute-start.46 = (bf16[9,8,768]{2,1,0:T(8,128)(2,1)S(1)}, bf16[9,8,768]{2,1,0:T(8,128)(2,1)S(1)}, u32[]{:S(2)}, u32[]{:S(2)}) collective-permute-start(bf16[9,8,768]{2,1,0:T(8,128)(2,1)S(1)} %fusion.12), channel_id=1, source_target_pairs={{0,6},{2,4},{4,2},{6,0},{1,7},{3,5},{5,3},{7,1},{8,14},{10,12},{12... | collective-permute-start | bytes 331784 | tf_op jit(solution)/shard_map/ppermute | solution.py:675
  218.6 3.3 %collective-permute-done.46 = bf16[9,8,768]{2,1,0:T(8,128)(2,1)S(1)} collective-permute-done((bf16[9,8,768]{2,1,0:T(8,128)(2,1)S(1)}, bf16[9,8,768]{2,1,0:T(8,128)(2,1)S(1)}, u32[]{:S(2)}, u32[]{:S(2)}) %collective-permute-start.46) | collective-permute-done | bytes 110624 | tf_op jit(solution)/shard_map/ppermute | solution.py:675
  221.9 4.2 %collective-permute-done.45 = bf16[9,8,768]{2,1,0:T(8,128)(2,1)S(1)} collective-permute-done((bf16[9,8,768]{2,1,0:T(8,128)(2,1)S(1)}, bf16[9,8,768]{2,1,0:T(8,128)(2,1)S(1)}, u32[]{:S(2)}, u32[]{:S(2)}) %collective-permute-start.45) | collective-permute-done | bytes 110624 | tf_op jit(solution)/shard_map/ppermute | solution.py:675
  229.0 10.5 %collective-permute-done.47.refs_1_ = bf16[4,9,8,768]{3,2,1,0:T(8,128)(2,1)S(1)} collective-permute-done((bf16[4,9,8,768]{3,2,1,0:T(8,128)(2,1)S(1)}, bf16[4,9,8,768]{3,2,1,0:T(8,128)(2,1)S(1)}, u32[]{:S(2)}, u32[]{:S(2)}) %collective-permute-start.47) | collective-permute-done | bytes 442400 | tf_op jit(solution)/shard_map/ppermute | solution.py:675
  243.3 6.4 %assemble_early.1 = (f32[768,2304]{1,0:T(8,128)}, f32[1152,768]{1,0:T(8,128)}, f32[768,768]{1,0:T(8,128)}, f32[1,768]{1,0:T(1,128)S(1)}) custom-call(s32[3]{0:T(128)S(1)} %pad_add_fusion.me_ref, bf16[4,4,264,384]{3,2,1,0:T(8,128)(2,1)S(1)} %pad_maximum_fusion.mine_ref, bf16[4,4,264,384]{3,2,1,0:T(8,128)(2,1)S(1)} %collective-permute-done.49.other_ref, ...), custom_call_target="tpu_custom_call" | custom-call | flops 1048576 | bytes 25165824 | tf_op jit(solution)/shard_map/assemble_early/pallas_call | solution.py:544
  252.8 8.9 %assemble_late.1 = (f32[768,2304]{1,0:T(8,128)}, f32[1,768]{1,0:T(1,128)}) custom-call(s32[3]{0:T(128)} %copy-done.8, bf16[4,9,8,768]{3,2,1,0:T(8,128)(2,1)} %copy-done.14, bf16[4,9,8,768]{3,2,1,0:T(8,128)(2,1)} %copy-done.15, bf16[4,9,8,768]{3,2,1,0:T(8,128)(2,1)} %copy-done.16, bf16[2,9,8,768]{3,2,1,0:T(8,128)(2,1)} %copy-done.20, ...), custom_call_target="tpu_custom_call" | custom-call | flops 1048576 | bytes 14680064 | tf_op jit(solution)/shard_map/assemble_late/pallas_call | solution.py:604
  (203 shorter events, 90.0 us)
Async XLA Ops:
  17.8 18.6 %collective-permute-start.3 = (bf16[192,512]{1,0:T(8,128)(2,1)}, bf16[192,512]{1,0:T(8,128)(2,1)}, u32[]{:S(2)}, u32[]{:S(2)}) collective-permute-start(bf16[192,512]{1,0:T(8,128)(2,1)} %get-tuple-element.256), channel_id=1, source_target_pairs={{0,8},{8,0},{16,24},{24,16},{1,9},{9,1},{17,25},{25,17},{2,10},{10... | collective-permute-start | bytes 589832 | tf_op jit(solution)/shard_map/ppermute | solution.py:675
  19.7 17.7 %collective-permute-start.4 = (bf16[192,512]{1,0:T(8,128)(2,1)}, bf16[192,512]{1,0:T(8,128)(2,1)}, u32[]{:S(2)}, u32[]{:S(2)}) collective-permute-start(bf16[192,512]{1,0:T(8,128)(2,1)} %get-tuple-element.255), channel_id=1, source_target_pairs={{0,16},{8,24},{16,0},{24,8},{1,17},{9,25},{17,1},{25,9},{2,18},{10... | collective-permute-start | bytes 589832 | tf_op jit(solution)/shard_map/ppermute | solution.py:675
  24.1 14.4 %collective-permute-start.5 = (bf16[192,512]{1,0:T(8,128)(2,1)}, bf16[192,512]{1,0:T(8,128)(2,1)S(1)}, u32[]{:S(2)}, u32[]{:S(2)}) collective-permute-start(bf16[192,512]{1,0:T(8,128)(2,1)} %get-tuple-element.254), channel_id=1, source_target_pairs={{0,24},{8,16},{16,8},{24,0},{1,25},{9,17},{17,9},{25,1},{2,26},{10... | collective-permute-start | bytes 589832 | tf_op jit(solution)/shard_map/ppermute | solution.py:675
  24.6 24.0 %collective-permute-start = (bf16[192,512]{1,0:T(8,128)(2,1)S(1)}, bf16[192,512]{1,0:T(8,128)(2,1)S(1)}, u32[]{:S(2)}, u32[]{:S(2)}) collective-permute-start(bf16[192,512]{1,0:T(8,128)(2,1)S(1)} %get-tuple-element.253), channel_id=1, source_target_pairs={{0,8},{8,0},{16,24},{24,16},{1,9},{9,1},{17,25},{25,17},{2,10},{10... | collective-permute-start | bytes 589832 | tf_op jit(solution)/shard_map/ppermute | solution.py:675
  26.1 22.5 %collective-permute-start.1 = (bf16[192,512]{1,0:T(8,128)(2,1)S(1)}, bf16[192,512]{1,0:T(8,128)(2,1)S(1)}, u32[]{:S(2)}, u32[]{:S(2)}) collective-permute-start(bf16[192,512]{1,0:T(8,128)(2,1)S(1)} %get-tuple-element.252), channel_id=1, source_target_pairs={{0,16},{8,24},{16,0},{24,8},{1,17},{9,25},{17,1},{25,9},{2,18},{10... | collective-permute-start | bytes 589832 | tf_op jit(solution)/shard_map/ppermute | solution.py:675
  37.4 39.7 %collective-permute-start.12 = (bf16[512,768]{1,0:T(8,128)(2,1)S(1)}, bf16[512,768]{1,0:T(8,128)(2,1)S(1)}, u32[]{:S(2)}, u32[]{:S(2)}) collective-permute-start(bf16[512,768]{1,0:T(8,128)(2,1)S(1)} %first_norm.1.hn_ref), channel_id=1, source_target_pairs={{0,8},{8,0},{16,24},{24,16},{1,9},{9,1},{17,25},{25,17},{2,10},{10... | collective-permute-start | bytes 2359304 | tf_op jit(solution)/shard_map/ppermute | solution.py:675
  38.5 38.6 %collective-permute-start.13 = (bf16[512,768]{1,0:T(8,128)(2,1)S(1)}, bf16[512,768]{1,0:T(8,128)(2,1)S(1)}, u32[]{:S(2)}, u32[]{:S(2)}) collective-permute-start(bf16[512,768]{1,0:T(8,128)(2,1)S(1)} %first_norm.1.hn_ref), channel_id=1, source_target_pairs={{0,16},{8,24},{16,0},{24,8},{1,17},{9,25},{17,1},{25,9},{2,18},{10... | collective-permute-start | bytes 2359304 | tf_op jit(solution)/shard_map/ppermute | solution.py:675
  77.1 14.5 %collective-permute-start.14 = (bf16[256,768]{1,0:T(8,128)(2,1)S(1)}, bf16[256,768]{1,0:T(8,128)(2,1)S(1)}, u32[]{:S(2)}, u32[]{:S(2)}) collective-permute-start(bf16[256,768]{1,0:T(8,128)(2,1)S(1)} %slice.210), channel_id=1, source_target_pairs={{0,8},{8,0},{16,24},{24,16},{1,9},{9,1},{17,25},{25,17},{2,10},{10... | collective-permute-start | bytes 1179656 | tf_op jit(solution)/shard_map/ppermute | solution.py:675
  110.3 19.3 %collective-permute-start.20 = (bf16[4,264,384]{2,1,0:T(8,128)(2,1)S(1)}, bf16[4,264,384]{2,1,0:T(8,128)(2,1)S(1)}, u32[]{:S(2)}, u32[]{:S(2)}) collective-permute-start(bf16[4,264,384]{2,1,0:T(8,128)(2,1)S(1)} %get-tuple-element.163), channel_id=1, source_target_pairs={{0,8},{8,0},{16,24},{24,16},{1,9},{9,1},{17,25},{25,17},{2,10},{10... | collective-permute-start | bytes 2433032 | tf_op jit(solution)/shard_map/ppermute | solution.py:675
  110.6 19.1 %collective-permute-start.21 = (bf16[4,264,384]{2,1,0:T(8,128)(2,1)S(1)}, bf16[4,264,384]{2,1,0:T(8,128)(2,1)S(1)}, u32[]{:S(2)}, u32[]{:S(2)}) collective-permute-start(bf16[4,264,384]{2,1,0:T(8,128)(2,1)S(1)} %get-tuple-element.164), channel_id=1, source_target_pairs={{0,16},{8,24},{16,0},{24,8},{1,17},{9,25},{17,1},{25,9},{2,18},{10... | collective-permute-start | bytes 2433032 | tf_op jit(solution)/shard_map/ppermute | solution.py:675
  129.9 16.0 %collective-permute-start.22 = (bf16[2,264,384]{2,1,0:T(8,128)(2,1)S(1)}, bf16[2,264,384]{2,1,0:T(8,128)(2,1)S(1)}, u32[]{:S(2)}, u32[]{:S(2)}) collective-permute-start(bf16[2,264,384]{2,1,0:T(8,128)(2,1)S(1)} %get-tuple-element.240), channel_id=1, source_target_pairs={{0,16},{8,24},{16,0},{24,8},{1,17},{9,25},{17,1},{25,9},{2,18},{10... | collective-permute-start | bytes 1216520 | tf_op jit(solution)/shard_map/ppermute | solution.py:675
  131.7 14.2 %collective-permute-start.23 = (bf16[2,264,384]{2,1,0:T(8,128)(2,1)S(1)}, bf16[2,264,384]{2,1,0:T(8,128)(2,1)S(1)}, u32[]{:S(2)}, u32[]{:S(2)}) collective-permute-start(bf16[2,264,384]{2,1,0:T(8,128)(2,1)S(1)} %get-tuple-element.239), channel_id=1, source_target_pairs={{0,8},{8,0},{16,24},{24,16},{1,9},{9,1},{17,25},{25,17},{2,10},{10... | collective-permute-start | bytes 1216520 | tf_op jit(solution)/shard_map/ppermute | solution.py:675
  148.1 20.1 %collective-permute-start.26 = (bf16[264,384]{1,0:T(8,128)(2,1)S(1)}, bf16[264,384]{1,0:T(8,128)(2,1)S(1)}, u32[]{:S(2)}, u32[]{:S(2)}) collective-permute-start(bf16[264,384]{1,0:T(8,128)(2,1)S(1)} %get-tuple-element.237), channel_id=1, source_target_pairs={{0,6},{2,4},{4,2},{6,0},{1,7},{3,5},{5,3},{7,1},{8,14},{10,12},{12... | collective-permute-start | bytes 608264 | tf_op jit(solution)/shard_map/ppermute | solution.py:675
  151.2 18.7 %collective-permute-start.25 = (bf16[264,384]{1,0:T(8,128)(2,1)S(1)}, bf16[264,384]{1,0:T(8,128)(2,1)S(1)}, u32[]{:S(2)}, u32[]{:S(2)}) collective-permute-start(bf16[264,384]{1,0:T(8,128)(2,1)S(1)} %get-tuple-element.236), channel_id=1, source_target_pairs={{0,4},{2,6},{4,0},{6,2},{1,5},{3,7},{5,1},{7,3},{8,12},{10,14},{12... | collective-permute-start | bytes 608264 | tf_op jit(solution)/shard_map/ppermute | solution.py:675
  151.2 18.7 %collective-permute-start.24 = (bf16[264,384]{1,0:T(8,128)(2,1)S(1)}, bf16[264,384]{1,0:T(8,128)(2,1)S(1)}, u32[]{:S(2)}, u32[]{:S(2)}) collective-permute-start(bf16[264,384]{1,0:T(8,128)(2,1)S(1)} %get-tuple-element.238), channel_id=1, source_target_pairs={{0,2},{2,0},{4,6},{6,4},{1,3},{3,1},{5,7},{7,5},{8,10},{10,8},{12,... | collective-permute-start | bytes 608264 | tf_op jit(solution)/shard_map/ppermute | solution.py:675
  152.7 17.4 %collective-permute-start.27 = (bf16[2,192,512]{2,1,0:T(8,128)(2,1)S(1)}, bf16[2,192,512]{2,1,0:T(8,128)(2,1)S(1)}, u32[]{:S(2)}, u32[]{:S(2)}) collective-permute-start(bf16[2,192,512]{2,1,0:T(8,128)(2,1)S(1)} %get-tuple-element.242), channel_id=1, source_target_pairs={{0,8},{8,0},{16,24},{24,16},{1,9},{9,1},{17,25},{25,17},{2,10},{10... | collective-permute-start | bytes 1179656 | tf_op jit(solution)/shard_map/ppermute | solution.py:675
  154.3 15.8 %collective-permute-start.28 = (bf16[2,192,512]{2,1,0:T(8,128)(2,1)S(1)}, bf16[2,192,512]{2,1,0:T(8,128)(2,1)S(1)}, u32[]{:S(2)}, u32[]{:S(2)}) collective-permute-start(bf16[2,192,512]{2,1,0:T(8,128)(2,1)S(1)} %get-tuple-element.243), channel_id=1, source_target_pairs={{0,16},{8,24},{16,0},{24,8},{1,17},{9,25},{17,1},{25,9},{2,18},{10... | collective-permute-start | bytes 1179656 | tf_op jit(solution)/shard_map/ppermute | solution.py:675
  171.8 18.0 %collective-permute-start.32 = (bf16[264,384]{1,0:T(8,128)(2,1)S(1)}, bf16[264,384]{1,0:T(8,128)(2,1)S(1)}, u32[]{:S(2)}, u32[]{:S(2)}) collective-permute-start(bf16[264,384]{1,0:T(8,128)(2,1)S(1)} %fusion.2), channel_id=1, source_target_pairs={{0,2},{2,0},{4,6},{6,4},{1,3},{3,1},{5,7},{7,5},{8,10},{10,8},{12,... | collective-permute-start | bytes 608264 | tf_op jit(solution)/shard_map/ppermute | solution.py:675
  172.6 17.2 %collective-permute-start.33 = (bf16[264,384]{1,0:T(8,128)(2,1)S(1)}, bf16[264,384]{1,0:T(8,128)(2,1)S(1)}, u32[]{:S(2)}, u32[]{:S(2)}) collective-permute-start(bf16[264,384]{1,0:T(8,128)(2,1)S(1)} %fusion.2), channel_id=1, source_target_pairs={{0,4},{2,6},{4,0},{6,2},{1,5},{3,7},{5,1},{7,3},{8,12},{10,14},{12... | collective-permute-start | bytes 608264 | tf_op jit(solution)/shard_map/ppermute | solution.py:675
  175.5 14.3 %collective-permute-start.34 = (bf16[264,384]{1,0:T(8,128)(2,1)S(1)}, bf16[264,384]{1,0:T(8,128)(2,1)S(1)}, u32[]{:S(2)}, u32[]{:S(2)}) collective-permute-start(bf16[264,384]{1,0:T(8,128)(2,1)S(1)} %fusion.2), channel_id=1, source_target_pairs={{0,6},{2,4},{4,2},{6,0},{1,7},{3,5},{5,3},{7,1},{8,14},{10,12},{12... | collective-permute-start | bytes 608264 | tf_op jit(solution)/shard_map/ppermute | solution.py:675
  191.5 20.5 %collective-permute-start.36 = (bf16[4,264,384]{2,1,0:T(8,128)(2,1)S(1)}, bf16[4,264,384]{2,1,0:T(8,128)(2,1)S(1)}, u32[]{:S(2)}, u32[]{:S(2)}) collective-permute-start(bf16[4,264,384]{2,1,0:T(8,128)(2,1)S(1)} %get-tuple-element.246), channel_id=1, source_target_pairs={{0,8},{8,0},{16,24},{24,16},{1,9},{9,1},{17,25},{25,17},{2,10},{10... | collective-permute-start | bytes 2433032 | tf_op jit(solution)/shard_map/ppermute | solution.py:675
  191.8 20.3 %collective-permute-start.37 = (bf16[4,264,384]{2,1,0:T(8,128)(2,1)S(1)}, bf16[4,264,384]{2,1,0:T(8,128)(2,1)S(1)}, u32[]{:S(2)}, u32[]{:S(2)}) collective-permute-start(bf16[4,264,384]{2,1,0:T(8,128)(2,1)S(1)} %get-tuple-element.246), channel_id=1, source_target_pairs={{0,16},{8,24},{16,0},{24,8},{1,17},{9,25},{17,1},{25,9},{2,18},{10... | collective-permute-start | bytes 2433032 | tf_op jit(solution)/shard_map/ppermute | solution.py:675
  212.1 14.0 %collective-permute-start.42 = (bf16[2,264,384]{2,1,0:T(8,128)(2,1)S(1)}, bf16[2,264,384]{2,1,0:T(8,128)(2,1)S(1)}, u32[]{:S(2)}, u32[]{:S(2)}) collective-permute-start(bf16[2,264,384]{2,1,0:T(8,128)(2,1)S(1)} %slice.246), channel_id=1, source_target_pairs={{0,8},{8,0},{16,24},{24,16},{1,9},{9,1},{17,25},{25,17},{2,10},{10... | collective-permute-start | bytes 1216520 | tf_op jit(solution)/shard_map/ppermute | solution.py:675
  229.0 20.7 %collective-permute-start.52 = (bf16[4,9,8,768]{3,2,1,0:T(8,128)(2,1)S(1)}, bf16[4,9,8,768]{3,2,1,0:T(8,128)(2,1)S(1)}, u32[]{:S(2)}, u32[]{:S(2)}) collective-permute-start(bf16[4,9,8,768]{3,2,1,0:T(8,128)(2,1)S(1)} %pad_maximum_fusion.4.refs_0_), channel_id=1, source_target_pairs={{0,1},{1,0},{2,3},{3,2},{4,5},{5,4},{6,7},{7,6},{8,9},{9,8},{10,11... | collective-permute-start | bytes 1327112 | tf_op jit(solution)/shard_map/ppermute | solution.py:675
  (58 other events, 949.0 us)

commit v3 on v2

--- a/solution.py
+++ b/solution.py
@@ -750,7 +750,7 @@
     send_two = add(keep[at[0] : at[1]], taken[at[0] : at[1]])
     early = add(keep[at[1] :], taken[at[1] :])
     a_own, a_two, b_own, b_one = (early[i * half : (i + 1) * half] for i in range(4))
-    send_one, send_two, early, upstream = tie(send_one, send_two, early, upstream)
+    send_one, send_two, early, upstream[1] = tie(send_one, send_two, early, upstream[1])
 
     def backward(j, upstream):
         return attend_backward(
@@ -771,14 +771,13 @@
     early = [add(a_own[i], from_one[i], by_two[i]) for i in range(half)]
     early += [add(b_own[i], from_two[i], by_one[i]) for i in range(half)]
     early = scatter_near(early)
-    upstream, kept, given = tie(upstream, kept, given)
     grads.append(backward(2, upstream))
 
     grads, early, pair[1], pair[2] = tie(grads, early, pair[1], pair[2])
     early = sum_far(early)
     slots = [early] + [swap(early, "near", k) for k in range(1, near)]
     last = [grads[2][0]] + [swap(grads[2][k], "seq", k) for k in range(1, parts)]
-    last, slots, grads[2], pair = tie(last, slots, grads[2], pair)
+    last, slots, grads[2], pair, kept, given = tie(last, slots, grads[2], pair, kept, given)
     early = jnp.stack(slots)
     one, two = swap(early, "seq", 1), swap(early, "seq", 2)
     kept_last, given_last = late_grads(me, grads[2:], hn_row, near)

time: 265 us -> 261 us (0.985)
  waiting for transfers between devices: 60.3 us -> 56.7 us
    ppermute x57, waiting for transfers between devices: 60.3 us -> 56.7 us  [swap(): return lax.ppermute(values, axis, [(i, i ^ k) for i in range(size)])]
  transfers between devices with their start and end apart: 57 -> 57, of which waited for: 21 -> 21; matrix products, arithmetic and copies ran while one was open for 2% -> 2% of each run, Pallas kernels for 39% -> 40%
where the time goes in v3:
time: 261 us; the launch traced here: 259 us
  Pallas kernels  123 us (47%)
  starting transfers between devices  62 us (24%)
  waiting for transfers between devices  56.7 us (22%)
  local copies, waits for them, and re-layouts  8.23 us (3%)
  other arithmetic  7.29 us (3%)
    ppermute x57, starting transfers between devices, swap(): return lax.ppermute(values, axis, [(i, i ^ k) for i in range(size)])  62 us
    ppermute x57, waiting for transfers between devices, swap(): return lax.ppermute(values, axis, [(i, i ^ k) for i in range(size)])  56.7 us
    pallas_call x3, Pallas kernels, attend_backward(): pl.pallas_call(functools.partial(backward_kernel, bq, parts, turn), grid_...  39.6 us
    pallas_call x3, Pallas kernels, attend_forward(): pl.pallas_call(functools.partial(forward_kernel, bq, parts), grid_spec=pl...  35.7 us
    pallas_call x1, Pallas kernels, middle_part(): pl.pallas_call(functools.partial(middle_kernel, parts), in_specs=[pl.Bloc...  11.8 us
    pallas_call x1, Pallas kernels, assemble_late(): pl.pallas_call(late_kernel, grid_spec=pltpu.PrefetchScalarGridSpec(num_sc...  8.9 us
    pallas_call x1, Pallas kernels, assemble_early(): pl.pallas_call(early_kernel, grid_spec=pltpu.PrefetchScalarGridSpec(num_s...  6.43 us
    pallas_call x3, Pallas kernels, project(): pl.pallas_call(project_kernel, grid_spec=pltpu.PrefetchScalarGridSpec(num...  6.17 us
  transfers between devices with their start and end apart: 57, of which 21 were waited for; matrix products, arithmetic and copies ran while one was open for 2% of the time, Pallas kernels for 40%

profile of v3, /device:TPU:0, one launch (start us, length us, event | category | flops | bytes accessed | tf_op | source)
XLA Modules:
  0.0 258.5 jit_solution(14797452633383194005)
XLA Ops:
  10.4 2.9 %collective-permute-start.6 = (bf16[192,512]{1,0:T(8,128)(2,1)}, bf16[192,512]{1,0:T(8,128)(2,1)}, u32[]{:S(2)}, u32[]{:S(2)}) collective-permute-start(bf16[192,512]{1,0:T(8,128)(2,1)} %get-tuple-element.245), channel_id=1, source_target_pairs={{0,8},{8,0},{16,24},{24,16},{1,9},{9,1},{17,25},{25,17},{2,10},{10... | collective-permute-start | bytes 589832 | tf_op jit(solution)/shard_map/ppermute | solution.py:675
  27.7 8.7 %attend_forward.5 = (bf16[4,64,512]{2,1,0:T(8,128)(2,1)S(1)}, f32[1,2048]{1,0:T(1,128)S(1)}) custom-call(s32[3]{0:T(128)S(1)} %pad_add_fusion.me_ref, bf16[4,192,512]{2,1,0:T(8,128)(2,1)S(1)} %project.5.refs_0_, bf16[192,512]{1,0:T(8,128)(2,1)} %collective-permute-done.6.refs_1_, bf16[192,512]{1,0:T(8,128)(2,1)} %collective-permute-done.7.refs_2_, ...), custom_call_target="tpu_custom_call" | custom-call | flops 4294967296 | bytes 4194304 | tf_op jit(solution)/shard_map/attend_forward/pallas_call | solution.py:185
  40.0 8.6 %attend_forward.4 = (bf16[4,64,512]{2,1,0:T(8,128)(2,1)S(1)}, f32[1,2048]{1,0:T(1,128)S(1)}) custom-call(s32[3]{0:T(128)S(1)} %pad_add_fusion.me_ref, bf16[4,192,512]{2,1,0:T(8,128)(2,1)S(1)} %project.4.refs_0_, bf16[192,512]{1,0:T(8,128)(2,1)} %collective-permute-done.3.refs_1_, bf16[192,512]{1,0:T(8,128)(2,1)} %collective-permute-done.4.refs_2_, ...), custom_call_target="tpu_custom_call" | custom-call | flops 4294967296 | bytes 4194304 | tf_op jit(solution)/shard_map/attend_forward/pallas_call | solution.py:185
  48.7 18.4 %attend_forward.3 = (bf16[4,64,512]{2,1,0:T(8,128)(2,1)S(1)}, f32[1,2048]{1,0:T(1,128)S(1)}) custom-call(s32[3]{0:T(128)S(1)} %pad_add_fusion.me_ref, bf16[4,192,512]{2,1,0:T(8,128)(2,1)S(1)} %project.3.refs_0_, bf16[192,512]{1,0:T(8,128)(2,1)S(1)} %collective-permute-done.refs_1_, bf16[192,512]{1,0:T(8,128)(2,1)S(1)} %collective-permute-done.1.refs_2_, ...), custom_call_target="tpu_custom_call" | custom-call | flops 4294967296 | bytes 4194304 | tf_op jit(solution)/shard_map/attend_forward/pallas_call | solution.py:185
  72.9 4.2 %collective-permute-done.10.refs_2_ = bf16[3,64,512]{2,1,0:T(8,128)(2,1)S(1)} collective-permute-done((bf16[3,64,512]{2,1,0:T(8,128)(2,1)S(1)}, bf16[3,64,512]{2,1,0:T(8,128)(2,1)S(1)}, u32[]{:S(2)}, u32[]{:S(2)}) %collective-permute-start.10) | collective-permute-done | bytes 196640 | tf_op jit(solution)/shard_map/ppermute | solution.py:675
  79.8 11.8 %middle_part.1 = (bf16[768,512]{1,0:T(8,128)(2,1)S(1)}, bf16[512,768]{1,0:T(8,128)(2,1)S(1)}, bf16[512,2304]{1,0:T(8,128)(2,1)S(1)}, bf16[512,1152]{1,0:T(8,128)...) custom-call(s32[3]{0:T(128)S(1)} %pad_add_fusion.me_ref, ...), custom_call_target="tpu_custom_call" | custom-call | flops 7549747200 | bytes 20971520 | tf_op jit(solution)/shard_map/middle_part/pallas_call | solution.py:388
  91.6 5.3 %early_grads.1 = (bf16[16,264,384]{2,1,0:T(8,128)(2,1)S(1)}, bf16[16,264,384]{2,1,0:T(8,128)(2,1)S(1)}) custom-call(s32[17]{0:T(128)S(1)} %pad_add_fusion.1.at_ref, bf16[512,768]{1,0:T(8,128)(2,1)S(1)} %get-tuple-element.141.n2_ref, bf16[512,2304]{1,0:T(8,128)(2,1)S(1)} %get-tuple-element.142.gu_ref, bf16[512,1152]{1,0:T(8,128)(2,1)S(1)} %get-tuple-element.143.inner_ref, ...), custom_call_target="tpu_custom_call" | custom-call | flops 3321888768 | bytes 14680064 | tf_op jit(solution)/shard_map/early_grads/pallas_call | solution.py:443
  106.9 4.2 %collective-permute-done.18.refs_6_ = bf16[3,64,512]{2,1,0:T(8,128)(2,1)S(1)} collective-permute-done((bf16[3,64,512]{2,1,0:T(8,128)(2,1)S(1)}, bf16[3,64,512]{2,1,0:T(8,128)(2,1)S(1)}, u32[]{:S(2)}, u32[]{:S(2)}) %collective-permute-start.18) | collective-permute-done | bytes 196640 | tf_op jit(solution)/shard_map/ppermute | solution.py:675
  111.1 12.3 %attend_backward.3.refs_0_ = bf16[4,192,512]{2,1,0:T(8,128)(2,1)S(1)} custom-call(s32[3]{0:T(128)S(1)} %pad_add_fusion.me_ref, bf16[4,192,512]{2,1,0:T(8,128)(2,1)S(1)} %project.3.refs_0_, bf16[192,512]{1,0:T(8,128)(2,1)S(1)} %collective-permute-done.refs_1_, bf16[192,512]{1,0:T(8,128)(2,1)S(1)} %collective-permute-done.1.refs_2_, ...), custom_call_target="tpu_custom_call" | custom-call | flops 10737418240 | bytes 6291456 | tf_op jit(solution)/shard_map/attend_backward/pallas_call | solution.py:291
  129.7 13.7 %attend_backward.4.refs_1_ = bf16[4,192,512]{2,1,0:T(8,128)(2,1)S(1)} custom-call(s32[3]{0:T(128)S(1)} %pad_add_fusion.me_ref, bf16[4,192,512]{2,1,0:T(8,128)(2,1)S(1)} %project.4.refs_0_, bf16[192,512]{1,0:T(8,128)(2,1)} %collective-permute-done.3.refs_1_, bf16[192,512]{1,0:T(8,128)(2,1)} %collective-permute-done.4.refs_2_, ...), custom_call_target="tpu_custom_call" | custom-call | flops 10737418240 | bytes 6291456 | tf_op jit(solution)/shard_map/attend_backward/pallas_call | solution.py:291
  143.7 3.2 %collective-permute-start.26 = (bf16[264,384]{1,0:T(8,128)(2,1)S(1)}, bf16[264,384]{1,0:T(8,128)(2,1)S(1)}, u32[]{:S(2)}, u32[]{:S(2)}) collective-permute-start(bf16[264,384]{1,0:T(8,128)(2,1)S(1)} %get-tuple-element.223), channel_id=1, source_target_pairs={{0,6},{2,4},{4,2},{6,0},{1,7},{3,5},{5,3},{7,1},{8,14},{10,12},{12... | collective-permute-start | bytes 608264 | tf_op jit(solution)/shard_map/ppermute | solution.py:675
  150.7 13.6 %attend_backward.5.refs_0_ = bf16[4,192,512]{2,1,0:T(8,128)(2,1)S(1)} custom-call(s32[3]{0:T(128)S(1)} %pad_add_fusion.me_ref, bf16[4,192,512]{2,1,0:T(8,128)(2,1)S(1)} %project.5.refs_0_, bf16[192,512]{1,0:T(8,128)(2,1)} %collective-permute-done.6.refs_1_, bf16[192,512]{1,0:T(8,128)(2,1)} %collective-permute-done.7.refs_2_, ...), custom_call_target="tpu_custom_call" | custom-call | flops 10737418240 | bytes 6291456 | tf_op jit(solution)/shard_map/attend_backward/pallas_call | solution.py:291
  167.3 3.0 %collective-permute-start.33 = (bf16[264,384]{1,0:T(8,128)(2,1)S(1)}, bf16[264,384]{1,0:T(8,128)(2,1)S(1)}, u32[]{:S(2)}, u32[]{:S(2)}) collective-permute-start(bf16[264,384]{1,0:T(8,128)(2,1)S(1)} %fusion.2), channel_id=1, source_target_pairs={{0,4},{2,6},{4,0},{6,2},{1,5},{3,7},{5,1},{7,3},{8,12},{10,14},{12... | collective-permute-start | bytes 608264 | tf_op jit(solution)/shard_map/ppermute | solution.py:675
  171.0 4.9 %collective-permute-done.35.refs_3_ = bf16[2,192,512]{2,1,0:T(8,128)(2,1)S(1)} collective-permute-done((bf16[2,192,512]{2,1,0:T(8,128)(2,1)S(1)}, bf16[2,192,512]{2,1,0:T(8,128)(2,1)S(1)}, u32[]{:S(2)}, u32[]{:S(2)}) %collective-permute-start.35) | collective-permute-done | bytes 393248 | tf_op jit(solution)/shard_map/ppermute | solution.py:675
  188.5 3.2 %collective-permute-start.41 = (bf16[9,8,768]{2,1,0:T(8,128)(2,1)S(1)}, bf16[9,8,768]{2,1,0:T(8,128)(2,1)S(1)}, u32[]{:S(2)}, u32[]{:S(2)}) collective-permute-start(bf16[9,8,768]{2,1,0:T(8,128)(2,1)S(1)} %get-tuple-element.247), channel_id=1, source_target_pairs={{0,6},{2,4},{4,2},{6,0},{1,7},{3,5},{5,3},{7,1},{8,14},{10,12},{12... | collective-permute-start | bytes 331784 | tf_op jit(solution)/shard_map/ppermute | solution.py:675
  193.0 4.8 %input_grad.1 = f32[512,768]{1,0:T(8,128)} custom-call(s32[3]{0:T(128)S(1)} %pad_add_fusion.me_ref, bf16[2,192,512]{2,1,0:T(8,128)(2,1)S(1)} %get-tuple-element.189.refs_0_, bf16[2,192,512]{2,1,0:T(8,128)(2,1)S(1)} %collective-permute-done.27.refs_1_, bf16[2,192,512]{2,1,0:T(8,128)(2,1)S(1)} %collective-permute-done.28.refs_2_, ...), custom_call_target="tpu_custom_call" | custom-call | flops 1811939328 | bytes 10485760 | tf_op jit(solution)/shard_map/input_grad/pallas_call | solution.py:661
  197.8 3.7 %collective-permute-done.40 = bf16[9,8,768]{2,1,0:T(8,128)(2,1)S(1)} collective-permute-done((bf16[9,8,768]{2,1,0:T(8,128)(2,1)S(1)}, bf16[9,8,768]{2,1,0:T(8,128)(2,1)S(1)}, u32[]{:S(2)}, u32[]{:S(2)}) %collective-permute-start.40) | collective-permute-done | bytes 110624 | tf_op jit(solution)/shard_map/ppermute | solution.py:675
  201.6 4.9 %collective-permute-done.36 = bf16[4,264,384]{2,1,0:T(8,128)(2,1)S(1)} collective-permute-done((bf16[4,264,384]{2,1,0:T(8,128)(2,1)S(1)}, bf16[4,264,384]{2,1,0:T(8,128)(2,1)S(1)}, u32[]{:S(2)}, u32[]{:S(2)}) %collective-permute-start.36) | collective-permute-done | bytes 811040 | tf_op jit(solution)/shard_map/ppermute | solution.py:675
  209.3 3.1 %collective-permute-start.46 = (bf16[9,8,768]{2,1,0:T(8,128)(2,1)S(1)}, bf16[9,8,768]{2,1,0:T(8,128)(2,1)S(1)}, u32[]{:S(2)}, u32[]{:S(2)}) collective-permute-start(bf16[9,8,768]{2,1,0:T(8,128)(2,1)S(1)} %fusion.12), channel_id=1, source_target_pairs={{0,6},{2,4},{4,2},{6,0},{1,7},{3,5},{5,3},{7,1},{8,14},{10,12},{12... | collective-permute-start | bytes 331784 | tf_op jit(solution)/shard_map/ppermute | solution.py:675
  213.7 3.5 %collective-permute-done.46 = bf16[9,8,768]{2,1,0:T(8,128)(2,1)S(1)} collective-permute-done((bf16[9,8,768]{2,1,0:T(8,128)(2,1)S(1)}, bf16[9,8,768]{2,1,0:T(8,128)(2,1)S(1)}, u32[]{:S(2)}, u32[]{:S(2)}) %collective-permute-start.46) | collective-permute-done | bytes 110624 | tf_op jit(solution)/shard_map/ppermute | solution.py:675
  217.2 4.7 %collective-permute-done.45 = bf16[9,8,768]{2,1,0:T(8,128)(2,1)S(1)} collective-permute-done((bf16[9,8,768]{2,1,0:T(8,128)(2,1)S(1)}, bf16[9,8,768]{2,1,0:T(8,128)(2,1)S(1)}, u32[]{:S(2)}, u32[]{:S(2)}) %collective-permute-start.45) | collective-permute-done | bytes 110624 | tf_op jit(solution)/shard_map/ppermute | solution.py:675
  225.2 10.1 %collective-permute-done.47.refs_1_ = bf16[4,9,8,768]{3,2,1,0:T(8,128)(2,1)S(1)} collective-permute-done((bf16[4,9,8,768]{3,2,1,0:T(8,128)(2,1)S(1)}, bf16[4,9,8,768]{3,2,1,0:T(8,128)(2,1)S(1)}, u32[]{:S(2)}, u32[]{:S(2)}) %collective-permute-start.47) | collective-permute-done | bytes 442400 | tf_op jit(solution)/shard_map/ppermute | solution.py:675
  238.6 6.4 %assemble_early.1 = (f32[768,2304]{1,0:T(8,128)}, f32[1152,768]{1,0:T(8,128)}, f32[768,768]{1,0:T(8,128)}, f32[1,768]{1,0:T(1,128)S(1)}) custom-call(s32[3]{0:T(128)S(1)} %pad_add_fusion.me_ref, bf16[4,4,264,384]{3,2,1,0:T(8,128)(2,1)S(1)} %pad_maximum_fusion.mine_ref, bf16[4,4,264,384]{3,2,1,0:T(8,128)(2,1)S(1)} %collective-permute-done.49.other_ref, ...), custom_call_target="tpu_custom_call" | custom-call | flops 1048576 | bytes 25165824 | tf_op jit(solution)/shard_map/assemble_early/pallas_call | solution.py:544
  248.1 8.9 %assemble_late.1 = (f32[768,2304]{1,0:T(8,128)}, f32[1,768]{1,0:T(1,128)}) custom-call(s32[3]{0:T(128)} %copy-done.8, bf16[4,9,8,768]{3,2,1,0:T(8,128)(2,1)} %copy-done.14, bf16[4,9,8,768]{3,2,1,0:T(8,128)(2,1)} %copy-done.15, bf16[4,9,8,768]{3,2,1,0:T(8,128)(2,1)} %copy-done.16, bf16[2,9,8,768]{3,2,1,0:T(8,128)(2,1)} %copy-done.22, ...), custom_call_target="tpu_custom_call" | custom-call | flops 1048576 | bytes 14680064 | tf_op jit(solution)/shard_map/assemble_late/pallas_call | solution.py:604
  (207 shorter events, 88.7 us)
Async XLA Ops:
  17.8 18.6 %collective-permute-start.3 = (bf16[192,512]{1,0:T(8,128)(2,1)}, bf16[192,512]{1,0:T(8,128)(2,1)}, u32[]{:S(2)}, u32[]{:S(2)}) collective-permute-start(bf16[192,512]{1,0:T(8,128)(2,1)} %get-tuple-element.242), channel_id=1, source_target_pairs={{0,8},{8,0},{16,24},{24,16},{1,9},{9,1},{17,25},{25,17},{2,10},{10... | collective-permute-start | bytes 589832 | tf_op jit(solution)/shard_map/ppermute | solution.py:675
  19.7 17.7 %collective-permute-start.4 = (bf16[192,512]{1,0:T(8,128)(2,1)}, bf16[192,512]{1,0:T(8,128)(2,1)}, u32[]{:S(2)}, u32[]{:S(2)}) collective-permute-start(bf16[192,512]{1,0:T(8,128)(2,1)} %get-tuple-element.241), channel_id=1, source_target_pairs={{0,16},{8,24},{16,0},{24,8},{1,17},{9,25},{17,1},{25,9},{2,18},{10... | collective-permute-start | bytes 589832 | tf_op jit(solution)/shard_map/ppermute | solution.py:675
  24.1 14.3 %collective-permute-start.5 = (bf16[192,512]{1,0:T(8,128)(2,1)}, bf16[192,512]{1,0:T(8,128)(2,1)S(1)}, u32[]{:S(2)}, u32[]{:S(2)}) collective-permute-start(bf16[192,512]{1,0:T(8,128)(2,1)} %get-tuple-element.240), channel_id=1, source_target_pairs={{0,24},{8,16},{16,8},{24,0},{1,25},{9,17},{17,9},{25,1},{2,26},{10... | collective-permute-start | bytes 589832 | tf_op jit(solution)/shard_map/ppermute | solution.py:675
  24.6 24.0 %collective-permute-start = (bf16[192,512]{1,0:T(8,128)(2,1)S(1)}, bf16[192,512]{1,0:T(8,128)(2,1)S(1)}, u32[]{:S(2)}, u32[]{:S(2)}) collective-permute-start(bf16[192,512]{1,0:T(8,128)(2,1)S(1)} %get-tuple-element.239), channel_id=1, source_target_pairs={{0,8},{8,0},{16,24},{24,16},{1,9},{9,1},{17,25},{25,17},{2,10},{10... | collective-permute-start | bytes 589832 | tf_op jit(solution)/shard_map/ppermute | solution.py:675
  26.1 22.5 %collective-permute-start.1 = (bf16[192,512]{1,0:T(8,128)(2,1)S(1)}, bf16[192,512]{1,0:T(8,128)(2,1)S(1)}, u32[]{:S(2)}, u32[]{:S(2)}) collective-permute-start(bf16[192,512]{1,0:T(8,128)(2,1)S(1)} %get-tuple-element.238), channel_id=1, source_target_pairs={{0,16},{8,24},{16,0},{24,8},{1,17},{9,25},{17,1},{25,9},{2,18},{10... | collective-permute-start | bytes 589832 | tf_op jit(solution)/shard_map/ppermute | solution.py:675
  37.4 39.7 %collective-permute-start.12 = (bf16[512,768]{1,0:T(8,128)(2,1)S(1)}, bf16[512,768]{1,0:T(8,128)(2,1)S(1)}, u32[]{:S(2)}, u32[]{:S(2)}) collective-permute-start(bf16[512,768]{1,0:T(8,128)(2,1)S(1)} %first_norm.1.hn_ref), channel_id=1, source_target_pairs={{0,8},{8,0},{16,24},{24,16},{1,9},{9,1},{17,25},{25,17},{2,10},{10... | collective-permute-start | bytes 2359304 | tf_op jit(solution)/shard_map/ppermute | solution.py:675
  38.5 38.7 %collective-permute-start.13 = (bf16[512,768]{1,0:T(8,128)(2,1)S(1)}, bf16[512,768]{1,0:T(8,128)(2,1)S(1)}, u32[]{:S(2)}, u32[]{:S(2)}) collective-permute-start(bf16[512,768]{1,0:T(8,128)(2,1)S(1)} %first_norm.1.hn_ref), channel_id=1, source_target_pairs={{0,16},{8,24},{16,0},{24,8},{1,17},{9,25},{17,1},{25,9},{2,18},{10... | collective-permute-start | bytes 2359304 | tf_op jit(solution)/shard_map/ppermute | solution.py:675
  77.2 14.5 %collective-permute-start.14 = (bf16[256,768]{1,0:T(8,128)(2,1)S(1)}, bf16[256,768]{1,0:T(8,128)(2,1)S(1)}, u32[]{:S(2)}, u32[]{:S(2)}) collective-permute-start(bf16[256,768]{1,0:T(8,128)(2,1)S(1)} %slice.210), channel_id=1, source_target_pairs={{0,8},{8,0},{16,24},{24,16},{1,9},{9,1},{17,25},{25,17},{2,10},{10... | collective-permute-start | bytes 1179656 | tf_op jit(solution)/shard_map/ppermute | solution.py:675
  104.9 21.4 %collective-permute-start.20 = (bf16[4,264,384]{2,1,0:T(8,128)(2,1)S(1)}, bf16[4,264,384]{2,1,0:T(8,128)(2,1)S(1)}, u32[]{:S(2)}, u32[]{:S(2)}) collective-permute-start(bf16[4,264,384]{2,1,0:T(8,128)(2,1)S(1)} %get-tuple-element.153), channel_id=1, source_target_pairs={{0,8},{8,0},{16,24},{24,16},{1,9},{9,1},{17,25},{25,17},{2,10},{10... | collective-permute-start | bytes 2433032 | tf_op jit(solution)/shard_map/ppermute | solution.py:675
  106.8 20.9 %collective-permute-start.21 = (bf16[4,264,384]{2,1,0:T(8,128)(2,1)S(1)}, bf16[4,264,384]{2,1,0:T(8,128)(2,1)S(1)}, u32[]{:S(2)}, u32[]{:S(2)}) collective-permute-start(bf16[4,264,384]{2,1,0:T(8,128)(2,1)S(1)} %get-tuple-element.154), channel_id=1, source_target_pairs={{0,16},{8,24},{16,0},{24,8},{1,17},{9,25},{17,1},{25,9},{2,18},{10... | collective-permute-start | bytes 2433032 | tf_op jit(solution)/shard_map/ppermute | solution.py:675
  127.9 15.5 %collective-permute-start.22 = (bf16[2,264,384]{2,1,0:T(8,128)(2,1)S(1)}, bf16[2,264,384]{2,1,0:T(8,128)(2,1)S(1)}, u32[]{:S(2)}, u32[]{:S(2)}) collective-permute-start(bf16[2,264,384]{2,1,0:T(8,128)(2,1)S(1)} %get-tuple-element.226), channel_id=1, source_target_pairs={{0,16},{8,24},{16,0},{24,8},{1,17},{9,25},{17,1},{25,9},{2,18},{10... | collective-permute-start | bytes 1216520 | tf_op jit(solution)/shard_map/ppermute | solution.py:675
  128.3 15.2 %collective-permute-start.23 = (bf16[2,264,384]{2,1,0:T(8,128)(2,1)S(1)}, bf16[2,264,384]{2,1,0:T(8,128)(2,1)S(1)}, u32[]{:S(2)}, u32[]{:S(2)}) collective-permute-start(bf16[2,264,384]{2,1,0:T(8,128)(2,1)S(1)} %get-tuple-element.225), channel_id=1, source_target_pairs={{0,8},{8,0},{16,24},{24,16},{1,9},{9,1},{17,25},{25,17},{2,10},{10... | collective-permute-start | bytes 1216520 | tf_op jit(solution)/shard_map/ppermute | solution.py:675
  143.7 20.6 %collective-permute-start.26 = (bf16[264,384]{1,0:T(8,128)(2,1)S(1)}, bf16[264,384]{1,0:T(8,128)(2,1)S(1)}, u32[]{:S(2)}, u32[]{:S(2)}) collective-permute-start(bf16[264,384]{1,0:T(8,128)(2,1)S(1)} %get-tuple-element.223), channel_id=1, source_target_pairs={{0,6},{2,4},{4,2},{6,0},{1,7},{3,5},{5,3},{7,1},{8,14},{10,12},{12... | collective-permute-start | bytes 608264 | tf_op jit(solution)/shard_map/ppermute | solution.py:675
  146.9 18.7 %collective-permute-start.25 = (bf16[264,384]{1,0:T(8,128)(2,1)S(1)}, bf16[264,384]{1,0:T(8,128)(2,1)S(1)}, u32[]{:S(2)}, u32[]{:S(2)}) collective-permute-start(bf16[264,384]{1,0:T(8,128)(2,1)S(1)} %get-tuple-element.222), channel_id=1, source_target_pairs={{0,4},{2,6},{4,0},{6,2},{1,5},{3,7},{5,1},{7,3},{8,12},{10,14},{12... | collective-permute-start | bytes 608264 | tf_op jit(solution)/shard_map/ppermute | solution.py:675
  146.9 18.7 %collective-permute-start.24 = (bf16[264,384]{1,0:T(8,128)(2,1)S(1)}, bf16[264,384]{1,0:T(8,128)(2,1)S(1)}, u32[]{:S(2)}, u32[]{:S(2)}) collective-permute-start(bf16[264,384]{1,0:T(8,128)(2,1)S(1)} %get-tuple-element.224), channel_id=1, source_target_pairs={{0,2},{2,0},{4,6},{6,4},{1,3},{3,1},{5,7},{7,5},{8,10},{10,8},{12,... | collective-permute-start | bytes 608264 | tf_op jit(solution)/shard_map/ppermute | solution.py:675
  148.3 17.4 %collective-permute-start.27 = (bf16[2,192,512]{2,1,0:T(8,128)(2,1)S(1)}, bf16[2,192,512]{2,1,0:T(8,128)(2,1)S(1)}, u32[]{:S(2)}, u32[]{:S(2)}) collective-permute-start(bf16[2,192,512]{2,1,0:T(8,128)(2,1)S(1)} %get-tuple-element.228), channel_id=1, source_target_pairs={{0,8},{8,0},{16,24},{24,16},{1,9},{9,1},{17,25},{25,17},{2,10},{10... | collective-permute-start | bytes 1179656 | tf_op jit(solution)/shard_map/ppermute | solution.py:675
  148.9 16.8 %collective-permute-start.28 = (bf16[2,192,512]{2,1,0:T(8,128)(2,1)S(1)}, bf16[2,192,512]{2,1,0:T(8,128)(2,1)S(1)}, u32[]{:S(2)}, u32[]{:S(2)}) collective-permute-start(bf16[2,192,512]{2,1,0:T(8,128)(2,1)S(1)} %get-tuple-element.229), channel_id=1, source_target_pairs={{0,16},{8,24},{16,0},{24,8},{1,17},{9,25},{17,1},{25,9},{2,18},{10... | collective-permute-start | bytes 1179656 | tf_op jit(solution)/shard_map/ppermute | solution.py:675
  166.5 17.8 %collective-permute-start.32 = (bf16[264,384]{1,0:T(8,128)(2,1)S(1)}, bf16[264,384]{1,0:T(8,128)(2,1)S(1)}, u32[]{:S(2)}, u32[]{:S(2)}) collective-permute-start(bf16[264,384]{1,0:T(8,128)(2,1)S(1)} %fusion.2), channel_id=1, source_target_pairs={{0,2},{2,0},{4,6},{6,4},{1,3},{3,1},{5,7},{7,5},{8,10},{10,8},{12,... | collective-permute-start | bytes 608264 | tf_op jit(solution)/shard_map/ppermute | solution.py:675
  167.3 17.0 %collective-permute-start.33 = (bf16[264,384]{1,0:T(8,128)(2,1)S(1)}, bf16[264,384]{1,0:T(8,128)(2,1)S(1)}, u32[]{:S(2)}, u32[]{:S(2)}) collective-permute-start(bf16[264,384]{1,0:T(8,128)(2,1)S(1)} %fusion.2), channel_id=1, source_target_pairs={{0,4},{2,6},{4,0},{6,2},{1,5},{3,7},{5,1},{7,3},{8,12},{10,14},{12... | collective-permute-start | bytes 608264 | tf_op jit(solution)/shard_map/ppermute | solution.py:675
  170.2 14.1 %collective-permute-start.34 = (bf16[264,384]{1,0:T(8,128)(2,1)S(1)}, bf16[264,384]{1,0:T(8,128)(2,1)S(1)}, u32[]{:S(2)}, u32[]{:S(2)}) collective-permute-start(bf16[264,384]{1,0:T(8,128)(2,1)S(1)} %fusion.2), channel_id=1, source_target_pairs={{0,6},{2,4},{4,2},{6,0},{1,7},{3,5},{5,3},{7,1},{8,14},{10,12},{12... | collective-permute-start | bytes 608264 | tf_op jit(solution)/shard_map/ppermute | solution.py:675
  186.0 20.5 %collective-permute-start.36 = (bf16[4,264,384]{2,1,0:T(8,128)(2,1)S(1)}, bf16[4,264,384]{2,1,0:T(8,128)(2,1)S(1)}, u32[]{:S(2)}, u32[]{:S(2)}) collective-permute-start(bf16[4,264,384]{2,1,0:T(8,128)(2,1)S(1)} %get-tuple-element.232), channel_id=1, source_target_pairs={{0,8},{8,0},{16,24},{24,16},{1,9},{9,1},{17,25},{25,17},{2,10},{10... | collective-permute-start | bytes 2433032 | tf_op jit(solution)/shard_map/ppermute | solution.py:675
  187.8 20.2 %collective-permute-start.37 = (bf16[4,264,384]{2,1,0:T(8,128)(2,1)S(1)}, bf16[4,264,384]{2,1,0:T(8,128)(2,1)S(1)}, u32[]{:S(2)}, u32[]{:S(2)}) collective-permute-start(bf16[4,264,384]{2,1,0:T(8,128)(2,1)S(1)} %get-tuple-element.232), channel_id=1, source_target_pairs={{0,16},{8,24},{16,0},{24,8},{1,17},{9,25},{17,1},{25,9},{2,18},{10... | collective-permute-start | bytes 2433032 | tf_op jit(solution)/shard_map/ppermute | solution.py:675
  208.0 13.9 %collective-permute-start.42 = (bf16[2,264,384]{2,1,0:T(8,128)(2,1)S(1)}, bf16[2,264,384]{2,1,0:T(8,128)(2,1)S(1)}, u32[]{:S(2)}, u32[]{:S(2)}) collective-permute-start(bf16[2,264,384]{2,1,0:T(8,128)(2,1)S(1)} %slice.246), channel_id=1, source_target_pairs={{0,8},{8,0},{16,24},{24,16},{1,9},{9,1},{17,25},{25,17},{2,10},{10... | collective-permute-start | bytes 1216520 | tf_op jit(solution)/shard_map/ppermute | solution.py:675
  225.2 19.9 %collective-permute-start.52 = (bf16[4,9,8,768]{3,2,1,0:T(8,128)(2,1)S(1)}, bf16[4,9,8,768]{3,2,1,0:T(8,128)(2,1)S(1)}, u32[]{:S(2)}, u32[]{:S(2)}) collective-permute-start(bf16[4,9,8,768]{3,2,1,0:T(8,128)(2,1)S(1)} %pad_maximum_fusion.4.refs_0_), channel_id=1, source_target_pairs={{0,1},{1,0},{2,3},{3,2},{4,5},{5,4},{6,7},{7,6},{8,9},{9,8},{10,11... | collective-permute-start | bytes 1327112 | tf_op jit(solution)/shard_map/ppermute | solution.py:675
  (60 other events, 949.0 us)

commit v4 on v3

--- a/solution.py
+++ b/solution.py
@@ -574,7 +574,7 @@
 
 def late_kernel(me_ref, *refs):
     mine, other = refs[:5], refs[5:10]
-    w_ref, norm_ref, out_ref, gain_ref, rows_s = refs[10:]
+    w_ref, norm_ref, out_ref, gain_ref, rows_s, gain_s = refs[10:]
     near = mine[0].shape[0]
     pieces = mine[0].shape[1] // 3
     width = rows_s.shape[1]
@@ -595,7 +595,11 @@
         out_ref[:, cols] = wide
         part = fold_lanes(wide * w_ref[:, cols].astype(F32))
         total = part if total is None else total + part
-    gain_ref[...] = jnp.sum(total.T, axis=0, keepdims=True) / norm_ref[...]
+    gain_s[:, lanes] = jnp.sum(total.T, axis=0, keepdims=True) / norm_ref[...]
+
+    @pl.when(pl.program_id(0) == pl.num_programs(0) - 1)
+    def _():
+        gain_ref[...] = gain_s[0]
 
 
 def assemble_late(me, mine, other, w_qkv, norm_one):
@@ -614,13 +618,16 @@
             ],
             out_specs=[
                 pl.BlockSpec((128, 3 * D), lambda b, me: (b, 0)),
-                pl.BlockSpec((1, 128), lambda b, me: (0, b)),
-            ],
-            scratch_shapes=[pltpu.VMEM((blocks, 3 * D // blocks, 128), F32)],
+                pl.BlockSpec((D,), lambda b, me: (0,)),
+            ],
+            scratch_shapes=[
+                pltpu.VMEM((blocks, 3 * D // blocks, 128), F32),
+                pltpu.VMEM((1, D), F32),
+            ],
         ),
         out_shape=[
             jax.ShapeDtypeStruct((D, 3 * D), F32),
-            jax.ShapeDtypeStruct((1, D), F32),
+            jax.ShapeDtypeStruct((D,), F32),
         ],
         compiler_params=pltpu.CompilerParams(vmem_limit_bytes=60 << 20),
         cost_estimate=cost(1 << 20, 14 << 20),
@@ -807,7 +814,7 @@
     return (
         result[None],
         grad_input[None],
-        sum_norm_one[0],
+        sum_norm_one,
         sum_w_qkv,
         sum_w_out,
         sum_norm_two[0],

time: 261 us -> 260 us (level)
  transfers between devices with their start and end apart: 57 -> 57, of which waited for: 21 -> 21; matrix products, arithmetic and copies ran while one was open for 2% -> 2% of each run, Pallas kernels for 40% -> 41%
where the time goes in v4:
time: 260 us; the launch traced here: 257 us
  Pallas kernels  123 us (47%)
  starting transfers between devices  62 us (24%)
  waiting for transfers between devices  56.7 us (22%)
  local copies, waits for them, and re-layouts  8.23 us (3%)
  other arithmetic  6.02 us (2%)
    ppermute x57, starting transfers between devices, swap(): return lax.ppermute(values, axis, [(i, i ^ k) for i in range(size)])  62 us
    ppermute x57, waiting for transfers between devices, swap(): return lax.ppermute(values, axis, [(i, i ^ k) for i in range(size)])  56.7 us
    pallas_call x3, Pallas kernels, attend_backward(): pl.pallas_call(functools.partial(backward_kernel, bq, parts, turn), grid_...  39.6 us
    pallas_call x3, Pallas kernels, attend_forward(): pl.pallas_call(functools.partial(forward_kernel, bq, parts), grid_spec=pl...  35.8 us
    pallas_call x1, Pallas kernels, middle_part(): pl.pallas_call(functools.partial(middle_kernel, parts), in_specs=[pl.Bloc...  11.8 us
    pallas_call x1, Pallas kernels, assemble_late(): pl.pallas_call(late_kernel, grid_spec=pltpu.PrefetchScalarGridSpec(num_sc...  9.08 us
    pallas_call x1, Pallas kernels, assemble_early(): pl.pallas_call(early_kernel, grid_spec=pltpu.PrefetchScalarGridSpec(num_s...  6.43 us
    pallas_call x3, Pallas kernels, project(): pl.pallas_call(project_kernel, grid_spec=pltpu.PrefetchScalarGridSpec(num...  6.17 us
  transfers between devices with their start and end apart: 57, of which 21 were waited for; matrix products, arithmetic and copies ran while one was open for 2% of the time, Pallas kernels for 41%

profile of v4, /device:TPU:0, one launch (start us, length us, event | category | flops | bytes accessed | tf_op | source)
XLA Modules:
  0.0 257.4 jit_solution(14985274354746726545)
XLA Ops:
  10.4 2.9 %collective-permute-start.6 = (bf16[192,512]{1,0:T(8,128)(2,1)}, bf16[192,512]{1,0:T(8,128)(2,1)}, u32[]{:S(2)}, u32[]{:S(2)}) collective-permute-start(bf16[192,512]{1,0:T(8,128)(2,1)} %get-tuple-element.245), channel_id=1, source_target_pairs={{0,8},{8,0},{16,24},{24,16},{1,9},{9,1},{17,25},{25,17},{2,10},{10... | collective-permute-start | bytes 589832 | tf_op jit(solution)/shard_map/ppermute | solution.py:682
  27.7 8.7 %attend_forward.5 = (bf16[4,64,512]{2,1,0:T(8,128)(2,1)S(1)}, f32[1,2048]{1,0:T(1,128)S(1)}) custom-call(s32[3]{0:T(128)S(1)} %pad_add_fusion.me_ref, bf16[4,192,512]{2,1,0:T(8,128)(2,1)S(1)} %project.5.refs_0_, bf16[192,512]{1,0:T(8,128)(2,1)} %collective-permute-done.6.refs_1_, bf16[192,512]{1,0:T(8,128)(2,1)} %collective-permute-done.7.refs_2_, ...), custom_call_target="tpu_custom_call" | custom-call | flops 4294967296 | bytes 4194304 | tf_op jit(solution)/shard_map/attend_forward/pallas_call | solution.py:185
  40.0 8.6 %attend_forward.4 = (bf16[4,64,512]{2,1,0:T(8,128)(2,1)S(1)}, f32[1,2048]{1,0:T(1,128)S(1)}) custom-call(s32[3]{0:T(128)S(1)} %pad_add_fusion.me_ref, bf16[4,192,512]{2,1,0:T(8,128)(2,1)S(1)} %project.4.refs_0_, bf16[192,512]{1,0:T(8,128)(2,1)} %collective-permute-done.3.refs_1_, bf16[192,512]{1,0:T(8,128)(2,1)} %collective-permute-done.4.refs_2_, ...), custom_call_target="tpu_custom_call" | custom-call | flops 4294967296 | bytes 4194304 | tf_op jit(solution)/shard_map/attend_forward/pallas_call | solution.py:185
  48.7 18.4 %attend_forward.3 = (bf16[4,64,512]{2,1,0:T(8,128)(2,1)S(1)}, f32[1,2048]{1,0:T(1,128)S(1)}) custom-call(s32[3]{0:T(128)S(1)} %pad_add_fusion.me_ref, bf16[4,192,512]{2,1,0:T(8,128)(2,1)S(1)} %project.3.refs_0_, bf16[192,512]{1,0:T(8,128)(2,1)S(1)} %collective-permute-done.refs_1_, bf16[192,512]{1,0:T(8,128)(2,1)S(1)} %collective-permute-done.1.refs_2_, ...), custom_call_target="tpu_custom_call" | custom-call | flops 4294967296 | bytes 4194304 | tf_op jit(solution)/shard_map/attend_forward/pallas_call | solution.py:185
  73.0 4.1 %collective-permute-done.10.refs_2_ = bf16[3,64,512]{2,1,0:T(8,128)(2,1)S(1)} collective-permute-done((bf16[3,64,512]{2,1,0:T(8,128)(2,1)S(1)}, bf16[3,64,512]{2,1,0:T(8,128)(2,1)S(1)}, u32[]{:S(2)}, u32[]{:S(2)}) %collective-permute-start.10) | collective-permute-done | bytes 196640 | tf_op jit(solution)/shard_map/ppermute | solution.py:682
  79.8 11.8 %middle_part.1 = (bf16[768,512]{1,0:T(8,128)(2,1)S(1)}, bf16[512,768]{1,0:T(8,128)(2,1)S(1)}, bf16[512,2304]{1,0:T(8,128)(2,1)S(1)}, bf16[512,1152]{1,0:T(8,128)...) custom-call(s32[3]{0:T(128)S(1)} %pad_add_fusion.me_ref, ...), custom_call_target="tpu_custom_call" | custom-call | flops 7549747200 | bytes 20971520 | tf_op jit(solution)/shard_map/middle_part/pallas_call | solution.py:388
  91.6 5.3 %early_grads.1 = (bf16[16,264,384]{2,1,0:T(8,128)(2,1)S(1)}, bf16[16,264,384]{2,1,0:T(8,128)(2,1)S(1)}) custom-call(s32[17]{0:T(128)S(1)} %pad_add_fusion.1.at_ref, bf16[512,768]{1,0:T(8,128)(2,1)S(1)} %get-tuple-element.141.n2_ref, bf16[512,2304]{1,0:T(8,128)(2,1)S(1)} %get-tuple-element.142.gu_ref, bf16[512,1152]{1,0:T(8,128)(2,1)S(1)} %get-tuple-element.143.inner_ref, ...), custom_call_target="tpu_custom_call" | custom-call | flops 3321888768 | bytes 14680064 | tf_op jit(solution)/shard_map/early_grads/pallas_call | solution.py:443
  106.9 4.2 %collective-permute-done.18.refs_6_ = bf16[3,64,512]{2,1,0:T(8,128)(2,1)S(1)} collective-permute-done((bf16[3,64,512]{2,1,0:T(8,128)(2,1)S(1)}, bf16[3,64,512]{2,1,0:T(8,128)(2,1)S(1)}, u32[]{:S(2)}, u32[]{:S(2)}) %collective-permute-start.18) | collective-permute-done | bytes 196640 | tf_op jit(solution)/shard_map/ppermute | solution.py:682
  111.1 12.3 %attend_backward.3.refs_0_ = bf16[4,192,512]{2,1,0:T(8,128)(2,1)S(1)} custom-call(s32[3]{0:T(128)S(1)} %pad_add_fusion.me_ref, bf16[4,192,512]{2,1,0:T(8,128)(2,1)S(1)} %project.3.refs_0_, bf16[192,512]{1,0:T(8,128)(2,1)S(1)} %collective-permute-done.refs_1_, bf16[192,512]{1,0:T(8,128)(2,1)S(1)} %collective-permute-done.1.refs_2_, ...), custom_call_target="tpu_custom_call" | custom-call | flops 10737418240 | bytes 6291456 | tf_op jit(solution)/shard_map/attend_backward/pallas_call | solution.py:291
  129.7 13.7 %attend_backward.4.refs_1_ = bf16[4,192,512]{2,1,0:T(8,128)(2,1)S(1)} custom-call(s32[3]{0:T(128)S(1)} %pad_add_fusion.me_ref, bf16[4,192,512]{2,1,0:T(8,128)(2,1)S(1)} %project.4.refs_0_, bf16[192,512]{1,0:T(8,128)(2,1)} %collective-permute-done.3.refs_1_, bf16[192,512]{1,0:T(8,128)(2,1)} %collective-permute-done.4.refs_2_, ...), custom_call_target="tpu_custom_call" | custom-call | flops 10737418240 | bytes 6291456 | tf_op jit(solution)/shard_map/attend_backward/pallas_call | solution.py:291
  143.7 3.1 %collective-permute-start.26 = (bf16[264,384]{1,0:T(8,128)(2,1)S(1)}, bf16[264,384]{1,0:T(8,128)(2,1)S(1)}, u32[]{:S(2)}, u32[]{:S(2)}) collective-permute-start(bf16[264,384]{1,0:T(8,128)(2,1)S(1)} %get-tuple-element.223), channel_id=1, source_target_pairs={{0,6},{2,4},{4,2},{6,0},{1,7},{3,5},{5,3},{7,1},{8,14},{10,12},{12... | collective-permute-start | bytes 608264 | tf_op jit(solution)/shard_map/ppermute | solution.py:682
  150.7 13.6 %attend_backward.5.refs_0_ = bf16[4,192,512]{2,1,0:T(8,128)(2,1)S(1)} custom-call(s32[3]{0:T(128)S(1)} %pad_add_fusion.me_ref, bf16[4,192,512]{2,1,0:T(8,128)(2,1)S(1)} %project.5.refs_0_, bf16[192,512]{1,0:T(8,128)(2,1)} %collective-permute-done.6.refs_1_, bf16[192,512]{1,0:T(8,128)(2,1)} %collective-permute-done.7.refs_2_, ...), custom_call_target="tpu_custom_call" | custom-call | flops 10737418240 | bytes 6291456 | tf_op jit(solution)/shard_map/attend_backward/pallas_call | solution.py:291
  167.3 3.0 %collective-permute-start.33 = (bf16[264,384]{1,0:T(8,128)(2,1)S(1)}, bf16[264,384]{1,0:T(8,128)(2,1)S(1)}, u32[]{:S(2)}, u32[]{:S(2)}) collective-permute-start(bf16[264,384]{1,0:T(8,128)(2,1)S(1)} %fusion.2), channel_id=1, source_target_pairs={{0,4},{2,6},{4,0},{6,2},{1,5},{3,7},{5,1},{7,3},{8,12},{10,14},{12... | collective-permute-start | bytes 608264 | tf_op jit(solution)/shard_map/ppermute | solution.py:682
  171.0 4.9 %collective-permute-done.35.refs_3_ = bf16[2,192,512]{2,1,0:T(8,128)(2,1)S(1)} collective-permute-done((bf16[2,192,512]{2,1,0:T(8,128)(2,1)S(1)}, bf16[2,192,512]{2,1,0:T(8,128)(2,1)S(1)}, u32[]{:S(2)}, u32[]{:S(2)}) %collective-permute-start.35) | collective-permute-done | bytes 393248 | tf_op jit(solution)/shard_map/ppermute | solution.py:682
  188.5 3.1 %collective-permute-start.41 = (bf16[9,8,768]{2,1,0:T(8,128)(2,1)S(1)}, bf16[9,8,768]{2,1,0:T(8,128)(2,1)S(1)}, u32[]{:S(2)}, u32[]{:S(2)}) collective-permute-start(bf16[9,8,768]{2,1,0:T(8,128)(2,1)S(1)} %get-tuple-element.247), channel_id=1, source_target_pairs={{0,6},{2,4},{4,2},{6,0},{1,7},{3,5},{5,3},{7,1},{8,14},{10,12},{12... | collective-permute-start | bytes 331784 | tf_op jit(solution)/shard_map/ppermute | solution.py:682
  193.0 4.8 %input_grad.1 = f32[512,768]{1,0:T(8,128)} custom-call(s32[3]{0:T(128)S(1)} %pad_add_fusion.me_ref, bf16[2,192,512]{2,1,0:T(8,128)(2,1)S(1)} %get-tuple-element.189.refs_0_, bf16[2,192,512]{2,1,0:T(8,128)(2,1)S(1)} %collective-permute-done.27.refs_1_, bf16[2,192,512]{2,1,0:T(8,128)(2,1)S(1)} %collective-permute-done.28.refs_2_, ...), custom_call_target="tpu_custom_call" | custom-call | flops 1811939328 | bytes 10485760 | tf_op jit(solution)/shard_map/input_grad/pallas_call | solution.py:668
  197.8 3.7 %collective-permute-done.40 = bf16[9,8,768]{2,1,0:T(8,128)(2,1)S(1)} collective-permute-done((bf16[9,8,768]{2,1,0:T(8,128)(2,1)S(1)}, bf16[9,8,768]{2,1,0:T(8,128)(2,1)S(1)}, u32[]{:S(2)}, u32[]{:S(2)}) %collective-permute-start.40) | collective-permute-done | bytes 110624 | tf_op jit(solution)/shard_map/ppermute | solution.py:682
  201.5 5.0 %collective-permute-done.36 = bf16[4,264,384]{2,1,0:T(8,128)(2,1)S(1)} collective-permute-done((bf16[4,264,384]{2,1,0:T(8,128)(2,1)S(1)}, bf16[4,264,384]{2,1,0:T(8,128)(2,1)S(1)}, u32[]{:S(2)}, u32[]{:S(2)}) %collective-permute-start.36) | collective-permute-done | bytes 811040 | tf_op jit(solution)/shard_map/ppermute | solution.py:682
  209.3 3.1 %collective-permute-start.46 = (bf16[9,8,768]{2,1,0:T(8,128)(2,1)S(1)}, bf16[9,8,768]{2,1,0:T(8,128)(2,1)S(1)}, u32[]{:S(2)}, u32[]{:S(2)}) collective-permute-start(bf16[9,8,768]{2,1,0:T(8,128)(2,1)S(1)} %fusion.12), channel_id=1, source_target_pairs={{0,6},{2,4},{4,2},{6,0},{1,7},{3,5},{5,3},{7,1},{8,14},{10,12},{12... | collective-permute-start | bytes 331784 | tf_op jit(solution)/shard_map/ppermute | solution.py:682
  213.7 3.4 %collective-permute-done.46 = bf16[9,8,768]{2,1,0:T(8,128)(2,1)S(1)} collective-permute-done((bf16[9,8,768]{2,1,0:T(8,128)(2,1)S(1)}, bf16[9,8,768]{2,1,0:T(8,128)(2,1)S(1)}, u32[]{:S(2)}, u32[]{:S(2)}) %collective-permute-start.46) | collective-permute-done | bytes 110624 | tf_op jit(solution)/shard_map/ppermute | solution.py:682
  217.1 4.7 %collective-permute-done.45 = bf16[9,8,768]{2,1,0:T(8,128)(2,1)S(1)} collective-permute-done((bf16[9,8,768]{2,1,0:T(8,128)(2,1)S(1)}, bf16[9,8,768]{2,1,0:T(8,128)(2,1)S(1)}, u32[]{:S(2)}, u32[]{:S(2)}) %collective-permute-start.45) | collective-permute-done | bytes 110624 | tf_op jit(solution)/shard_map/ppermute | solution.py:682
  225.2 10.1 %collective-permute-done.47.refs_1_ = bf16[4,9,8,768]{3,2,1,0:T(8,128)(2,1)S(1)} collective-permute-done((bf16[4,9,8,768]{3,2,1,0:T(8,128)(2,1)S(1)}, bf16[4,9,8,768]{3,2,1,0:T(8,128)(2,1)S(1)}, u32[]{:S(2)}, u32[]{:S(2)}) %collective-permute-start.47) | collective-permute-done | bytes 442400 | tf_op jit(solution)/shard_map/ppermute | solution.py:682
  238.6 6.4 %assemble_early.1 = (f32[768,2304]{1,0:T(8,128)}, f32[1152,768]{1,0:T(8,128)}, f32[768,768]{1,0:T(8,128)}, f32[1,768]{1,0:T(1,128)S(1)}) custom-call(s32[3]{0:T(128)S(1)} %pad_add_fusion.me_ref, bf16[4,4,264,384]{3,2,1,0:T(8,128)(2,1)S(1)} %pad_maximum_fusion.mine_ref, bf16[4,4,264,384]{3,2,1,0:T(8,128)(2,1)S(1)} %collective-permute-done.49.other_ref, ...), custom_call_target="tpu_custom_call" | custom-call | flops 1048576 | bytes 25165824 | tf_op jit(solution)/shard_map/assemble_early/pallas_call | solution.py:544
  248.1 9.1 %assemble_late.1 = (f32[768,2304]{1,0:T(8,128)}, f32[768]{0:T(1024)}) custom-call(s32[3]{0:T(128)} %copy-done.8, bf16[4,9,8,768]{3,2,1,0:T(8,128)(2,1)} %copy-done.14, bf16[4,9,8,768]{3,2,1,0:T(8,128)(2,1)} %copy-done.15, bf16[4,9,8,768]{3,2,1,0:T(8,128)(2,1)} %copy-done.16, bf16[2,9,8,768]{3,2,1,0:T(8,128)(2,1)} %copy-done.22, ...), custom_call_target="tpu_custom_call" | custom-call | flops 1048576 | bytes 14680064 | tf_op jit(solution)/shard_map/assemble_late/pallas_call | solution.py:608
  (206 shorter events, 87.6 us)
Async XLA Ops:
  17.8 18.7 %collective-permute-start.3 = (bf16[192,512]{1,0:T(8,128)(2,1)}, bf16[192,512]{1,0:T(8,128)(2,1)}, u32[]{:S(2)}, u32[]{:S(2)}) collective-permute-start(bf16[192,512]{1,0:T(8,128)(2,1)} %get-tuple-element.242), channel_id=1, source_target_pairs={{0,8},{8,0},{16,24},{24,16},{1,9},{9,1},{17,25},{25,17},{2,10},{10... | collective-permute-start | bytes 589832 | tf_op jit(solution)/shard_map/ppermute | solution.py:682
  19.7 17.7 %collective-permute-start.4 = (bf16[192,512]{1,0:T(8,128)(2,1)}, bf16[192,512]{1,0:T(8,128)(2,1)}, u32[]{:S(2)}, u32[]{:S(2)}) collective-permute-start(bf16[192,512]{1,0:T(8,128)(2,1)} %get-tuple-element.241), channel_id=1, source_target_pairs={{0,16},{8,24},{16,0},{24,8},{1,17},{9,25},{17,1},{25,9},{2,18},{10... | collective-permute-start | bytes 589832 | tf_op jit(solution)/shard_map/ppermute | solution.py:682
  24.1 14.3 %collective-permute-start.5 = (bf16[192,512]{1,0:T(8,128)(2,1)}, bf16[192,512]{1,0:T(8,128)(2,1)S(1)}, u32[]{:S(2)}, u32[]{:S(2)}) collective-permute-start(bf16[192,512]{1,0:T(8,128)(2,1)} %get-tuple-element.240), channel_id=1, source_target_pairs={{0,24},{8,16},{16,8},{24,0},{1,25},{9,17},{17,9},{25,1},{2,26},{10... | collective-permute-start | bytes 589832 | tf_op jit(solution)/shard_map/ppermute | solution.py:682
  24.6 24.0 %collective-permute-start = (bf16[192,512]{1,0:T(8,128)(2,1)S(1)}, bf16[192,512]{1,0:T(8,128)(2,1)S(1)}, u32[]{:S(2)}, u32[]{:S(2)}) collective-permute-start(bf16[192,512]{1,0:T(8,128)(2,1)S(1)} %get-tuple-element.239), channel_id=1, source_target_pairs={{0,8},{8,0},{16,24},{24,16},{1,9},{9,1},{17,25},{25,17},{2,10},{10... | collective-permute-start | bytes 589832 | tf_op jit(solution)/shard_map/ppermute | solution.py:682
  26.1 22.5 %collective-permute-start.1 = (bf16[192,512]{1,0:T(8,128)(2,1)S(1)}, bf16[192,512]{1,0:T(8,128)(2,1)S(1)}, u32[]{:S(2)}, u32[]{:S(2)}) collective-permute-start(bf16[192,512]{1,0:T(8,128)(2,1)S(1)} %get-tuple-element.238), channel_id=1, source_target_pairs={{0,16},{8,24},{16,0},{24,8},{1,17},{9,25},{17,1},{25,9},{2,18},{10... | collective-permute-start | bytes 589832 | tf_op jit(solution)/shard_map/ppermute | solution.py:682
  37.4 39.7 %collective-permute-start.12 = (bf16[512,768]{1,0:T(8,128)(2,1)S(1)}, bf16[512,768]{1,0:T(8,128)(2,1)S(1)}, u32[]{:S(2)}, u32[]{:S(2)}) collective-permute-start(bf16[512,768]{1,0:T(8,128)(2,1)S(1)} %first_norm.1.hn_ref), channel_id=1, source_target_pairs={{0,8},{8,0},{16,24},{24,16},{1,9},{9,1},{17,25},{25,17},{2,10},{10... | collective-permute-start | bytes 2359304 | tf_op jit(solution)/shard_map/ppermute | solution.py:682
  38.4 38.7 %collective-permute-start.13 = (bf16[512,768]{1,0:T(8,128)(2,1)S(1)}, bf16[512,768]{1,0:T(8,128)(2,1)S(1)}, u32[]{:S(2)}, u32[]{:S(2)}) collective-permute-start(bf16[512,768]{1,0:T(8,128)(2,1)S(1)} %first_norm.1.hn_ref), channel_id=1, source_target_pairs={{0,16},{8,24},{16,0},{24,8},{1,17},{9,25},{17,1},{25,9},{2,18},{10... | collective-permute-start | bytes 2359304 | tf_op jit(solution)/shard_map/ppermute | solution.py:682
  77.2 14.5 %collective-permute-start.14 = (bf16[256,768]{1,0:T(8,128)(2,1)S(1)}, bf16[256,768]{1,0:T(8,128)(2,1)S(1)}, u32[]{:S(2)}, u32[]{:S(2)}) collective-permute-start(bf16[256,768]{1,0:T(8,128)(2,1)S(1)} %slice.210), channel_id=1, source_target_pairs={{0,8},{8,0},{16,24},{24,16},{1,9},{9,1},{17,25},{25,17},{2,10},{10... | collective-permute-start | bytes 1179656 | tf_op jit(solution)/shard_map/ppermute | solution.py:682
  104.9 21.4 %collective-permute-start.20 = (bf16[4,264,384]{2,1,0:T(8,128)(2,1)S(1)}, bf16[4,264,384]{2,1,0:T(8,128)(2,1)S(1)}, u32[]{:S(2)}, u32[]{:S(2)}) collective-permute-start(bf16[4,264,384]{2,1,0:T(8,128)(2,1)S(1)} %get-tuple-element.153), channel_id=1, source_target_pairs={{0,8},{8,0},{16,24},{24,16},{1,9},{9,1},{17,25},{25,17},{2,10},{10... | collective-permute-start | bytes 2433032 | tf_op jit(solution)/shard_map/ppermute | solution.py:682
  106.8 20.9 %collective-permute-start.21 = (bf16[4,264,384]{2,1,0:T(8,128)(2,1)S(1)}, bf16[4,264,384]{2,1,0:T(8,128)(2,1)S(1)}, u32[]{:S(2)}, u32[]{:S(2)}) collective-permute-start(bf16[4,264,384]{2,1,0:T(8,128)(2,1)S(1)} %get-tuple-element.154), channel_id=1, source_target_pairs={{0,16},{8,24},{16,0},{24,8},{1,17},{9,25},{17,1},{25,9},{2,18},{10... | collective-permute-start | bytes 2433032 | tf_op jit(solution)/shard_map/ppermute | solution.py:682
  127.9 15.5 %collective-permute-start.22 = (bf16[2,264,384]{2,1,0:T(8,128)(2,1)S(1)}, bf16[2,264,384]{2,1,0:T(8,128)(2,1)S(1)}, u32[]{:S(2)}, u32[]{:S(2)}) collective-permute-start(bf16[2,264,384]{2,1,0:T(8,128)(2,1)S(1)} %get-tuple-element.226), channel_id=1, source_target_pairs={{0,16},{8,24},{16,0},{24,8},{1,17},{9,25},{17,1},{25,9},{2,18},{10... | collective-permute-start | bytes 1216520 | tf_op jit(solution)/shard_map/ppermute | solution.py:682
  128.3 15.2 %collective-permute-start.23 = (bf16[2,264,384]{2,1,0:T(8,128)(2,1)S(1)}, bf16[2,264,384]{2,1,0:T(8,128)(2,1)S(1)}, u32[]{:S(2)}, u32[]{:S(2)}) collective-permute-start(bf16[2,264,384]{2,1,0:T(8,128)(2,1)S(1)} %get-tuple-element.225), channel_id=1, source_target_pairs={{0,8},{8,0},{16,24},{24,16},{1,9},{9,1},{17,25},{25,17},{2,10},{10... | collective-permute-start | bytes 1216520 | tf_op jit(solution)/shard_map/ppermute | solution.py:682
  143.7 20.6 %collective-permute-start.26 = (bf16[264,384]{1,0:T(8,128)(2,1)S(1)}, bf16[264,384]{1,0:T(8,128)(2,1)S(1)}, u32[]{:S(2)}, u32[]{:S(2)}) collective-permute-start(bf16[264,384]{1,0:T(8,128)(2,1)S(1)} %get-tuple-element.223), channel_id=1, source_target_pairs={{0,6},{2,4},{4,2},{6,0},{1,7},{3,5},{5,3},{7,1},{8,14},{10,12},{12... | collective-permute-start | bytes 608264 | tf_op jit(solution)/shard_map/ppermute | solution.py:682
  146.9 18.7 %collective-permute-start.25 = (bf16[264,384]{1,0:T(8,128)(2,1)S(1)}, bf16[264,384]{1,0:T(8,128)(2,1)S(1)}, u32[]{:S(2)}, u32[]{:S(2)}) collective-permute-start(bf16[264,384]{1,0:T(8,128)(2,1)S(1)} %get-tuple-element.222), channel_id=1, source_target_pairs={{0,4},{2,6},{4,0},{6,2},{1,5},{3,7},{5,1},{7,3},{8,12},{10,14},{12... | collective-permute-start | bytes 608264 | tf_op jit(solution)/shard_map/ppermute | solution.py:682
  146.9 18.7 %collective-permute-start.24 = (bf16[264,384]{1,0:T(8,128)(2,1)S(1)}, bf16[264,384]{1,0:T(8,128)(2,1)S(1)}, u32[]{:S(2)}, u32[]{:S(2)}) collective-permute-start(bf16[264,384]{1,0:T(8,128)(2,1)S(1)} %get-tuple-element.224), channel_id=1, source_target_pairs={{0,2},{2,0},{4,6},{6,4},{1,3},{3,1},{5,7},{7,5},{8,10},{10,8},{12,... | collective-permute-start | bytes 608264 | tf_op jit(solution)/shard_map/ppermute | solution.py:682
  148.3 17.4 %collective-permute-start.27 = (bf16[2,192,512]{2,1,0:T(8,128)(2,1)S(1)}, bf16[2,192,512]{2,1,0:T(8,128)(2,1)S(1)}, u32[]{:S(2)}, u32[]{:S(2)}) collective-permute-start(bf16[2,192,512]{2,1,0:T(8,128)(2,1)S(1)} %get-tuple-element.228), channel_id=1, source_target_pairs={{0,8},{8,0},{16,24},{24,16},{1,9},{9,1},{17,25},{25,17},{2,10},{10... | collective-permute-start | bytes 1179656 | tf_op jit(solution)/shard_map/ppermute | solution.py:682
  149.0 16.8 %collective-permute-start.28 = (bf16[2,192,512]{2,1,0:T(8,128)(2,1)S(1)}, bf16[2,192,512]{2,1,0:T(8,128)(2,1)S(1)}, u32[]{:S(2)}, u32[]{:S(2)}) collective-permute-start(bf16[2,192,512]{2,1,0:T(8,128)(2,1)S(1)} %get-tuple-element.229), channel_id=1, source_target_pairs={{0,16},{8,24},{16,0},{24,8},{1,17},{9,25},{17,1},{25,9},{2,18},{10... | collective-permute-start | bytes 1179656 | tf_op jit(solution)/shard_map/ppermute | solution.py:682
  166.5 17.8 %collective-permute-start.32 = (bf16[264,384]{1,0:T(8,128)(2,1)S(1)}, bf16[264,384]{1,0:T(8,128)(2,1)S(1)}, u32[]{:S(2)}, u32[]{:S(2)}) collective-permute-start(bf16[264,384]{1,0:T(8,128)(2,1)S(1)} %fusion.2), channel_id=1, source_target_pairs={{0,2},{2,0},{4,6},{6,4},{1,3},{3,1},{5,7},{7,5},{8,10},{10,8},{12,... | collective-permute-start | bytes 608264 | tf_op jit(solution)/shard_map/ppermute | solution.py:682
  167.3 17.1 %collective-permute-start.33 = (bf16[264,384]{1,0:T(8,128)(2,1)S(1)}, bf16[264,384]{1,0:T(8,128)(2,1)S(1)}, u32[]{:S(2)}, u32[]{:S(2)}) collective-permute-start(bf16[264,384]{1,0:T(8,128)(2,1)S(1)} %fusion.2), channel_id=1, source_target_pairs={{0,4},{2,6},{4,0},{6,2},{1,5},{3,7},{5,1},{7,3},{8,12},{10,14},{12... | collective-permute-start | bytes 608264 | tf_op jit(solution)/shard_map/ppermute | solution.py:682
  170.2 14.1 %collective-permute-start.34 = (bf16[264,384]{1,0:T(8,128)(2,1)S(1)}, bf16[264,384]{1,0:T(8,128)(2,1)S(1)}, u32[]{:S(2)}, u32[]{:S(2)}) collective-permute-start(bf16[264,384]{1,0:T(8,128)(2,1)S(1)} %fusion.2), channel_id=1, source_target_pairs={{0,6},{2,4},{4,2},{6,0},{1,7},{3,5},{5,3},{7,1},{8,14},{10,12},{12... | collective-permute-start | bytes 608264 | tf_op jit(solution)/shard_map/ppermute | solution.py:682
  186.0 20.5 %collective-permute-start.36 = (bf16[4,264,384]{2,1,0:T(8,128)(2,1)S(1)}, bf16[4,264,384]{2,1,0:T(8,128)(2,1)S(1)}, u32[]{:S(2)}, u32[]{:S(2)}) collective-permute-start(bf16[4,264,384]{2,1,0:T(8,128)(2,1)S(1)} %get-tuple-element.232), channel_id=1, source_target_pairs={{0,8},{8,0},{16,24},{24,16},{1,9},{9,1},{17,25},{25,17},{2,10},{10... | collective-permute-start | bytes 2433032 | tf_op jit(solution)/shard_map/ppermute | solution.py:682
  187.8 20.2 %collective-permute-start.37 = (bf16[4,264,384]{2,1,0:T(8,128)(2,1)S(1)}, bf16[4,264,384]{2,1,0:T(8,128)(2,1)S(1)}, u32[]{:S(2)}, u32[]{:S(2)}) collective-permute-start(bf16[4,264,384]{2,1,0:T(8,128)(2,1)S(1)} %get-tuple-element.232), channel_id=1, source_target_pairs={{0,16},{8,24},{16,0},{24,8},{1,17},{9,25},{17,1},{25,9},{2,18},{10... | collective-permute-start | bytes 2433032 | tf_op jit(solution)/shard_map/ppermute | solution.py:682
  208.0 13.9 %collective-permute-start.42 = (bf16[2,264,384]{2,1,0:T(8,128)(2,1)S(1)}, bf16[2,264,384]{2,1,0:T(8,128)(2,1)S(1)}, u32[]{:S(2)}, u32[]{:S(2)}) collective-permute-start(bf16[2,264,384]{2,1,0:T(8,128)(2,1)S(1)} %slice.246), channel_id=1, source_target_pairs={{0,8},{8,0},{16,24},{24,16},{1,9},{9,1},{17,25},{25,17},{2,10},{10... | collective-permute-start | bytes 1216520 | tf_op jit(solution)/shard_map/ppermute | solution.py:682
  225.2 19.9 %collective-permute-start.52 = (bf16[4,9,8,768]{3,2,1,0:T(8,128)(2,1)S(1)}, bf16[4,9,8,768]{3,2,1,0:T(8,128)(2,1)S(1)}, u32[]{:S(2)}, u32[]{:S(2)}) collective-permute-start(bf16[4,9,8,768]{3,2,1,0:T(8,128)(2,1)S(1)} %pad_maximum_fusion.4.refs_0_), channel_id=1, source_target_pairs={{0,1},{1,0},{2,3},{3,2},{4,5},{5,4},{6,7},{7,6},{8,9},{9,8},{10,11... | collective-permute-start | bytes 1327112 | tf_op jit(solution)/shard_map/ppermute | solution.py:682
  (60 other events, 949.0 us)
